TPU v7x, 32 devices: a whole 2x2x4 slice. The times are simulated.
32 devices in a mesh: parts: 2 (over y), seq: 4 (over z), sub: 4 (over x, core).
Axes of the slice: x: 2, y: 2, z: 4, core: 2. Of those that a mesh axis runs over, the one named last changes fastest.
Arguments:
- q_space: bfloat16 [16, 512, 2048], P(('parts', 'seq'), None, 'sub'), parts along dimension 0, may hold values from -6 to 6
- k_space: bfloat16 [16, 512, 2048], P(('parts', 'seq'), None, 'sub'), parts along dimension 0, may hold values from -6 to 6
- v_space: bfloat16 [16, 512, 2048], P(('parts', 'seq'), None, 'sub'), parts along dimension 0, may hold values from -6 to 6
- q_time: bfloat16 [16, 4, 128, 2048], P('parts', None, 'seq', 'sub'), parts along dimension 0, may hold values from -6 to 6
- k_time: bfloat16 [16, 4, 128, 2048], P('parts', None, 'seq', 'sub'), parts along dimension 0, may hold values from -6 to 6
- out_weight: bfloat16 [2048, 3072], P('sub', 'seq'), may hold values from -0.125 to 0.125
- cotangent: bfloat16 [16, 512, 3072], P(('parts', 'seq'), 'sub'), parts along dimension 0, may hold values from -6 to 6
Outputs:
- dq_space: bfloat16 [16, 512, 2048], P(('parts', 'seq'), None, 'sub'), parts along dimension 0
- dk_space: bfloat16 [16, 512, 2048], P(('parts', 'seq'), None, 'sub'), parts along dimension 0
- dv_space: bfloat16 [16, 512, 2048], P(('parts', 'seq'), None, 'sub'), parts along dimension 0
- d_weight: float32 [4096, 3072], P(('parts', 'sub'), 'seq'), parts along dimension 0
There are 2 independent parts, one for each index of `parts`. A program takes and returns all parts, laid end to end along the dimension named above; an argument that names none is the same for every part. Nothing has to cross between parts.
All inputs are finite; a program needn't handle non-finite values.
Results may differ from a plain program's by a relative error of at most 0.01.
Values may be sent and summed in bfloat16 or wider, within the bound.
No kernel may reach another device: no remote copies, remote signals or barrier semaphores. Data moves between devices by JAX's collectives and lax.ppermute only.
A program may use at most 128 MiB of HBM per device.

v0:
```python
import math

import jax
import jax.numpy as jnp
from jax import lax
from jax.sharding import PartitionSpec as P

HD = 128


def normalize(scores):
    row_top = jnp.max(scores, axis=-1, keepdims=True)
    raised = jnp.exp(scores - row_top)
    return raised / jnp.sum(raised, axis=-1, keepdims=True)


def space_chances(query, keys):
    scores = jnp.einsum("fqhd,fkhd->fhqk", query, keys, preferred_element_type=jnp.float32) * (
        1.0 / math.sqrt(HD)
    )
    return normalize(scores)


def on_device(q_space, k_space, v_space, q_time, k_time, out_weight, cotangent):
    frame_count, patches, columns = q_space.shape
    head_count = columns // HD
    band_count = lax.axis_size("sub")
    seq_count = lax.axis_size("seq")
    all_frames = frame_count * seq_count
    band_len = patches // band_count
    time_len = band_len // seq_count
    split_shape = (frame_count, patches, head_count, HD)
    space_query = q_space.reshape(split_shape)
    space_keys = k_space.reshape(split_shape)
    space_values = v_space.reshape(split_shape)
    chances = space_chances(space_query, space_keys)
    space_out = jnp.einsum(
        "fhqk,fkhd->fqhd",
        chances.astype(jnp.bfloat16),
        space_values,
        preferred_element_type=jnp.float32,
    ).astype(jnp.bfloat16)
    moved = lax.all_to_all(
        space_out.reshape(frame_count, band_count, band_len, columns),
        "seq",
        split_axis=2,
        concat_axis=0,
        tiled=True,
    )
    time_shape = (all_frames, band_count, time_len, head_count, HD)
    time_query = q_time.reshape(time_shape)
    time_keys = k_time.reshape(time_shape)
    time_values = moved.reshape(time_shape)
    time_scores = jnp.einsum(
        "fbphd,gbphd->bphfg", time_query, time_keys, preferred_element_type=jnp.float32
    ) * (1.0 / math.sqrt(HD))
    time_chances = normalize(time_scores).astype(jnp.bfloat16)
    time_out = jnp.einsum(
        "bphfg,gbphd->fbphd", time_chances, time_values, preferred_element_type=jnp.float32
    ).astype(jnp.bfloat16)
    time_out = time_out.reshape(all_frames, band_count, time_len, columns)
    weight_rows = lax.all_gather(out_weight, "seq", axis=1, tiled=True)
    returned = lax.all_to_all(time_out, "seq", split_axis=0, concat_axis=2, tiled=True)
    frame_out = returned.reshape(frame_count, patches, columns)
    segment = lax.all_gather(cotangent, "sub", axis=1, tiled=True)
    weight_sum = jnp.einsum("fnh,fnd->hd", frame_out, segment, preferred_element_type=jnp.float32)
    update = jnp.einsum("fnd,hd->fnh", segment, weight_rows, preferred_element_type=jnp.float32)
    out_grad = update
    weight_sum, out_grad = (weight_sum, out_grad)
    rounded = out_grad.astype(jnp.bfloat16).reshape(frame_count, band_count, band_len, columns)
    time_grad = lax.all_to_all(rounded, "seq", split_axis=2, concat_axis=0, tiled=True)
    d_weight = lax.psum_scatter(
        weight_sum.astype(jnp.bfloat16), "seq", scatter_dimension=1, tiled=True
    ).astype(jnp.float32)
    value_time = jnp.einsum(
        "bphfg,fbphd->gbphd",
        time_chances,
        time_grad.reshape(time_shape),
        preferred_element_type=jnp.float32,
    ).astype(jnp.bfloat16)
    space_grad = lax.all_to_all(
        value_time.reshape(all_frames, band_count, time_len, columns),
        "seq",
        split_axis=0,
        concat_axis=2,
        tiled=True,
    )
    space_grad = space_grad.reshape(split_shape)
    recomputed = space_chances(space_query, space_keys)
    value_grad = jnp.einsum(
        "fhqk,fqhd->fkhd",
        recomputed.astype(jnp.bfloat16),
        space_grad,
        preferred_element_type=jnp.float32,
    ).astype(jnp.bfloat16)
    chance_grad = jnp.einsum(
        "fqhd,fkhd->fhqk", space_grad, space_values, preferred_element_type=jnp.float32
    )
    centre_term = jnp.sum(recomputed * chance_grad, axis=-1, keepdims=True)
    score_grad = (recomputed * (chance_grad - centre_term) * (1.0 / math.sqrt(HD))).astype(
        jnp.bfloat16
    )
    query_grad = jnp.einsum(
        "fhqk,fkhd->fqhd", score_grad, space_keys, preferred_element_type=jnp.float32
    ).astype(jnp.bfloat16)
    keys_grad = jnp.einsum(
        "fhqk,fqhd->fkhd", score_grad, space_query, preferred_element_type=jnp.float32
    ).astype(jnp.bfloat16)
    flat_shape = (frame_count, patches, columns)
    return (
        query_grad.reshape(flat_shape),
        keys_grad.reshape(flat_shape),
        value_grad.reshape(flat_shape),
        d_weight,
    )


def solution(mesh):
    in_specs = (
        P(("parts", "seq"), None, "sub"),
        P(("parts", "seq"), None, "sub"),
        P(("parts", "seq"), None, "sub"),
        P("parts", None, "seq", "sub"),
        P("parts", None, "seq", "sub"),
        P("sub", "seq"),
        P(("parts", "seq"), "sub", None),
    )
    out_specs = (
        P(("parts", "seq"), None, "sub"),
        P(("parts", "seq"), None, "sub"),
        P(("parts", "seq"), None, "sub"),
        P(("parts", "sub"), "seq"),
    )
    return jax.shard_map(
        on_device, mesh=mesh, in_specs=in_specs, out_specs=out_specs, check_vma=False
    )
```

profile of v0, /device:TPU:0, one launch (start us, length us, event | category | flops | bytes accessed | tf_op | source)
XLA Modules:
  0.0 300.6 jit_solution(187689830887894949)
XLA Ops:
  7.2 0.0 all-gather.3.cloned.1.call-start
  7.2 0.7 all-gather.3.cloned.1.call-update
  7.9 0.0 all-gather.5.cloned.1.call-start
  8.0 0.7 all-gather.5.cloned.1.call-update
  8.7 1.5 copy.121
  10.2 1.9 copy.120
  12.1 5.1 %fusion.79 = (f32[2,4,512]{2,1,0:T(4,128)S(1)}, f32[2,4,512,512]{2,3,1,0:T(8,128)}) fusion(bf16[2,512,4,128]{1,3,2,0:T(8,128)(2,1)S(1)} %bitcast.79, bf16[2,512,4,128]{1,3,2,0:T(8,128)(2,1)S(1)} %bitcast.81), kind=kOutput, calls=%fused_computation.55 | convolution fusion | flops 543162880 | bytes 10502144 | tf_op jit(solution)/shard_map/sub | solution.py:13
  17.1 5.8 %fusion.40 = bf16[2,512,4,128]{3,1,2,0:T(8,128)(2,1)S(1)} fusion(f32[2,4,512,512]{2,3,1,0:T(8,128)} %get-tuple-element.23, f32[2,4,512]{2,1,0:T(4,128)S(1)} %get-tuple-element.22, bf16[2,512,512]{2,1,0:T(8,128)(2,1)S(1)} %copy-done), kind=kOutput, calls=%fused_computation.33 | convolution fusion | flops 541589504 | bytes 10502144 | tf_op jit(solution)/shard_map/fhqk,fkhd->fqhd/dot_general | solution.py:37
  22.9 0.8 copy.103
  23.7 0.4 reshape.77
  24.2 1.8 copy.104
  26.0 6.5 %all-to-all-start.2 = ((bf16[2,4,128,512]{3,1,0,2:T(4,128)(2,1)}), bf16[2,4,128,512]{3,1,0,2:T(4,128)(2,1)S(1)}, u32[]{:S(2)}, u32[]{:S(2)}) async-start(bf16[2,4,128,512]{3,1,0,2:T(4,128)(2,1)} %copy.104), calls=%async_computation.2 | async-start | bytes 2097152 | tf_op jit(solution)/shard_map/all_to_all | solution.py:43
  32.5 1.4 reshape.69
  33.8 2.1 reshape.70
  36.0 4.8 %fusion.74 = (f32[4,32,4,8]{3,2,1,0:T(4,128)S(1)}, f32[4,32,4,8,8]{3,4,2,1,0:T(8,128)}) fusion(bf16[8,4,32,4,128]{4,3,2,1,0:T(4,128)(2,1)} %reshape.70, bf16[8,4,32,4,128]{4,3,2,1,0:T(4,128)(2,1)S(1)} %reshape.69), kind=kOutput, calls=%fused_computation.54 | convolution fusion | flops 8486919 | bytes 2244608 | tf_op jit(solution)/shard_map/sub | solution.py:13
  40.7 17.3 %all-to-all-done.2 = bf16[2,4,128,512]{3,1,0,2:T(4,128)(2,1)S(1)} async-done(((bf16[2,4,128,512]{3,1,0,2:T(4,128)(2,1)}), bf16[2,4,128,512]{3,1,0,2:T(4,128)(2,1)S(1)}, u32[]{:S(2)}, u32[]{:S(2)}) %all-to-all-start.2) | async-done | bytes 1048608 | tf_op jit(solution)/shard_map/all_to_all | solution.py:43
  58.0 0.3 copy.157
  58.3 0.3 reshape.78
  58.6 2.6 fusion.39
  61.2 0.6 copy.108
  61.8 0.4 reshape.79
  62.2 52.4 %all_to_all.60 = bf16[8,4,32,512]{3,2,1,0:T(8,128)(2,1)S(1)} all-to-all(bf16[8,4,32,512]{3,2,1,0:T(8,128)(2,1)S(1)} %reshape.79), channel_id=1, replica_groups=mesh['parts'=2,'seq'=4,'sub'=4] {'seq'}, dimensions={0} | all-to-all | bytes 2097152 | tf_op jit(solution)/shard_map/all_to_all | solution.py:63
  114.6 0.1 copy.109
  114.7 0.0 all-gather.3.cloned.1.call-done
  114.8 7.6 %bitcast_convert_fusion = bf16[512,3072]{1,0:T(8,128)(2,1)} fusion(bf16[2,512,512]{2,1,0:T(8,128)(2,1)S(1)} %bitcast.83, bf16[2,512,3072]{2,1,0:T(8,128)(2,1)} %all-gather.3.cloned.1.call-done), kind=kOutput, calls=%fused_computation.9 | convolution fusion | flops 3222798336 | bytes 10485760 | tf_op jit(solution)/shard_map/fnh,fnd->hd/dot_general | solution.py:66
  122.4 0.0 reduce-scatter.2.cloned.1.call-update
  122.4 18.3 %all-gather.5.cloned.1.call-done = bf16[512,3072]{1,0:T(8,128)(2,1)} async-done(((bf16[512,768]{1,0:T(8,128)(2,1)}), bf16[512,3072]{1,0:T(8,128)(2,1)}) %all-gather.5.cloned.1.call-update) | async-done | bytes 3145744 | tf_op jit(solution)/shard_map/all_gather | solution.py:62
  140.8 7.1 %fusion.35 = bf16[2,512,512]{2,1,0:T(8,128)(2,1)S(1)} fusion(bf16[2,512,3072]{2,1,0:T(8,128)(2,1)} %all-gather.3.cloned.1.call-done, bf16[512,3072]{1,0:T(8,128)(2,1)} %all-gather.5.cloned.1.call-done), kind=kOutput, calls=%fused_computation.30 | convolution fusion | flops 3221749760 | bytes 10485760 | tf_op jit(solution)/shard_map/fnd,hd->fnh/dot_general | solution.py:67
  147.9 0.8 copy.85
  148.7 57.4 %all_to_all.61 = bf16[2,4,128,512]{3,1,0,2:T(4,128)(2,1)S(1)} all-to-all(bf16[2,4,128,512]{3,1,0,2:T(4,128)(2,1)S(1)} %copy.85), channel_id=1, replica_groups=mesh['parts'=2,'seq'=4,'sub'=4] {'seq'}, dimensions={2} | all-to-all | bytes 2097152 | tf_op jit(solution)/shard_map/all_to_all | solution.py:71
  206.2 0.3 copy.86
  206.5 0.1 copy.87
  206.6 0.3 reshape.68
  206.9 2.6 fusion.38
  209.4 0.6 copy.91
  210.0 0.4 reshape.71
  210.5 36.4 %all_to_all.62 = bf16[8,4,32,512]{3,2,1,0:T(8,128)(2,1)S(1)} all-to-all(bf16[8,4,32,512]{3,2,1,0:T(8,128)(2,1)S(1)} %reshape.71), channel_id=1, replica_groups=mesh['parts'=2,'seq'=4,'sub'=4] {'seq'}, dimensions={0} | all-to-all | bytes 2097152 | tf_op jit(solution)/shard_map/all_to_all | solution.py:81
  246.8 0.1 copy.158
  246.9 0.3 reshape.72
  247.2 0.7 copy.99
  247.9 5.9 %fusion.23 = bf16[2,4,128,512]{3,2,1,0:T(8,128)(2,1)} fusion(bf16[2,512,4,128]{1,3,2,0:T(8,128)(2,1)S(1)} %copy.99, f32[2,4,512,512]{2,3,1,0:T(8,128)} %get-tuple-element.23, f32[2,4,512]{2,1,0:T(4,128)S(1)} %get-tuple-element.22), kind=kOutput, calls=%fused_computation.24 | convolution fusion | flops 541589504 | bytes 10502144 | tf_op jit(solution)/shard_map/fhqk,fqhd->fkhd/dot_general | solution.py:90
  253.8 2.4 copy.113
  256.1 4.4 %fusion.44 = f32[2,4,512,512]{2,3,1,0:T(8,128)} fusion(bf16[2,512,4,128]{1,3,2,0:T(8,128)(2,1)S(1)} %copy.99, bf16[2,512,512]{2,1,0:T(8,128)(2,1)S(1)} %copy-done), kind=kOutput, calls=%fused_computation.35 | convolution fusion | flops 536870912 | bytes 10485760 | tf_op jit(solution)/shard_map/fqhd,fkhd->fhqk/dot_general | solution.py:96
  260.6 15.2 %fusion.29 = bf16[2,4,512,128]{2,3,1,0:T(8,128)(2,1)} fusion(bf16[2,512,4,128]{1,3,2,0:T(8,128)(2,1)S(1)} %bitcast.82, f32[2,4,512,512]{2,3,1,0:T(8,128)} %fusion.44, f32[2,4,512,512]{2,3,1,0:T(8,128)} %get-tuple-element.23, f32[2,4,512]{2,1,0:T(4,128)S(1)} %get-tuple-element.22), kind=kOutput, calls=%fused_computation.26 | convolution fusion | flops 552079872 | bytes 18890752 | tf_op jit(solution)/shard_map/fhqk,fkhd->fqhd/dot_general | solution.py:103
  275.8 2.3 copy.111
  278.1 12.3 %fusion.32 = bf16[2,4,512,128]{2,3,1,0:T(8,128)(2,1)S(1)} fusion(bf16[2,512,4,128]{1,3,2,0:T(8,128)(2,1)S(1)} %bitcast.80, f32[2,4,512,512]{2,3,1,0:T(8,128)} %fusion.44, f32[2,4,512,512]{2,3,1,0:T(8,128)} %get-tuple-element.23, f32[2,4,512]{2,1,0:T(4,128)S(1)} %get-tuple-element.22), kind=kOutput, calls=%fused_computation.27 | convolution fusion | flops 552079872 | bytes 18890752 | tf_op jit(solution)/shard_map/fhqk,fqhd->fkhd/dot_general | solution.py:106
  290.3 1.3 copy.112
  291.7 2.4 convert_element_type.72
  (12 shorter events, 0.0 us)
Async XLA Ops:
  7.2 10.0 %copy-start = (bf16[2,512,512]{2,1,0:T(8,128)(2,1)S(1)}, bf16[2,512,512]{2,1,0:T(8,128)(2,1)}, u32[]{:S(2)}) copy-start(bf16[2,512,512]{2,1,0:T(8,128)(2,1)} %param.9) | copy-start | bytes 3145732
  7.2 107.6 %all-gather.3.cloned.1.call-start = ((), (), s32[]{:S(2)}) async-start(), calls=%async_computation.5 | async-start | bytes 7864320 | tf_op jit(solution)/shard_map/all_gather | solution.py:65
  7.9 132.9 %all-gather.5.cloned.1.call-start = ((), (), s32[]{:S(2)}) async-start(), calls=%async_computation.6 | async-start | bytes 3932160 | tf_op jit(solution)/shard_map/all_gather | solution.py:62
  10.2 7.0 %copy-start.1 = (bf16[2,512,512]{1,2,0:T(8,128)(2,1)}, bf16[2,512,512]{1,2,0:T(8,128)(2,1)S(1)}, u32[]{:S(2)}) copy-start(bf16[2,512,512]{1,2,0:T(8,128)(2,1)S(1)} %copy.121) | copy-start | bytes 3145732
  12.1 10.9 %copy-start.3 = (bf16[2,512,512]{1,2,0:T(8,128)(2,1)}, bf16[2,512,512]{1,2,0:T(8,128)(2,1)S(1)}, u32[]{:S(2)}) copy-start(bf16[2,512,512]{1,2,0:T(8,128)(2,1)S(1)} %copy.120) | copy-start | bytes 3145732
  26.0 32.0 %all-to-all-start.2 = ((bf16[2,4,128,512]{3,1,0,2:T(4,128)(2,1)}), bf16[2,4,128,512]{3,1,0,2:T(4,128)(2,1)S(1)}, u32[]{:S(2)}, u32[]{:S(2)}) async-start(bf16[2,4,128,512]{3,1,0,2:T(4,128)(2,1)} %copy.104), calls=%async_computation.2 | async-start | bytes 2097152 | tf_op jit(solution)/shard_map/all_to_all | solution.py:43
  32.5 259.2 %reduce-scatter.2.cloned.1.call-start = ((), (), s32[]{:S(2)}) async-start(), calls=%async_computation.7 | async-start | bytes 3932160 | tf_op jit(solution)/shard_map/reduce_scatter | solution.py:72
  253.7 6.8 %copy-start.4 = (bf16[2,512,512]{1,2,0:T(8,128)(2,1)S(1)}, bf16[2,512,512]{1,2,0:T(8,128)(2,1)}, u32[]{:S(2)}) copy-start(bf16[2,512,512]{1,2,0:T(8,128)(2,1)} %copy-done.3) | copy-start | bytes 3145732
  260.6 17.5 %copy-start.2 = (bf16[2,512,512]{1,2,0:T(8,128)(2,1)S(1)}, bf16[2,512,512]{1,2,0:T(8,128)(2,1)}, u32[]{:S(2)}) copy-start(bf16[2,512,512]{1,2,0:T(8,128)(2,1)} %copy-done.1) | copy-start | bytes 3145732
Sparse Core Ops, SparseCore 0:
  9.6 49.0 all-gather.2
  60.3 80.4 all-gather.4
  143.1 83.3 reduce-scatter.1
where the time goes:
time: 301 us
  blocking collectives  146 us (49%)
  matrix products  73.3 us (24%)
  waiting for transfers between devices  37 us (12%)
  local copies, waits for them, and re-layouts  21.2 us (7%)
  between operations  14 us (5%)
  starting transfers between devices  6.55 us (2%)
    all_to_all x1, blocking collectives, on_device(): lax.all_to_all(rounded, 'seq', split_axis=2, concat_axis=0, tiled=True)  57.4 us
    all_to_all x1, blocking collectives, on_device(): lax.all_to_all(time_out, 'seq', split_axis=0, concat_axis=2, tiled=True)  52.4 us
    all_to_all x1, blocking collectives, on_device(): lax.all_to_all(value_time.reshape(all_frames, band_count, time_len, colum...  36.4 us
    all_gather x1, waiting for transfers between devices, on_device(): weight_rows = lax.all_gather(out_weight, 'seq', axis=1, tiled=True)  18.3 us
    all_to_all x1, waiting for transfers between devices, on_device(): lax.all_to_all(space_out.reshape(frame_count, band_count, band_len, colum...  17.3 us
    dot_general x1, matrix products, on_device(): jnp.einsum('fhqk,fkhd->fqhd', score_grad, space_keys, preferred_element_t...  15.2 us
    dot_general x1, matrix products, on_device(): jnp.einsum('fhqk,fqhd->fkhd', score_grad, space_query, preferred_element_...  12.3 us
    sub x2, matrix products, normalize(): raised = jnp.exp(scores - row_top)  9.81 us
  transfers between devices with their start and end apart: 4, of which 2 were waited for; matrix products, arithmetic and copies ran while one was open for 31% of the time, Pallas kernels for 0%

commit v1 on v0

--- a/solution.py
+++ b/solution.py
@@ -1,11 +1,15 @@
+import functools
 import math
 
 import jax
 import jax.numpy as jnp
 from jax import lax
+from jax.experimental import pallas as pl
+from jax.experimental.pallas import tpu as pltpu
 from jax.sharding import PartitionSpec as P
 
 HD = 128
+SCALE = 1.0 / math.sqrt(HD)
 
 
 def normalize(scores):
@@ -115,6 +119,290 @@
     )
 
 
+def xor_send(value, axis, distance):
+    count = lax.axis_size(axis)
+    return lax.ppermute(value, axis, [(i, i ^ distance) for i in range(count)])
+
+
+def swap_parts(value):
+    return lax.ppermute(value, "parts", [(0, 1), (1, 0)])
+
+
+def nt_dot(a, b):
+    return lax.dot_general(a, b, (((1,), (1,)), ((), ())), preferred_element_type=jnp.float32)
+
+
+def tn_dot(a, b):
+    return lax.dot_general(a, b, (((0,), (0,)), ((), ())), preferred_element_type=jnp.float32)
+
+
+def nn_dot(a, b):
+    return lax.dot_general(a, b, (((1,), (0,)), ((), ())), preferred_element_type=jnp.float32)
+
+
+def softmax_rows(scores, scale, axis):
+    raised = jnp.exp((scores - jnp.max(scores, axis=axis, keepdims=True)) * scale)
+    return raised * (1.0 / jnp.sum(raised, axis=axis, keepdims=True))
+
+
+def params():
+    return pltpu.CompilerParams(vmem_limit_bytes=56 * 1024 * 1024)
+
+
+def space_forward_kernel(ids, q, k, v, *rest):
+    seq_count, (probs, spare) = len(rest) - 2, rest[-2:]
+    me = ids[0]
+    low = softmax_rows(nt_dot(k[0], q[0]), SCALE, 0).astype(jnp.bfloat16)
+    probs[0] = low
+    out = tn_dot(v[0], low).T.astype(jnp.bfloat16)
+    spare[...] = out.reshape(spare.shape)
+    for step in range(seq_count):
+        rest[step][0] = spare[:, me ^ step]
+
+
+def space_forward(ids, q, k, v, seq_count, band_count, time_len):
+    frames, patches, columns = q.shape
+    heads = columns // HD
+    wide = pl.BlockSpec((1, patches, HD), lambda f, h, ids: (f, 0, h))
+    piece = pl.BlockSpec((1, band_count, time_len, HD), lambda f, h, ids: (f, 0, 0, h))
+    piece_shape = jax.ShapeDtypeStruct((frames, band_count, time_len, columns), jnp.bfloat16)
+    square = pl.BlockSpec((1, patches, patches), lambda f, h, ids: (f * heads + h, 0, 0))
+    square_shape = jax.ShapeDtypeStruct((frames * heads, patches, patches), jnp.bfloat16)
+    outs = pl.pallas_call(
+        space_forward_kernel,
+        grid_spec=pltpu.PrefetchScalarGridSpec(
+            num_scalar_prefetch=1,
+            grid=(frames, heads),
+            in_specs=[wide, wide, wide],
+            out_specs=[piece] * seq_count + [square],
+            scratch_shapes=[pltpu.VMEM((band_count, seq_count, time_len, HD), jnp.bfloat16)],
+        ),
+        out_shape=[piece_shape] * seq_count + [square_shape],
+        compiler_params=params(),
+        name="space_forward",
+    )(ids, q, k, v)
+    return outs[:seq_count], outs[seq_count]
+
+
+def time_probs_kernel(ids, q, k, probs, probs_t, *, seq_count):
+    me = ids[0]
+    frames, _, time_len, _ = q.shape
+    local = frames // seq_count
+    rows = frames * time_len
+
+    def ordered(ref):
+        picked = [ref[pl.ds((me ^ step) * local, local), 0] for step in range(seq_count)]
+        return jnp.concatenate(picked, axis=0).reshape(rows, HD)
+
+    query, keys = ordered(q), ordered(k)
+    place = [lax.broadcasted_iota(jnp.int32, (rows, rows), axis) % time_len for axis in (0, 1)]
+    same = place[0] == place[1]
+    low = jnp.float32(-1e30)
+    probs[0, 0] = softmax_rows(jnp.where(same, nt_dot(query, keys), low), SCALE, 1).astype(jnp.bfloat16)
+    probs_t[0, 0] = softmax_rows(jnp.where(same, nt_dot(keys, query), low), SCALE, 0).astype(jnp.bfloat16)
+
+
+def time_probs(ids, q, k, seq_count):
+    frames, bands, time_len, columns = q.shape
+    heads = columns // HD
+    rows = frames * time_len
+    spec = pl.BlockSpec((frames, 1, time_len, HD), lambda r, h, ids: (0, ids[1] ^ r, 0, h))
+    square = pl.BlockSpec((1, 1, rows, rows), lambda r, h, ids: (r, h, 0, 0))
+    square_shape = jax.ShapeDtypeStruct((bands, heads, rows, rows), jnp.bfloat16)
+    return pl.pallas_call(
+        functools.partial(time_probs_kernel, seq_count=seq_count),
+        grid_spec=pltpu.PrefetchScalarGridSpec(
+            num_scalar_prefetch=1,
+            grid=(bands, heads),
+            in_specs=[spec, spec],
+            out_specs=[square, square],
+        ),
+        out_shape=[square_shape, square_shape],
+        compiler_params=params(),
+        name="time_probs",
+    )(ids, q, k)
+
+
+def time_out_kernel(ids, probs, *rest):
+    out = rest[-1]
+    rows = probs.shape[2]
+    for head in range(probs.shape[1]):
+        lanes = slice(head * HD, (head + 1) * HD)
+        values = jnp.concatenate([ref[:, 0, :, lanes] for ref in rest[:-1]], axis=0).reshape(rows, HD)
+        out[0, :, lanes] = nn_dot(probs[0, head], values).astype(jnp.bfloat16)
+
+
+def time_out(ids, probs, pieces):
+    bands, heads, rows, _ = probs.shape
+    local, _, time_len, columns = pieces[0].shape
+    piece = pl.BlockSpec((local, 1, time_len, columns), lambda r, ids: (0, ids[1] ^ r, 0, 0))
+    return pl.pallas_call(
+        time_out_kernel,
+        grid_spec=pltpu.PrefetchScalarGridSpec(
+            num_scalar_prefetch=1,
+            grid=(bands,),
+            in_specs=[pl.BlockSpec((1, heads, rows, rows), lambda r, ids: (r, 0, 0, 0))] + [piece] * len(pieces),
+            out_specs=pl.BlockSpec((1, rows, columns), lambda r, ids: (r, 0, 0)),
+        ),
+        out_shape=jax.ShapeDtypeStruct((bands, rows, columns), jnp.bfloat16),
+        compiler_params=params(),
+        name="time_out",
+    )(ids, probs, *pieces)
+
+
+def weight_grad_kernel(ids, left, *rest):
+    out, width = rest[-1], rest[0].shape[-1]
+    right = jnp.concatenate([ref[...].reshape(-1, width) for ref in rest[:-1]], axis=0)
+    out[...] = tn_dot(left[...], right).astype(out.dtype)
+
+
+def weight_grad(ids, left, cots, step, width, dtype):
+    tokens, columns = left.shape
+    tile = 256
+    inner = width // tile
+    local, time_len, _ = cots[0].shape
+    cot_spec = pl.BlockSpec((local, time_len, tile), lambda j, ids: (0, 0, (ids[0] ^ step) * inner + j))
+    return pl.pallas_call(
+        weight_grad_kernel,
+        grid_spec=pltpu.PrefetchScalarGridSpec(
+            num_scalar_prefetch=1,
+            grid=(inner,),
+            in_specs=[pl.BlockSpec((tokens, columns), lambda j, ids: (0, 0))] + [cot_spec] * len(cots),
+            out_specs=pl.BlockSpec((columns, tile), lambda j, ids: (0, j)),
+        ),
+        out_shape=jax.ShapeDtypeStruct((columns, width), dtype),
+        compiler_params=params(),
+        name="weight_grad",
+    )(ids, left, *cots)
+
+
+def space_grad_kernel(ids, probs_t, own, *rest, seq_count, band_count):
+    mine, rest = rest[: seq_count - 1], rest[seq_count - 1 :]
+    theirs, rest = rest[: seq_count - 1], rest[seq_count - 1 :]
+    cots, outs, weight = rest[: band_count * seq_count], rest[-1 - seq_count : -1], rest[-1]
+    me, sub, part = ids[0], ids[1], ids[2]
+    rows, width = own.shape
+    half = rows // 2
+    weight[:, pl.ds(pl.multiple_of(me * width, 128), width)] = own[...]
+    for step in range(1, seq_count):
+        place = pl.ds(pl.multiple_of((me ^ step) * width, 128), width)
+        weight[pl.ds(pl.multiple_of(part * half, 128), half), place] = mine[step - 1][...]
+        weight[pl.ds(pl.multiple_of((1 - part) * half, 128), half), place] = theirs[step - 1][...]
+    local, time_len, depth = cots[0].shape
+    for r in range(band_count):
+        block = [cots[r * seq_count + step][...].reshape(local * time_len, depth) for step in range(seq_count)]
+        grad = nt_dot(jnp.concatenate(block, axis=0), weight[...]).astype(jnp.bfloat16)
+        for head in range(rows // HD):
+            lanes = slice(head * HD, (head + 1) * HD)
+            back = nn_dot(probs_t[r, head], grad[:, lanes]).astype(jnp.bfloat16)
+            back = back.reshape(seq_count, local, time_len, HD)
+            for step in range(seq_count):
+                outs[step][:, sub ^ r, :, lanes] = back[step]
+
+
+def space_grad(ids, probs_t, own, mine, theirs, cots, seq_count, band_count):
+    local, time_len, depth = cots[0].shape
+    rows = own.shape[0]
+    full = lambda array: pl.BlockSpec(array.shape, lambda i, ids: (0,) * array.ndim)
+    operands = (probs_t, own, *mine, *theirs, *cots)
+    out_shape = jax.ShapeDtypeStruct((local, band_count, time_len, rows), jnp.bfloat16)
+    return pl.pallas_call(
+        functools.partial(space_grad_kernel, seq_count=seq_count, band_count=band_count),
+        grid_spec=pltpu.PrefetchScalarGridSpec(
+            num_scalar_prefetch=1,
+            grid=(1,),
+            in_specs=[full(array) for array in operands],
+            out_specs=[pl.BlockSpec(out_shape.shape, lambda i, ids: (0, 0, 0, 0))] * seq_count,
+            scratch_shapes=[pltpu.VMEM((rows, depth), jnp.bfloat16)],
+        ),
+        out_shape=[out_shape] * seq_count,
+        compiler_params=params(),
+        name="space_grad",
+    )(ids, *operands)
+
+
+def space_backward_kernel(ids, q, k, v, probs, *rest):
+    pieces, (dq, dk, dv, spare) = rest[:-4], rest[-4:]
+    me = ids[0]
+    for step, piece in enumerate(pieces):
+        spare[:, me ^ step] = piece[0]
+    upstream = spare[...].reshape(q.shape[1:])
+    low = probs[0]
+    dv[0] = nn_dot(low, upstream).astype(jnp.bfloat16)
+    chance = nt_dot(v[0], upstream)
+    wide = low.astype(jnp.float32)
+    centre = jnp.sum(wide * chance, axis=0, keepdims=True)
+    score = (wide * (chance - centre)).astype(jnp.bfloat16)
+    dk[0] = (nn_dot(score, q[0]) * SCALE).astype(jnp.bfloat16)
+    dq[0] = (tn_dot(k[0], score) * SCALE).T.astype(jnp.bfloat16)
+
+
+def space_backward(ids, q, k, v, probs, pieces):
+    frames, patches, columns = q.shape
+    heads = columns // HD
+    _, band_count, time_len, _ = pieces[0].shape
+    wide = pl.BlockSpec((1, patches, HD), lambda f, h, ids: (f, 0, h))
+    piece = pl.BlockSpec((1, band_count, time_len, HD), lambda f, h, ids: (f, 0, 0, h))
+    square = pl.BlockSpec((1, patches, patches), lambda f, h, ids: (f * heads + h, 0, 0))
+    return pl.pallas_call(
+        space_backward_kernel,
+        grid_spec=pltpu.PrefetchScalarGridSpec(
+            num_scalar_prefetch=1,
+            grid=(frames, heads),
+            in_specs=[wide, wide, wide, square] + [piece] * len(pieces),
+            out_specs=[wide, wide, wide],
+            scratch_shapes=[pltpu.VMEM((band_count, len(pieces), time_len, HD), jnp.bfloat16)],
+        ),
+        out_shape=[jax.ShapeDtypeStruct(q.shape, jnp.bfloat16)] * 3,
+        compiler_params=params(),
+        name="space_backward",
+    )(ids, q, k, v, probs, *pieces)
+
+
+def on_small_slice(q_space, k_space, v_space, q_time, k_time, out_weight, cotangent):
+    seq_count, band_count = lax.axis_size("seq"), lax.axis_size("sub")
+    time_len = q_space.shape[1] // band_count // seq_count
+    me, sub, part = lax.axis_index("seq"), lax.axis_index("sub"), lax.axis_index("parts")
+    ids = jnp.stack([me, sub, part]).astype(jnp.int32)
+    rows, width = out_weight.shape
+
+    cot = [None] * seq_count
+    for step in (2, 3, 1, 0):
+        own = lax.dynamic_slice_in_dim(cotangent, (me ^ step) * time_len, time_len, 1)
+        cot[step] = own if step == 0 else xor_send(own, "seq", step)
+    half = lax.dynamic_slice_in_dim(out_weight, part * (rows // 2), rows // 2, 0)
+    second = xor_send(half, "seq", 2)
+    first = xor_send(half, "seq", 1)
+    third = xor_send(second, "seq", 1)
+    mine = [first, second, third]
+    theirs = [swap_parts(piece) for piece in mine]
+    bands = [cot, None, None, None]
+    bands[2] = [xor_send(piece, "sub", 2) for piece in cot]
+    bands[1] = [xor_send(piece, "sub", 1) for piece in cot]
+    bands[3] = [xor_send(piece, "sub", 1) for piece in bands[2]]
+    cots = [piece for band in bands for piece in band]
+
+    pieces, probs = space_forward(ids, q_space, k_space, v_space, seq_count, band_count, time_len)
+    moved = [pieces[0]] + [xor_send(pieces[step], "seq", step) for step in range(1, seq_count)]
+    chances, chances_t = time_probs(ids, q_time, k_time, seq_count)
+
+    back = space_grad(ids, chances_t, out_weight, mine, theirs, cots, seq_count, band_count)
+    returned = [back[0]] + [xor_send(back[step], "seq", step) for step in range(1, seq_count)]
+
+    mixed = time_out(ids, chances, moved).reshape(-1, rows)
+    third_sum = weight_grad(ids, mixed, cots, 3, width, jnp.bfloat16)
+    second_sum = weight_grad(ids, mixed, cots, 2, width, jnp.float32)
+    first_sum = weight_grad(ids, mixed, cots, 1, width, jnp.bfloat16)
+    own_sum = weight_grad(ids, mixed, cots, 0, width, jnp.float32)
+    paired = (second_sum + xor_send(third_sum, "seq", 1).astype(jnp.float32)).astype(jnp.bfloat16)
+    near = xor_send(first_sum, "seq", 1).astype(jnp.float32)
+    far = xor_send(paired, "seq", 2).astype(jnp.float32)
+    d_weight = own_sum + near + far
+
+    dq, dk, dv = space_backward(ids, q_space, k_space, v_space, probs, returned)
+    return dq, dk, dv, d_weight
+
+
 def solution(mesh):
     in_specs = (
         P(("parts", "seq"), None, "sub"),
@@ -131,6 +419,7 @@
         P(("parts", "seq"), None, "sub"),
         P(("parts", "sub"), "seq"),
     )
+    small = (mesh.shape["parts"], mesh.shape["seq"], mesh.shape["sub"]) == (2, 4, 4)
     return jax.shard_map(
-        on_device, mesh=mesh, in_specs=in_specs, out_specs=out_specs, check_vma=False
-    )
+        on_small_slice if small else on_device, mesh=mesh, in_specs=in_specs, out_specs=out_specs, check_vma=False
+    )

time: 301 us -> 240 us (0.80)
  blocking collectives: 146 us -> 0 us
  waiting for transfers between devices: 37 us -> 123 us
  matrix products: 73.3 us -> 0 us
  Pallas kernels: 0 us -> 72.4 us
  starting transfers between devices: 6.55 us -> 34.9 us
  local copies, waits for them, and re-layouts: 21.2 us -> 2.97 us
  between operations: 14 us -> 1 us
    all_to_all x3 -> x0, blocking collectives: 146 us -> none  [the longest x1 57.4 us: on_device(): lax.all_to_all(rounded, 'seq', split_axis=2, concat_axis=0, tiled=True)]
    ppermute x0 -> x30, waiting for transfers between devices: none -> 123 us  [the longest x27 116 us: xor_send(): return lax.ppermute(value, axis, [(i, i ^ distance) for i in range(count)])]
    pallas_call x0 -> x9, Pallas kernels: none -> 72.4 us  [the longest x4 21.2 us: weight_grad(): pl.pallas_call(weight_grad_kernel, grid_spec=pltpu.PrefetchScalarGridSpec...]
    dot_general x9 -> x0, matrix products: 63.5 us -> none  [the longest x1 15.2 us: on_device(): jnp.einsum('fhqk,fkhd->fqhd', score_grad, space_keys, preferred_element_t...]
    ppermute x0 -> x30, starting transfers between devices: none -> 34.9 us  [the longest x27 31.4 us: xor_send(): return lax.ppermute(value, axis, [(i, i ^ distance) for i in range(count)])]
    all_gather x2 -> x0, waiting for transfers between devices: 18.4 us -> none  [the longest x1 18.3 us: on_device(): weight_rows = lax.all_gather(out_weight, 'seq', axis=1, tiled=True)]
    all_to_all x1 -> x0, waiting for transfers between devices: 17.3 us -> none  [on_device(): lax.all_to_all(space_out.reshape(frame_count, band_count, band_len, colum...]
    reshape x13 -> x0, local copies, waits for them, and re-layouts: 12.3 us -> none  [the longest x2 2.22 us: on_device(): space_out.reshape(frame_count, band_count, band_len, columns)]
  transfers between devices with their start and end apart: 4 -> 30, of which waited for: 2 -> 11; matrix products, arithmetic and copies ran while one was open for 31% -> 1% of each run, Pallas kernels for 0% -> 24%
where the time goes in v1:
time: 240 us; the launch traced here: 238 us
  waiting for transfers between devices  123 us (51%)
  Pallas kernels  72.4 us (30%)
  starting transfers between devices  34.9 us (15%)
  other arithmetic  3.58 us (1%)
  local copies, waits for them, and re-layouts  2.97 us (1%)
    ppermute x27, waiting for transfers between devices, xor_send(): return lax.ppermute(value, axis, [(i, i ^ distance) for i in range(count)])  116 us
    ppermute x27, starting transfers between devices, xor_send(): return lax.ppermute(value, axis, [(i, i ^ distance) for i in range(count)])  31.4 us
    pallas_call x4, Pallas kernels, weight_grad(): pl.pallas_call(weight_grad_kernel, grid_spec=pltpu.PrefetchScalarGridSpec...  21.2 us
    pallas_call x1, Pallas kernels, time_probs(): pl.pallas_call(functools.partial(time_probs_kernel, seq_count=seq_count),...  13 us
    pallas_call x1, Pallas kernels, space_backward(): pl.pallas_call(space_backward_kernel, grid_spec=pltpu.PrefetchScalarGridS...  11.7 us
    pallas_call x1, Pallas kernels, space_forward(): pl.pallas_call(space_forward_kernel, grid_spec=pltpu.PrefetchScalarGridSp...  11 us
    pallas_call x1, Pallas kernels, space_grad(): pl.pallas_call(functools.partial(space_grad_kernel, seq_count=seq_count,...  10.6 us
    ppermute x3, waiting for transfers between devices, swap_parts(): return lax.ppermute(value, 'parts', [(0, 1), (1, 0)])  6.87 us
  transfers between devices with their start and end apart: 30, of which 11 were waited for; matrix products, arithmetic and copies ran while one was open for 1% of the time, Pallas kernels for 24%

profile of v1, /device:TPU:0, one launch (start us, length us, event | category | flops | bytes accessed | tf_op | source)
XLA Modules:
  0.0 237.8 jit_solution(12124925512308925103)
XLA Ops:
  0.6 0.7 pad_add_fusion.ids
  1.3 11.0 %space_forward.1 = (bf16[2,4,32,512]{3,2,1,0:T(8,128)(2,1)}, bf16[2,4,32,512]{3,2,1,0:T(8,128)(2,1)}, bf16[2,4,32,512]{3,2,1,0:T(8,128)(2,1)}, bf16[2,4,32,512]{3,2,1,0:T(8,128)(2,1)}, bf16[8,512,512]{2,1,0:T(8,128)(2,1)}) custom-call(s32[3]{0:T(128)} %pad_add_fusion.ids, bf16[2,512,512]{2,1,0:T(8,128)(2,1)} %q.5, bf16[2,512,512]{2,1,0:T(8,128)(2,1)} %k.5, ...), custom_call_target="tpu_custom_call" | custom-call | tf_op jit(solution)/shard_map/space_forward/pallas_call | solution.py:171
  12.3 3.0 %collective-permute-start.24 = (bf16[2,4,32,512]{3,2,1,0:T(8,128)(2,1)}, bf16[2,4,32,512]{3,2,1,0:T(8,128)(2,1)S(1)}, u32[]{:S(2)}, u32[]{:S(2)}) collective-permute-start(bf16[2,4,32,512]{3,2,1,0:T(8,128)(2,1)} %get-tuple-element.29), channel_id=1, source_target_pairs={{0,4},{4,0},{8,12},{12,8},{1,5},{5,1},{9,13},{13,9},{2,6},{6,2},{1... | collective-permute-start | bytes 786440 | tf_op jit(solution)/shard_map/ppermute | solution.py:124
  15.3 2.6 %collective-permute-start.25 = (bf16[2,4,32,512]{3,2,1,0:T(8,128)(2,1)}, bf16[2,4,32,512]{3,2,1,0:T(8,128)(2,1)S(1)}, u32[]{:S(2)}, u32[]{:S(2)}) collective-permute-start(bf16[2,4,32,512]{3,2,1,0:T(8,128)(2,1)} %get-tuple-element.30), channel_id=1, source_target_pairs={{0,8},{4,12},{8,0},{12,4},{1,9},{5,13},{9,1},{13,5},{2,10},{6,14},... | collective-permute-start | bytes 786440 | tf_op jit(solution)/shard_map/ppermute | solution.py:124
  17.9 0.1 constant_dynamic-slice_fusion
  18.1 3.9 %collective-permute-start.8 = (bf16[2,32,3072]{2,1,0:T(8,128)(2,1)S(1)}, bf16[2,32,3072]{2,1,0:T(8,128)(2,1)S(1)}, u32[]{:S(2)}, u32[]{:S(2)}) collective-permute-start(bf16[2,32,3072]{2,1,0:T(8,128)(2,1)S(1)} %get-tuple-element.32), channel_id=1, source_target_pairs={{0,12},{4,8},{8,4},{12,0},{1,13},{5,9},{9,5},{13,1},{2,14},{6,10},... | collective-permute-start | bytes 1179656 | tf_op jit(solution)/shard_map/ppermute | solution.py:124
  22.0 5.5 %collective-permute-done.24.rest_1_ = bf16[2,4,32,512]{3,2,1,0:T(8,128)(2,1)S(1)} collective-permute-done((bf16[2,4,32,512]{3,2,1,0:T(8,128)(2,1)}, bf16[2,4,32,512]{3,2,1,0:T(8,128)(2,1)S(1)}, u32[]{:S(2)}, u32[]{:S(2)}) %collective-permute-start.24) | collective-permute-done | bytes 262176 | tf_op jit(solution)/shard_map/ppermute | solution.py:124
  27.5 2.3 collective-permute-start.7
  29.8 15.6 %collective-permute-done.25.rest_2_ = bf16[2,4,32,512]{3,2,1,0:T(8,128)(2,1)S(1)} collective-permute-done((bf16[2,4,32,512]{3,2,1,0:T(8,128)(2,1)}, bf16[2,4,32,512]{3,2,1,0:T(8,128)(2,1)S(1)}, u32[]{:S(2)}, u32[]{:S(2)}) %collective-permute-start.25) | collective-permute-done | bytes 262176 | tf_op jit(solution)/shard_map/ppermute | solution.py:124
  45.4 1.5 collective-permute-start.13
  46.9 0.6 collective-permute-start.16
  47.5 2.9 %collective-permute-done.6.rest_7_.rest_1_ = bf16[2,32,3072]{2,1,0:T(8,128)(2,1)S(1)} collective-permute-done((bf16[2,32,3072]{2,1,0:T(8,128)(2,1)S(1)}, bf16[2,32,3072]{2,1,0:T(8,128)(2,1)S(1)}, u32[]{:S(2)}, u32[]{:S(2)}) %collective-permute-start.6) | collective-permute-done | bytes 393248 | tf_op jit(solution)/shard_map/ppermute | solution.py:124
  50.5 24.4 %collective-permute-done.7.rest_8_.rest_2_ = bf16[2,32,3072]{2,1,0:T(8,128)(2,1)S(1)} collective-permute-done((bf16[2,32,3072]{2,1,0:T(8,128)(2,1)S(1)}, bf16[2,32,3072]{2,1,0:T(8,128)(2,1)S(1)}, u32[]{:S(2)}, u32[]{:S(2)}) %collective-permute-start.7) | collective-permute-done | bytes 393248 | tf_op jit(solution)/shard_map/ppermute | solution.py:124
  74.9 1.5 collective-permute-start.14
  76.4 0.6 collective-permute-start.15
  77.0 0.2 collective-permute-start.11
  77.2 0.4 collective-permute-start.17
  77.5 9.4 %collective-permute-done.14.rest_15_.rest_9_ = bf16[2,32,3072]{2,1,0:T(8,128)(2,1)S(1)} collective-permute-done((bf16[2,32,3072]{2,1,0:T(8,128)(2,1)S(1)}, bf16[2,32,3072]{2,1,0:T(8,128)(2,1)S(1)}, u32[]{:S(2)}, u32[]{:S(2)}) %collective-permute-start.14) | collective-permute-done | bytes 393248 | tf_op jit(solution)/shard_map/ppermute | solution.py:124
  86.9 0.5 collective-permute-start.18
  87.4 5.6 %collective-permute-done.15.rest_16_.rest_10_ = bf16[2,32,3072]{2,1,0:T(8,128)(2,1)S(1)} collective-permute-done((bf16[2,32,3072]{2,1,0:T(8,128)(2,1)S(1)}, bf16[2,32,3072]{2,1,0:T(8,128)(2,1)S(1)}, u32[]{:S(2)}, u32[]{:S(2)}) %collective-permute-start.15) | collective-permute-done | bytes 393248 | tf_op jit(solution)/shard_map/ppermute | solution.py:124
  93.0 13.0 %time_probs.1 = (bf16[4,4,256,256]{3,2,1,0:T(8,128)(2,1)}, bf16[4,4,256,256]{3,2,1,0:T(8,128)(2,1)}) custom-call(s32[3]{0:T(128)} %pad_add_fusion.ids, bf16[8,4,32,512]{3,2,1,0:T(8,128)(2,1)} %q.4, bf16[8,4,32,512]{3,2,1,0:T(8,128)(2,1)} %k.4), custom_call_target="tpu_custom_call" | custom-call | tf_op jit(solution)/shard_map/time_probs/pallas_call | solution.py:212
  106.0 4.8 %time_out.1 = bf16[4,256,512]{2,1,0:T(8,128)(2,1)} custom-call(s32[3]{0:T(128)} %pad_add_fusion.ids, bf16[4,4,256,256]{3,2,1,0:T(8,128)(2,1)} %get-tuple-element.27.probs, bf16[2,4,32,512]{3,2,1,0:T(8,128)(2,1)} %get-tuple-element.28.rest_0_, bf16[2,4,32,512]{3,2,1,0:T(8,128)(2,1)} %copy-done.25, bf16[2,4,32,512]{3,2,1,0:T(8,128)(2,1)} %copy-done.26, ...), custom_call_target="tpu_custom_call" | custom-call | tf_op jit(solution)/shard_map/time_out/pallas_call | solution.py:239
  111.1 0.7 copy-done.11
  112.2 5.3 %weight_grad.7 = bf16[512,768]{1,0:T(8,128)(2,1)} custom-call(s32[3]{0:T(128)} %pad_add_fusion.ids, bf16[1024,512]{1,0:T(8,128)(2,1)} %bitcast.4, bf16[2,32,3072]{2,1,0:T(8,128)(2,1)} %copy-done, bf16[2,32,3072]{2,1,0:T(8,128)(2,1)} %copy-done.2, bf16[2,32,3072]{2,1,0:T(8,128)(2,1)} %copy-done.3, bf16[2,32,3072]{2,1,0:T(8,128)(2,1)} %copy-done.1, ...), custom_call_target="tpu_custom_call" | custom-call | tf_op jit(solution)/shard_map/weight_grad/pallas_call | solution.py:265
  117.6 0.6 collective-permute-start.28
  118.2 2.6 %collective-permute-start.1 = (bf16[256,768]{1,0:T(8,128)(2,1)S(1)}, bf16[256,768]{1,0:T(8,128)(2,1)S(1)}, u32[]{:S(2)}, u32[]{:S(2)}) collective-permute-start(bf16[256,768]{1,0:T(8,128)(2,1)S(1)} %constant_dynamic-slice_fusion.4), channel_id=1, source_target_pairs={{0,8},{4,12},{8,0},{12,4},{1,9},{5,13},{9,1},{13,5},{2,10},{6,14},... | collective-permute-start | bytes 1179656 | tf_op jit(solution)/shard_map/ppermute | solution.py:124
  120.8 0.6 collective-permute-start
  121.4 23.3 %collective-permute-done.1.rest_1_ = bf16[256,768]{1,0:T(8,128)(2,1)S(1)} collective-permute-done((bf16[256,768]{1,0:T(8,128)(2,1)S(1)}, bf16[256,768]{1,0:T(8,128)(2,1)S(1)}, u32[]{:S(2)}, u32[]{:S(2)}) %collective-permute-start.1) | collective-permute-done | bytes 393248 | tf_op jit(solution)/shard_map/ppermute | solution.py:124
  144.7 3.5 %collective-permute-start.2 = (bf16[256,768]{1,0:T(8,128)(2,1)S(1)}, bf16[256,768]{1,0:T(8,128)(2,1)S(1)}, u32[]{:S(2)}, u32[]{:S(2)}) collective-permute-start(bf16[256,768]{1,0:T(8,128)(2,1)S(1)} %collective-permute-done.1.rest_1_), channel_id=1, source_target_pairs={{0,4},{4,0},{8,12},{12,8},{1,5},{5,1},{9,13},{13,9},{2,6},{6,2},{1... | collective-permute-start | bytes 1179656 | tf_op jit(solution)/shard_map/ppermute | solution.py:124
  148.2 5.2 %weight_grad.5 = bf16[512,768]{1,0:T(8,128)(2,1)} custom-call(s32[3]{0:T(128)} %pad_add_fusion.ids, bf16[1024,512]{1,0:T(8,128)(2,1)} %bitcast.5, bf16[2,32,3072]{2,1,0:T(8,128)(2,1)} %copy-done, bf16[2,32,3072]{2,1,0:T(8,128)(2,1)} %copy-done.2, bf16[2,32,3072]{2,1,0:T(8,128)(2,1)} %copy-done.3, bf16[2,32,3072]{2,1,0:T(8,128)(2,1)} %copy-done.1, ...), custom_call_target="tpu_custom_call" | custom-call | tf_op jit(solution)/shard_map/weight_grad/pallas_call | solution.py:265
  153.5 5.4 %weight_grad.6 = f32[512,768]{1,0:T(8,128)} custom-call(s32[3]{0:T(128)} %pad_add_fusion.ids, bf16[1024,512]{1,0:T(8,128)(2,1)} %bitcast.6, bf16[2,32,3072]{2,1,0:T(8,128)(2,1)} %copy-done, bf16[2,32,3072]{2,1,0:T(8,128)(2,1)} %copy-done.2, bf16[2,32,3072]{2,1,0:T(8,128)(2,1)} %copy-done.3, bf16[2,32,3072]{2,1,0:T(8,128)(2,1)} %copy-done.1, ...), custom_call_target="tpu_custom_call" | custom-call | tf_op jit(solution)/shard_map/weight_grad/pallas_call | solution.py:265
  158.9 1.6 add_convert_fusion
  160.4 1.9 collective-permute-start.29
  162.4 1.5 collective-permute-start.4
  163.9 0.5 collective-permute-start.3
  164.4 15.9 %collective-permute-done.2.rest_2_ = bf16[256,768]{1,0:T(8,128)(2,1)S(1)} collective-permute-done((bf16[256,768]{1,0:T(8,128)(2,1)S(1)}, bf16[256,768]{1,0:T(8,128)(2,1)S(1)}, u32[]{:S(2)}, u32[]{:S(2)}) %collective-permute-start.2) | collective-permute-done | bytes 393248 | tf_op jit(solution)/shard_map/ppermute | solution.py:124
  180.3 1.5 collective-permute-start.5
  181.9 1.0 collective-permute-done.3.rest_3_
  182.8 5.9 %collective-permute-done.5.rest_5_ = bf16[256,768]{1,0:T(8,128)(2,1)S(1)} collective-permute-done((bf16[256,768]{1,0:T(8,128)(2,1)S(1)}, bf16[256,768]{1,0:T(8,128)(2,1)S(1)}, u32[]{:S(2)}, u32[]{:S(2)}) %collective-permute-start.5) | collective-permute-done | bytes 393248 | tf_op jit(solution)/shard_map/ppermute | solution.py:128
  188.8 0.7 copy-done.24
  189.5 10.6 %space_grad.1 = (bf16[2,4,32,512]{3,2,1,0:T(8,128)(2,1)}, bf16[2,4,32,512]{3,2,1,0:T(8,128)(2,1)}, bf16[2,4,32,512]{3,2,1,0:T(8,128)(2,1)}, bf16[2,4,32,512]{3,2,1,0:T(8,128)(2,1)}) custom-call(s32[3]{0:T(128)} %pad_add_fusion.ids, bf16[4,4,256,256]{3,2,1,0:T(8,128)(2,1)} %get-tuple-element.19.probs_t, bf16[512,768]{1,0:T(8,128)(2,1)} %own.1, ...), custom_call_target="tpu_custom_call" | custom-call | tf_op jit(solution)/shard_map/space_grad/pallas_call | solution.py:309
  200.1 0.6 collective-permute-start.21
  200.7 4.5 %collective-permute-start.22 = (bf16[2,4,32,512]{3,2,1,0:T(8,128)(2,1)}, bf16[2,4,32,512]{3,2,1,0:T(8,128)(2,1)S(1)}, u32[]{:S(2)}, u32[]{:S(2)}) collective-permute-start(bf16[2,4,32,512]{3,2,1,0:T(8,128)(2,1)} %get-tuple-element.22), channel_id=1, source_target_pairs={{0,8},{4,12},{8,0},{12,4},{1,9},{5,13},{9,1},{13,5},{2,10},{6,14},... | collective-permute-start | bytes 786440 | tf_op jit(solution)/shard_map/ppermute | solution.py:124
  205.2 5.3 %weight_grad.4 = f32[512,768]{1,0:T(8,128)} custom-call(s32[3]{0:T(128)} %pad_add_fusion.ids, bf16[1024,512]{1,0:T(8,128)(2,1)} %bitcast.7, bf16[2,32,3072]{2,1,0:T(8,128)(2,1)} %copy-done, bf16[2,32,3072]{2,1,0:T(8,128)(2,1)} %copy-done.2, bf16[2,32,3072]{2,1,0:T(8,128)(2,1)} %copy-done.3, bf16[2,32,3072]{2,1,0:T(8,128)(2,1)} %copy-done.1, ...), custom_call_target="tpu_custom_call" | custom-call | tf_op jit(solution)/shard_map/weight_grad/pallas_call | solution.py:265
  210.6 13.3 %collective-permute-done.22.rest_2_ = bf16[2,4,32,512]{3,2,1,0:T(8,128)(2,1)S(1)} collective-permute-done((bf16[2,4,32,512]{3,2,1,0:T(8,128)(2,1)}, bf16[2,4,32,512]{3,2,1,0:T(8,128)(2,1)S(1)}, u32[]{:S(2)}, u32[]{:S(2)}) %collective-permute-start.22) | collective-permute-done | bytes 262176 | tf_op jit(solution)/shard_map/ppermute | solution.py:124
  223.9 0.7 copy-done.29
  224.7 11.7 %space_backward.1 = (bf16[2,512,512]{2,1,0:T(8,128)(2,1)}, bf16[2,512,512]{2,1,0:T(8,128)(2,1)}, bf16[2,512,512]{2,1,0:T(8,128)(2,1)}) custom-call(s32[3]{0:T(128)} %pad_add_fusion.ids, bf16[2,512,512]{2,1,0:T(8,128)(2,1)} %q.5, bf16[2,512,512]{2,1,0:T(8,128)(2,1)} %k.5, bf16[2,512,512]{2,1,0:T(8,128)(2,1)} %v.3, ...), custom_call_target="tpu_custom_call" | custom-call | tf_op jit(solution)/shard_map/space_backward/pallas_call | solution.py:347
  236.4 1.3 convert_add_fusion
  (88 shorter events, 0.9 us)
Async XLA Ops:
  1.3 16.6 %copy-start.18 = (bf16[2,128,3072]{2,1,0:T(8,128)(2,1)S(1)}, bf16[2,128,3072]{2,1,0:T(8,128)(2,1)}, u32[]{:S(2)}) copy-start(bf16[2,128,3072]{2,1,0:T(8,128)(2,1)} %param.13) | copy-start | bytes 4718596
  12.3 15.2 %collective-permute-start.24 = (bf16[2,4,32,512]{3,2,1,0:T(8,128)(2,1)}, bf16[2,4,32,512]{3,2,1,0:T(8,128)(2,1)S(1)}, u32[]{:S(2)}, u32[]{:S(2)}) collective-permute-start(bf16[2,4,32,512]{3,2,1,0:T(8,128)(2,1)} %get-tuple-element.29), channel_id=1, source_target_pairs={{0,4},{4,0},{8,12},{12,8},{1,5},{5,1},{9,13},{13,9},{2,6},{6,2},{1... | collective-permute-start | bytes 786440 | tf_op jit(solution)/shard_map/ppermute | solution.py:124
  15.3 30.0 %collective-permute-start.25 = (bf16[2,4,32,512]{3,2,1,0:T(8,128)(2,1)}, bf16[2,4,32,512]{3,2,1,0:T(8,128)(2,1)S(1)}, u32[]{:S(2)}, u32[]{:S(2)}) collective-permute-start(bf16[2,4,32,512]{3,2,1,0:T(8,128)(2,1)} %get-tuple-element.30), channel_id=1, source_target_pairs={{0,8},{4,12},{8,0},{12,4},{1,9},{5,13},{9,1},{13,5},{2,10},{6,14},... | collective-permute-start | bytes 786440 | tf_op jit(solution)/shard_map/ppermute | solution.py:124
  17.9 29.0 %collective-permute-start.26 = (bf16[2,4,32,512]{3,2,1,0:T(8,128)(2,1)}, bf16[2,4,32,512]{3,2,1,0:T(8,128)(2,1)S(1)}, u32[]{:S(2)}, u32[]{:S(2)}) collective-permute-start(bf16[2,4,32,512]{3,2,1,0:T(8,128)(2,1)} %get-tuple-element.31), channel_id=1, source_target_pairs={{0,12},{4,8},{8,4},{12,0},{1,13},{5,9},{9,5},{13,1},{2,14},{6,10},... | collective-permute-start | bytes 786440 | tf_op jit(solution)/shard_map/ppermute | solution.py:124
  18.1 92.8 %copy-start = (bf16[2,32,3072]{2,1,0:T(8,128)(2,1)}, bf16[2,32,3072]{2,1,0:T(8,128)(2,1)S(1)}, u32[]{:S(2)}) copy-start(bf16[2,32,3072]{2,1,0:T(8,128)(2,1)S(1)} %get-tuple-element.34.rest_6_.rest_0_) | copy-start | bytes 1179652
  18.1 28.8 %collective-permute-start.8 = (bf16[2,32,3072]{2,1,0:T(8,128)(2,1)S(1)}, bf16[2,32,3072]{2,1,0:T(8,128)(2,1)S(1)}, u32[]{:S(2)}, u32[]{:S(2)}) collective-permute-start(bf16[2,32,3072]{2,1,0:T(8,128)(2,1)S(1)} %get-tuple-element.32), channel_id=1, source_target_pairs={{0,12},{4,8},{8,4},{12,0},{1,13},{5,9},{9,5},{13,1},{2,14},{6,10},... | collective-permute-start | bytes 1179656 | tf_op jit(solution)/shard_map/ppermute | solution.py:124
  22.0 28.5 %collective-permute-start.6 = (bf16[2,32,3072]{2,1,0:T(8,128)(2,1)S(1)}, bf16[2,32,3072]{2,1,0:T(8,128)(2,1)S(1)}, u32[]{:S(2)}, u32[]{:S(2)}) collective-permute-start(bf16[2,32,3072]{2,1,0:T(8,128)(2,1)S(1)} %get-tuple-element.33), channel_id=1, source_target_pairs={{0,4},{4,0},{8,12},{12,8},{1,5},{5,1},{9,13},{13,9},{2,6},{6,2},{1... | collective-permute-start | bytes 1179656 | tf_op jit(solution)/shard_map/ppermute | solution.py:124
  27.5 78.5 %copy-start.25 = (bf16[2,4,32,512]{3,2,1,0:T(8,128)(2,1)}, bf16[2,4,32,512]{3,2,1,0:T(8,128)(2,1)S(1)}, u32[]{:S(2)}) copy-start(bf16[2,4,32,512]{3,2,1,0:T(8,128)(2,1)S(1)} %collective-permute-done.24.rest_1_) | copy-start | bytes 786436
  27.5 47.3 %collective-permute-start.7 = (bf16[2,32,3072]{2,1,0:T(8,128)(2,1)S(1)}, bf16[2,32,3072]{2,1,0:T(8,128)(2,1)S(1)}, u32[]{:S(2)}, u32[]{:S(2)}) collective-permute-start(bf16[2,32,3072]{2,1,0:T(8,128)(2,1)S(1)} %get-tuple-element.35), channel_id=1, source_target_pairs={{0,8},{4,12},{8,0},{12,4},{1,9},{5,13},{9,1},{13,5},{2,10},{6,14},... | collective-permute-start | bytes 1179656 | tf_op jit(solution)/shard_map/ppermute | solution.py:124
  45.4 60.6 %copy-start.26 = (bf16[2,4,32,512]{3,2,1,0:T(8,128)(2,1)}, bf16[2,4,32,512]{3,2,1,0:T(8,128)(2,1)S(1)}, u32[]{:S(2)}) copy-start(bf16[2,4,32,512]{3,2,1,0:T(8,128)(2,1)S(1)} %collective-permute-done.25.rest_2_) | copy-start | bytes 786436
  45.4 31.0 %collective-permute-start.13 = (bf16[2,32,3072]{2,1,0:T(8,128)(2,1)S(1)}, bf16[2,32,3072]{2,1,0:T(8,128)(2,1)S(1)}, u32[]{:S(2)}, u32[]{:S(2)}) collective-permute-start(bf16[2,32,3072]{2,1,0:T(8,128)(2,1)S(1)} %get-tuple-element.34.rest_6_.rest_0_), channel_id=1, source_target_pairs={{0,2},{1,3},{2,0},{3,1},{4,6},{5,7},{6,4},{7,5},{8,10},{9,11},{10,... | collective-permute-start | bytes 1179656 | tf_op jit(solution)/shard_map/ppermute | solution.py:124
  46.9 59.1 %copy-start.27 = (bf16[2,4,32,512]{3,2,1,0:T(8,128)(2,1)}, bf16[2,4,32,512]{3,2,1,0:T(8,128)(2,1)S(1)}, u32[]{:S(2)}) copy-start(bf16[2,4,32,512]{3,2,1,0:T(8,128)(2,1)S(1)} %collective-permute-done.26.rest_3_) | copy-start | bytes 786436
  46.9 29.5 %collective-permute-start.9 = (bf16[2,32,3072]{2,1,0:T(8,128)(2,1)S(1)}, bf16[2,32,3072]{2,1,0:T(8,128)(2,1)S(1)}, u32[]{:S(2)}, u32[]{:S(2)}) collective-permute-start(bf16[2,32,3072]{2,1,0:T(8,128)(2,1)S(1)} %get-tuple-element.34.rest_6_.rest_0_), channel_id=1, source_target_pairs={{0,1},{1,0},{2,3},{3,2},{4,5},{5,4},{6,7},{7,6},{8,9},{9,8},{10,11... | collective-permute-start | bytes 1179656 | tf_op jit(solution)/shard_map/ppermute | solution.py:124
  46.9 64.0 %copy-start.1 = (bf16[2,32,3072]{2,1,0:T(8,128)(2,1)}, bf16[2,32,3072]{2,1,0:T(8,128)(2,1)S(1)}, u32[]{:S(2)}) copy-start(bf16[2,32,3072]{2,1,0:T(8,128)(2,1)S(1)} %collective-permute-done.8.rest_9_.rest_3_) | copy-start | bytes 1179652
  46.9 30.1 %collective-permute-start.16 = (bf16[2,32,3072]{2,1,0:T(8,128)(2,1)S(1)}, bf16[2,32,3072]{2,1,0:T(8,128)(2,1)S(1)}, u32[]{:S(2)}, u32[]{:S(2)}) collective-permute-start(bf16[2,32,3072]{2,1,0:T(8,128)(2,1)S(1)} %collective-permute-done.8.rest_9_.rest_3_), channel_id=1, source_target_pairs={{0,2},{1,3},{2,0},{3,1},{4,6},{5,7},{6,4},{7,5},{8,10},{9,11},{10,... | collective-permute-start | bytes 1179656 | tf_op jit(solution)/shard_map/ppermute | solution.py:124
  50.5 60.4 %copy-start.2 = (bf16[2,32,3072]{2,1,0:T(8,128)(2,1)}, bf16[2,32,3072]{2,1,0:T(8,128)(2,1)S(1)}, u32[]{:S(2)}) copy-start(bf16[2,32,3072]{2,1,0:T(8,128)(2,1)S(1)} %collective-permute-done.6.rest_7_.rest_1_) | copy-start | bytes 1179652
  50.5 26.7 %collective-permute-start.12 = (bf16[2,32,3072]{2,1,0:T(8,128)(2,1)S(1)}, bf16[2,32,3072]{2,1,0:T(8,128)(2,1)S(1)}, u32[]{:S(2)}, u32[]{:S(2)}) collective-permute-start(bf16[2,32,3072]{2,1,0:T(8,128)(2,1)S(1)} %collective-permute-done.8.rest_9_.rest_3_), channel_id=1, source_target_pairs={{0,1},{1,0},{2,3},{3,2},{4,5},{5,4},{6,7},{7,6},{8,9},{9,8},{10,11... | collective-permute-start | bytes 1179656 | tf_op jit(solution)/shard_map/ppermute | solution.py:124
  74.9 36.0 %copy-start.3 = (bf16[2,32,3072]{2,1,0:T(8,128)(2,1)}, bf16[2,32,3072]{2,1,0:T(8,128)(2,1)S(1)}, u32[]{:S(2)}) copy-start(bf16[2,32,3072]{2,1,0:T(8,128)(2,1)S(1)} %collective-permute-done.7.rest_8_.rest_2_) | copy-start | bytes 1179652
  74.9 12.1 %collective-permute-start.14 = (bf16[2,32,3072]{2,1,0:T(8,128)(2,1)S(1)}, bf16[2,32,3072]{2,1,0:T(8,128)(2,1)S(1)}, u32[]{:S(2)}, u32[]{:S(2)}) collective-permute-start(bf16[2,32,3072]{2,1,0:T(8,128)(2,1)S(1)} %collective-permute-done.6.rest_7_.rest_1_), channel_id=1, source_target_pairs={{0,2},{1,3},{2,0},{3,1},{4,6},{5,7},{6,4},{7,5},{8,10},{9,11},{10,... | collective-permute-start | bytes 1179656 | tf_op jit(solution)/shard_map/ppermute | solution.py:124
  76.4 34.5 %copy-start.4 = (bf16[2,32,3072]{2,1,0:T(8,128)(2,1)}, bf16[2,32,3072]{2,1,0:T(8,128)(2,1)S(1)}, u32[]{:S(2)}) copy-start(bf16[2,32,3072]{2,1,0:T(8,128)(2,1)S(1)} %collective-permute-done.13.rest_14_.rest_8_) | copy-start | bytes 1179652
  76.4 10.6 %collective-permute-start.10 = (bf16[2,32,3072]{2,1,0:T(8,128)(2,1)S(1)}, bf16[2,32,3072]{2,1,0:T(8,128)(2,1)S(1)}, u32[]{:S(2)}, u32[]{:S(2)}) collective-permute-start(bf16[2,32,3072]{2,1,0:T(8,128)(2,1)S(1)} %collective-permute-done.6.rest_7_.rest_1_), channel_id=1, source_target_pairs={{0,1},{1,0},{2,3},{3,2},{4,5},{5,4},{6,7},{7,6},{8,9},{9,8},{10,11... | collective-permute-start | bytes 1179656 | tf_op jit(solution)/shard_map/ppermute | solution.py:124
  76.4 34.5 %copy-start.5 = (bf16[2,32,3072]{2,1,0:T(8,128)(2,1)}, bf16[2,32,3072]{2,1,0:T(8,128)(2,1)S(1)}, u32[]{:S(2)}) copy-start(bf16[2,32,3072]{2,1,0:T(8,128)(2,1)S(1)} %collective-permute-done.9.rest_10_.rest_4_) | copy-start | bytes 1179652
  76.4 16.6 %collective-permute-start.15 = (bf16[2,32,3072]{2,1,0:T(8,128)(2,1)S(1)}, bf16[2,32,3072]{2,1,0:T(8,128)(2,1)S(1)}, u32[]{:S(2)}, u32[]{:S(2)}) collective-permute-start(bf16[2,32,3072]{2,1,0:T(8,128)(2,1)S(1)} %collective-permute-done.7.rest_8_.rest_2_), channel_id=1, source_target_pairs={{0,2},{1,3},{2,0},{3,1},{4,6},{5,7},{6,4},{7,5},{8,10},{9,11},{10,... | collective-permute-start | bytes 1179656 | tf_op jit(solution)/shard_map/ppermute | solution.py:124
  77.0 33.9 %copy-start.6 = (bf16[2,32,3072]{2,1,0:T(8,128)(2,1)}, bf16[2,32,3072]{2,1,0:T(8,128)(2,1)S(1)}, u32[]{:S(2)}) copy-start(bf16[2,32,3072]{2,1,0:T(8,128)(2,1)S(1)} %collective-permute-done.16.rest_17_.rest_11_) | copy-start | bytes 1179652
  77.0 34.0 %collective-permute-start.11 = (bf16[2,32,3072]{2,1,0:T(8,128)(2,1)S(1)}, bf16[2,32,3072]{2,1,0:T(8,128)(2,1)S(1)}, u32[]{:S(2)}, u32[]{:S(2)}) collective-permute-start(bf16[2,32,3072]{2,1,0:T(8,128)(2,1)S(1)} %collective-permute-done.7.rest_8_.rest_2_), channel_id=1, source_target_pairs={{0,1},{1,0},{2,3},{3,2},{4,5},{5,4},{6,7},{7,6},{8,9},{9,8},{10,11... | collective-permute-start | bytes 1179656 | tf_op jit(solution)/shard_map/ppermute | solution.py:124
  77.2 33.8 %copy-start.7 = (bf16[2,32,3072]{2,1,0:T(8,128)(2,1)}, bf16[2,32,3072]{2,1,0:T(8,128)(2,1)S(1)}, u32[]{:S(2)}) copy-start(bf16[2,32,3072]{2,1,0:T(8,128)(2,1)S(1)} %collective-permute-done.12.rest_13_.rest_7_) | copy-start | bytes 1179652
  77.2 33.8 %collective-permute-start.17 = (bf16[2,32,3072]{2,1,0:T(8,128)(2,1)S(1)}, bf16[2,32,3072]{2,1,0:T(8,128)(2,1)S(1)}, u32[]{:S(2)}, u32[]{:S(2)}) collective-permute-start(bf16[2,32,3072]{2,1,0:T(8,128)(2,1)S(1)} %collective-permute-done.13.rest_14_.rest_8_), channel_id=1, source_target_pairs={{0,1},{1,0},{2,3},{3,2},{4,5},{5,4},{6,7},{7,6},{8,9},{9,8},{10,11... | collective-permute-start | bytes 1179656 | tf_op jit(solution)/shard_map/ppermute | solution.py:124
  86.9 24.0 %copy-start.8 = (bf16[2,32,3072]{2,1,0:T(8,128)(2,1)}, bf16[2,32,3072]{2,1,0:T(8,128)(2,1)S(1)}, u32[]{:S(2)}) copy-start(bf16[2,32,3072]{2,1,0:T(8,128)(2,1)S(1)} %collective-permute-done.14.rest_15_.rest_9_) | copy-start | bytes 1179652
  86.9 24.1 %collective-permute-start.20 = (bf16[2,32,3072]{2,1,0:T(8,128)(2,1)S(1)}, bf16[2,32,3072]{2,1,0:T(8,128)(2,1)S(1)}, u32[]{:S(2)}, u32[]{:S(2)}) collective-permute-start(bf16[2,32,3072]{2,1,0:T(8,128)(2,1)S(1)} %collective-permute-done.16.rest_17_.rest_11_), channel_id=1, source_target_pairs={{0,1},{1,0},{2,3},{3,2},{4,5},{5,4},{6,7},{7,6},{8,9},{9,8},{10,11... | collective-permute-start | bytes 1179656 | tf_op jit(solution)/shard_map/ppermute | solution.py:124
  86.9 24.0 %copy-start.9 = (bf16[2,32,3072]{2,1,0:T(8,128)(2,1)}, bf16[2,32,3072]{2,1,0:T(8,128)(2,1)S(1)}, u32[]{:S(2)}) copy-start(bf16[2,32,3072]{2,1,0:T(8,128)(2,1)S(1)} %collective-permute-done.10.rest_11_.rest_5_) | copy-start | bytes 1179652
  86.9 24.1 %collective-permute-start.18 = (bf16[2,32,3072]{2,1,0:T(8,128)(2,1)S(1)}, bf16[2,32,3072]{2,1,0:T(8,128)(2,1)S(1)}, u32[]{:S(2)}, u32[]{:S(2)}) collective-permute-start(bf16[2,32,3072]{2,1,0:T(8,128)(2,1)S(1)} %collective-permute-done.14.rest_15_.rest_9_), channel_id=1, source_target_pairs={{0,1},{1,0},{2,3},{3,2},{4,5},{5,4},{6,7},{7,6},{8,9},{9,8},{10,11... | collective-permute-start | bytes 1179656 | tf_op jit(solution)/shard_map/ppermute | solution.py:124
  93.0 18.0 %copy-start.10 = (bf16[2,32,3072]{2,1,0:T(8,128)(2,1)}, bf16[2,32,3072]{2,1,0:T(8,128)(2,1)S(1)}, u32[]{:S(2)}) copy-start(bf16[2,32,3072]{2,1,0:T(8,128)(2,1)S(1)} %collective-permute-done.15.rest_16_.rest_10_) | copy-start | bytes 1179652
  93.0 18.1 %collective-permute-start.19 = (bf16[2,32,3072]{2,1,0:T(8,128)(2,1)S(1)}, bf16[2,32,3072]{2,1,0:T(8,128)(2,1)S(1)}, u32[]{:S(2)}, u32[]{:S(2)}) collective-permute-start(bf16[2,32,3072]{2,1,0:T(8,128)(2,1)S(1)} %collective-permute-done.15.rest_16_.rest_10_), channel_id=1, source_target_pairs={{0,1},{1,0},{2,3},{3,2},{4,5},{5,4},{6,7},{7,6},{8,9},{9,8},{10,11... | collective-permute-start | bytes 1179656 | tf_op jit(solution)/shard_map/ppermute | solution.py:124
  117.6 41.3 %collective-permute-start.28 = (bf16[512,768]{1,0:T(8,128)(2,1)}, bf16[512,768]{1,0:T(8,128)(2,1)S(1)}, u32[]{:S(2)}, u32[]{:S(2)}) collective-permute-start(bf16[512,768]{1,0:T(8,128)(2,1)} %weight_grad.7), channel_id=1, source_target_pairs={{0,4},{4,0},{8,12},{12,8},{1,5},{5,1},{9,13},{13,9},{2,6},{6,2},{1... | collective-permute-start | bytes 2359304 | tf_op jit(solution)/shard_map/ppermute | solution.py:124
  118.2 26.5 %collective-permute-start.1 = (bf16[256,768]{1,0:T(8,128)(2,1)S(1)}, bf16[256,768]{1,0:T(8,128)(2,1)S(1)}, u32[]{:S(2)}, u32[]{:S(2)}) collective-permute-start(bf16[256,768]{1,0:T(8,128)(2,1)S(1)} %constant_dynamic-slice_fusion.4), channel_id=1, source_target_pairs={{0,8},{4,12},{8,0},{12,4},{1,9},{5,13},{9,1},{13,5},{2,10},{6,14},... | collective-permute-start | bytes 1179656 | tf_op jit(solution)/shard_map/ppermute | solution.py:124
  120.8 43.1 %collective-permute-start = (bf16[256,768]{1,0:T(8,128)(2,1)S(1)}, bf16[256,768]{1,0:T(8,128)(2,1)S(1)}, u32[]{:S(2)}, u32[]{:S(2)}) collective-permute-start(bf16[256,768]{1,0:T(8,128)(2,1)S(1)} %constant_dynamic-slice_fusion.4), channel_id=1, source_target_pairs={{0,4},{4,0},{8,12},{12,8},{1,5},{5,1},{9,13},{13,9},{2,6},{6,2},{1... | collective-permute-start | bytes 1179656 | tf_op jit(solution)/shard_map/ppermute | solution.py:124
  144.7 17.7 %copy-start.19 = (bf16[256,768]{1,0:T(8,128)(2,1)}, bf16[256,768]{1,0:T(8,128)(2,1)S(1)}, u32[]{:S(2)}) copy-start(bf16[256,768]{1,0:T(8,128)(2,1)S(1)} %collective-permute-done.1.rest_1_) | copy-start | bytes 1179652
  144.7 35.6 %collective-permute-start.2 = (bf16[256,768]{1,0:T(8,128)(2,1)S(1)}, bf16[256,768]{1,0:T(8,128)(2,1)S(1)}, u32[]{:S(2)}, u32[]{:S(2)}) collective-permute-start(bf16[256,768]{1,0:T(8,128)(2,1)S(1)} %collective-permute-done.1.rest_1_), channel_id=1, source_target_pairs={{0,4},{4,0},{8,12},{12,8},{1,5},{5,1},{9,13},{13,9},{2,6},{6,2},{1... | collective-permute-start | bytes 1179656 | tf_op jit(solution)/shard_map/ppermute | solution.py:124
  153.4 83.0 %collective-permute-start.27 = (bf16[512,768]{1,0:T(8,128)(2,1)}, bf16[512,768]{1,0:T(8,128)(2,1)S(1)}, u32[]{:S(2)}, u32[]{:S(2)}) collective-permute-start(bf16[512,768]{1,0:T(8,128)(2,1)} %weight_grad.5), channel_id=1, source_target_pairs={{0,4},{4,0},{8,12},{12,8},{1,5},{5,1},{9,13},{13,9},{2,6},{6,2},{1... | collective-permute-start | bytes 2359304 | tf_op jit(solution)/shard_map/ppermute | solution.py:124
  160.4 76.0 %collective-permute-start.29 = (bf16[512,768]{1,0:T(8,128)(2,1)S(1)}, bf16[512,768]{1,0:T(8,128)(2,1)S(1)}, u32[]{:S(2)}, u32[]{:S(2)}) collective-permute-start(bf16[512,768]{1,0:T(8,128)(2,1)S(1)} %add_convert_fusion), channel_id=1, source_target_pairs={{0,8},{4,12},{8,0},{12,4},{1,9},{5,13},{9,1},{13,5},{2,10},{6,14},... | collective-permute-start | bytes 2359304 | tf_op jit(solution)/shard_map/ppermute | solution.py:124
  162.4 19.5 %collective-permute-start.4 = (bf16[256,768]{1,0:T(8,128)(2,1)S(1)}, bf16[256,768]{1,0:T(8,128)(2,1)S(1)}, u32[]{:S(2)}, u32[]{:S(2)}) collective-permute-start(bf16[256,768]{1,0:T(8,128)(2,1)S(1)} %collective-permute-done.1.rest_1_), channel_id=1, source_target_pairs={{0,16},{16,0},{1,17},{17,1},{2,18},{18,2},{3,19},{19,3},{4,20},{20... | collective-permute-start | bytes 1179656 | tf_op jit(solution)/shard_map/ppermute | solution.py:128
  163.9 24.8 %copy-start.20 = (bf16[256,768]{1,0:T(8,128)(2,1)}, bf16[256,768]{1,0:T(8,128)(2,1)S(1)}, u32[]{:S(2)}) copy-start(bf16[256,768]{1,0:T(8,128)(2,1)S(1)} %collective-permute-done.rest_0_) | copy-start | bytes 1179652
  163.9 18.9 %collective-permute-start.3 = (bf16[256,768]{1,0:T(8,128)(2,1)S(1)}, bf16[256,768]{1,0:T(8,128)(2,1)S(1)}, u32[]{:S(2)}, u32[]{:S(2)}) collective-permute-start(bf16[256,768]{1,0:T(8,128)(2,1)S(1)} %collective-permute-done.rest_0_), channel_id=1, source_target_pairs={{0,16},{16,0},{1,17},{17,1},{2,18},{18,2},{3,19},{19,3},{4,20},{20... | collective-permute-start | bytes 1179656 | tf_op jit(solution)/shard_map/ppermute | solution.py:128
  180.3 8.4 %collective-permute-start.5 = (bf16[256,768]{1,0:T(8,128)(2,1)S(1)}, bf16[256,768]{1,0:T(8,128)(2,1)S(1)}, u32[]{:S(2)}, u32[]{:S(2)}) collective-permute-start(bf16[256,768]{1,0:T(8,128)(2,1)S(1)} %collective-permute-done.2.rest_2_), channel_id=1, source_target_pairs={{0,16},{16,0},{1,17},{17,1},{2,18},{18,2},{3,19},{19,3},{4,20},{20... | collective-permute-start | bytes 1179656 | tf_op jit(solution)/shard_map/ppermute | solution.py:128
  200.1 10.4 %collective-permute-start.21 = (bf16[2,4,32,512]{3,2,1,0:T(8,128)(2,1)}, bf16[2,4,32,512]{3,2,1,0:T(8,128)(2,1)S(1)}, u32[]{:S(2)}, u32[]{:S(2)}) collective-permute-start(bf16[2,4,32,512]{3,2,1,0:T(8,128)(2,1)} %get-tuple-element.21), channel_id=1, source_target_pairs={{0,4},{4,0},{8,12},{12,8},{1,5},{5,1},{9,13},{13,9},{2,6},{6,2},{1... | collective-permute-start | bytes 786440 | tf_op jit(solution)/shard_map/ppermute | solution.py:124
  200.7 23.2 %collective-permute-start.22 = (bf16[2,4,32,512]{3,2,1,0:T(8,128)(2,1)}, bf16[2,4,32,512]{3,2,1,0:T(8,128)(2,1)S(1)}, u32[]{:S(2)}, u32[]{:S(2)}) collective-permute-start(bf16[2,4,32,512]{3,2,1,0:T(8,128)(2,1)} %get-tuple-element.22), channel_id=1, source_target_pairs={{0,8},{4,12},{8,0},{12,4},{1,9},{5,13},{9,1},{13,5},{2,10},{6,14},... | collective-permute-start | bytes 786440 | tf_op jit(solution)/shard_map/ppermute | solution.py:124
  205.2 18.7 %collective-permute-start.23 = (bf16[2,4,32,512]{3,2,1,0:T(8,128)(2,1)}, bf16[2,4,32,512]{3,2,1,0:T(8,128)(2,1)S(1)}, u32[]{:S(2)}, u32[]{:S(2)}) collective-permute-start(bf16[2,4,32,512]{3,2,1,0:T(8,128)(2,1)} %get-tuple-element.23), channel_id=1, source_target_pairs={{0,12},{4,8},{8,4},{12,0},{1,13},{5,9},{9,5},{13,1},{2,14},{6,10},... | collective-permute-start | bytes 786440 | tf_op jit(solution)/shard_map/ppermute | solution.py:124
  210.6 13.3 %copy-start.28 = (bf16[2,4,32,512]{3,2,1,0:T(8,128)(2,1)}, bf16[2,4,32,512]{3,2,1,0:T(8,128)(2,1)S(1)}, u32[]{:S(2)}) copy-start(bf16[2,4,32,512]{3,2,1,0:T(8,128)(2,1)S(1)} %collective-permute-done.21.rest_1_) | copy-start | bytes 786436
  (13 other events, 46.1 us)

commit v2 on v0

--- a/solution.py
+++ b/solution.py
@@ -1,11 +1,15 @@
+import functools
 import math
 
 import jax
 import jax.numpy as jnp
 from jax import lax
+from jax.experimental import pallas as pl
+from jax.experimental.pallas import tpu as pltpu
 from jax.sharding import PartitionSpec as P
 
 HD = 128
+SCALE = 1.0 / math.sqrt(HD)
 
 
 def normalize(scores):
@@ -115,6 +119,303 @@
     )
 
 
+def xor_send(value, axis, distance):
+    count = lax.axis_size(axis)
+    return lax.ppermute(value, axis, [(i, i ^ distance) for i in range(count)])
+
+
+def trade(value):
+    return lax.all_to_all(value, "seq", split_axis=0, concat_axis=0, tiled=True)
+
+
+def swap_parts(value):
+    return lax.ppermute(value, "parts", [(0, 1), (1, 0)])
+
+
+def after(value, other):
+    return lax.optimization_barrier((value, other))[0]
+
+
+def nt_dot(a, b):
+    return lax.dot_general(a, b, (((1,), (1,)), ((), ())), preferred_element_type=jnp.float32)
+
+
+def tn_dot(a, b):
+    return lax.dot_general(a, b, (((0,), (0,)), ((), ())), preferred_element_type=jnp.float32)
+
+
+def nn_dot(a, b):
+    return lax.dot_general(a, b, (((1,), (0,)), ((), ())), preferred_element_type=jnp.float32)
+
+
+def softmax_rows(scores, scale, axis):
+    raised = jnp.exp((scores - jnp.max(scores, axis=axis, keepdims=True)) * scale)
+    return raised * (1.0 / jnp.sum(raised, axis=axis, keepdims=True))
+
+
+def params():
+    return pltpu.CompilerParams(vmem_limit_bytes=56 * 1024 * 1024)
+
+
+def space_forward_kernel(q, k, v, out, probs):
+    low = softmax_rows(nt_dot(k[0], q[0]), SCALE, 0).astype(jnp.bfloat16)
+    probs[0] = low
+    seq_count, _, band_count, time_len, _ = out.shape
+    mixed = tn_dot(v[0], low).T.astype(jnp.bfloat16).reshape(band_count, seq_count, time_len, HD)
+    for step in range(seq_count):
+        out[step, 0] = mixed[:, step]
+
+
+def space_forward(q, k, v, seq_count, band_count, time_len):
+    frames, patches, columns = q.shape
+    heads = columns // HD
+    wide = pl.BlockSpec((1, patches, HD), lambda f, h: (f, 0, h))
+    return pl.pallas_call(
+        space_forward_kernel,
+        grid=(frames, heads),
+        in_specs=[wide, wide, wide],
+        out_specs=[
+            pl.BlockSpec((seq_count, 1, band_count, time_len, HD), lambda f, h: (0, f, 0, 0, h)),
+            pl.BlockSpec((1, patches, patches), lambda f, h: (f * heads + h, 0, 0)),
+        ],
+        out_shape=[
+            jax.ShapeDtypeStruct((seq_count, frames, band_count, time_len, columns), jnp.bfloat16),
+            jax.ShapeDtypeStruct((frames * heads, patches, patches), jnp.bfloat16),
+        ],
+        compiler_params=params(),
+        name="space_forward",
+    )(q, k, v)
+
+
+def time_probs_kernel(ids, q, k, probs_t, bias):
+    frames, _, time_len, _ = q.shape
+    rows = frames * time_len
+
+    @pl.when((pl.program_id(0) == 0) & (pl.program_id(1) == 0))
+    def _():
+        place = [lax.broadcasted_iota(jnp.int32, (rows, rows), axis) % time_len for axis in (0, 1)]
+        bias[...] = jnp.where(place[0] == place[1], 0.0, -1e30).astype(jnp.float32)
+
+    scores = nt_dot(k[...].reshape(rows, HD), q[...].reshape(rows, HD)) + bias[...]
+    probs_t[0, 0] = softmax_rows(scores, SCALE, 0).astype(jnp.bfloat16)
+
+
+def time_probs(ids, q, k):
+    frames, bands, time_len, columns = q.shape
+    heads = columns // HD
+    rows = frames * time_len
+    spec = pl.BlockSpec((frames, 1, time_len, HD), lambda r, h, ids: (0, ids[1] ^ r, 0, h))
+    return pl.pallas_call(
+        time_probs_kernel,
+        grid_spec=pltpu.PrefetchScalarGridSpec(
+            num_scalar_prefetch=1,
+            grid=(bands, heads),
+            in_specs=[spec, spec],
+            out_specs=pl.BlockSpec((1, 1, rows, rows), lambda r, h, ids: (r, h, 0, 0)),
+            scratch_shapes=[pltpu.VMEM((rows, rows), jnp.float32)],
+        ),
+        out_shape=jax.ShapeDtypeStruct((bands, heads, rows, rows), jnp.bfloat16),
+        compiler_params=params(),
+        name="time_probs",
+    )(ids, q, k)
+
+
+def time_out_kernel(ids, probs_t, values, out):
+    rows = probs_t.shape[2]
+    for head in range(probs_t.shape[1]):
+        lanes = slice(head * HD, (head + 1) * HD)
+        own = values[:, :, 0, :, lanes].reshape(rows, HD)
+        out[lanes, :] = tn_dot(own, probs_t[0, head]).astype(jnp.bfloat16)
+
+
+def time_out(ids, probs_t, values):
+    bands, heads, rows, _ = probs_t.shape
+    seq_count, local, _, time_len, columns = values.shape
+    return pl.pallas_call(
+        time_out_kernel,
+        grid_spec=pltpu.PrefetchScalarGridSpec(
+            num_scalar_prefetch=1,
+            grid=(bands,),
+            in_specs=[
+                pl.BlockSpec((1, heads, rows, rows), lambda r, ids: (r, 0, 0, 0)),
+                pl.BlockSpec((seq_count, local, 1, time_len, columns), lambda r, ids: (0, 0, ids[1] ^ r, 0, 0)),
+            ],
+            out_specs=pl.BlockSpec((columns, rows), lambda r, ids: (0, r)),
+        ),
+        out_shape=jax.ShapeDtypeStruct((columns, bands * rows), jnp.bfloat16),
+        compiler_params=params(),
+        name="time_out",
+    )(ids, probs_t, values)
+
+
+def tokens_of(refs):
+    sides = [jnp.concatenate([ref[...].reshape(-1, ref.shape[-1]) for ref in side], axis=0) for side in refs]
+    return jnp.concatenate(sides, axis=1)
+
+
+def weight_grad_kernel(ids, left, *rest):
+    cots, out = rest[:-1], rest[-1]
+    half = len(cots) // 2
+    out[...] = nn_dot(left[...], tokens_of((cots[:half], cots[half:]))).astype(out.dtype)
+
+
+def weight_grad(ids, left, cots, step, width, dtype):
+    columns, tokens = left.shape
+    cot_spec = pl.BlockSpec((*cots[0].shape[:2], width // 2), lambda i, ids: (0, 0, ids[0] ^ step))
+    return pl.pallas_call(
+        weight_grad_kernel,
+        grid_spec=pltpu.PrefetchScalarGridSpec(
+            num_scalar_prefetch=1,
+            grid=(1,),
+            in_specs=[pl.BlockSpec((columns, tokens), lambda i, ids: (0, 0))] + [cot_spec] * len(cots),
+            out_specs=pl.BlockSpec((columns, width), lambda i, ids: (0, 0)),
+        ),
+        out_shape=jax.ShapeDtypeStruct((columns, width), dtype),
+        compiler_params=params(),
+        name="weight_grad",
+    )(ids, left, *cots)
+
+
+def space_grad_kernel(ids, probs_t, own, near, third, other_near, other_third, *rest, seq_count, band_count):
+    cots, out, grad = rest[:-2], rest[-2], rest[-1]
+    sub, part = ids[1], ids[2]
+    rows = own.shape[0]
+    half = rows // 2
+    tokens = tokens_of((cots[:band_count], cots[band_count:]))
+
+    def own_half(which):
+        return own[pl.ds(pl.multiple_of(which * half, 128), half)]
+
+    halves = (
+        lambda: (own_half(part), own_half(1 - part)),
+        lambda: (near[:half], other_near[:half]),
+        lambda: (near[half:], other_near[half:]),
+        lambda: (third[...], other_third[...]),
+    )
+    for step in range(seq_count):
+
+        @pl.when(pl.program_id(0) == step)
+        def _():
+            grown = nt_dot(tokens, jnp.concatenate(halves[step](), axis=0))
+            grad[...] = grown if step == 0 else grad[...] + grown
+
+    frames, time_len, _ = cots[0].shape
+    block, heads = grad.shape[0] // band_count, half // HD
+
+    @pl.when(pl.program_id(0) == seq_count - 1)
+    def _():
+        for r in range(band_count):
+            for place in range(2 * heads):
+                head = (part ^ (place // heads)) * heads + place % heads
+                lanes = pl.ds(pl.multiple_of(head * HD, HD), HD)
+                low = grad[r * block : (r + 1) * block, place * HD : (place + 1) * HD].astype(jnp.bfloat16)
+                back = nn_dot(probs_t[r, head], low).astype(jnp.bfloat16)
+                out[:, :, sub ^ r, :, lanes] = back.reshape(seq_count, frames // seq_count, time_len, HD)
+
+
+def space_grad(ids, probs_t, weights, cots, seq_count, band_count):
+    frames, time_len, depth = cots[0].shape
+    rows, width = weights[0].shape
+    full = lambda array: pl.BlockSpec(array.shape, lambda i, ids: (0,) * array.ndim)
+    cot_spec = pl.BlockSpec((frames, time_len, width // 2), lambda i, ids: (0, 0, ids[0] ^ i))
+    out_shape = (seq_count, frames // seq_count, band_count, time_len, rows)
+    return pl.pallas_call(
+        functools.partial(space_grad_kernel, seq_count=seq_count, band_count=band_count),
+        grid_spec=pltpu.PrefetchScalarGridSpec(
+            num_scalar_prefetch=1,
+            grid=(seq_count,),
+            in_specs=[full(probs_t)] + [full(array) for array in weights] + [cot_spec] * len(cots),
+            out_specs=pl.BlockSpec(out_shape, lambda i, ids: (0, 0, 0, 0, 0)),
+            scratch_shapes=[pltpu.VMEM((frames * time_len * band_count, rows), jnp.float32)],
+        ),
+        out_shape=jax.ShapeDtypeStruct(out_shape, jnp.bfloat16),
+        compiler_params=params(),
+        name="space_grad",
+    )(ids, probs_t, *weights, *cots)
+
+
+def space_backward_kernel(q, k, v, probs, piece, dq, dk, dv, spare):
+    for step in range(piece.shape[0]):
+        spare[:, step] = piece[step, 0]
+    upstream = spare[...].reshape(q.shape[1:])
+    low = probs[0]
+    dv[0] = nn_dot(low, upstream).astype(jnp.bfloat16)
+    chance = nt_dot(v[0], upstream)
+    wide = low.astype(jnp.float32)
+    centre = jnp.sum(wide * chance, axis=0, keepdims=True)
+    score = (wide * (chance - centre)).astype(jnp.bfloat16)
+    dk[0] = (nn_dot(score, q[0]) * SCALE).astype(jnp.bfloat16)
+    dq[0] = (tn_dot(k[0], score) * SCALE).T.astype(jnp.bfloat16)
+
+
+def space_backward(q, k, v, probs, back):
+    frames, patches, columns = q.shape
+    heads = columns // HD
+    seq_count, _, band_count, time_len, _ = back.shape
+    wide = pl.BlockSpec((1, patches, HD), lambda f, h: (f, 0, h))
+    piece = pl.BlockSpec((seq_count, 1, band_count, time_len, HD), lambda f, h: (0, f, 0, 0, h))
+    square = pl.BlockSpec((1, patches, patches), lambda f, h: (f * heads + h, 0, 0))
+    return pl.pallas_call(
+        space_backward_kernel,
+        grid=(frames, heads),
+        in_specs=[wide, wide, wide, square, piece],
+        out_specs=[wide, wide, wide],
+        out_shape=[jax.ShapeDtypeStruct(q.shape, jnp.bfloat16)] * 3,
+        scratch_shapes=[pltpu.VMEM((band_count, seq_count, time_len, HD), jnp.bfloat16)],
+        compiler_params=params(),
+        name="space_backward",
+    )(q, k, v, probs, back)
+
+
+def on_small_slice(q_space, k_space, v_space, q_time, k_time, out_weight, cotangent):
+    seq_count, band_count = lax.axis_size("seq"), lax.axis_size("sub")
+    time_len = q_space.shape[1] // band_count // seq_count
+    me, sub, part = lax.axis_index("seq"), lax.axis_index("sub"), lax.axis_index("parts")
+    ids = jnp.stack([me, sub, part]).astype(jnp.int32)
+    rows, width = out_weight.shape
+
+    local, depth = cotangent.shape[0], cotangent.shape[2]
+    split = []
+    for side in range(2):
+        starts = [shard * width + side * (width // 2) for shard in range(seq_count)]
+        picked = jnp.concatenate([cotangent[:, :, start : start + width // 2] for start in starts], axis=2)
+        picked = picked.reshape(local, seq_count, time_len, depth // 2).transpose(1, 0, 2, 3)
+        split.append(picked.reshape(seq_count * local, time_len, depth // 2))
+    here = [trade(split[side]) for side in range(2)]
+    q_space = after(q_space, split)
+    mixed, probs = space_forward(q_space, k_space, v_space, seq_count, band_count, time_len)
+    moved = trade(mixed)
+    q_time = after(q_time, mixed)
+    chances = time_probs(ids, q_time, k_time)
+    here[1] = after(here[1], chances)
+    cots = []
+    for side in here:
+        across = xor_send(side, "sub", 2)
+        cots += [side, xor_send(side, "sub", 1), across, xor_send(across, "sub", 1)]
+
+    half = lax.dynamic_slice_in_dim(out_weight, part * (rows // 2), rows // 2, 0)
+    half = after(half, here[1])
+    second = xor_send(half, "seq", 2)
+    first = xor_send(half, "seq", 1)
+    third = xor_send(second, "seq", 1)
+    near_rows = jnp.concatenate([first, second], axis=0)
+    weights = [out_weight, near_rows, third, swap_parts(near_rows), swap_parts(third)]
+    returned = trade(space_grad(ids, chances, weights, cots, seq_count, band_count))
+
+    turned = time_out(ids, chances, moved)
+    third_sum = weight_grad(ids, turned, cots, 3, width, jnp.bfloat16)
+    second_sum = weight_grad(ids, turned, cots, 2, width, jnp.float32)
+    first_sum = weight_grad(ids, turned, cots, 1, width, jnp.bfloat16)
+    own_sum = weight_grad(ids, turned, cots, 0, width, jnp.float32)
+    paired = (second_sum + xor_send(third_sum, "seq", 1).astype(jnp.float32)).astype(jnp.bfloat16)
+    near = xor_send(first_sum, "seq", 1).astype(jnp.float32)
+    far = xor_send(paired, "seq", 2).astype(jnp.float32)
+    d_weight = own_sum + near + far
+
+    dq, dk, dv = space_backward(q_space, k_space, v_space, probs, returned)
+    return dq, dk, dv, d_weight
+
+
 def solution(mesh):
     in_specs = (
         P(("parts", "seq"), None, "sub"),
@@ -131,6 +432,7 @@
         P(("parts", "seq"), None, "sub"),
         P(("parts", "sub"), "seq"),
     )
+    small = (mesh.shape["parts"], mesh.shape["seq"], mesh.shape["sub"]) == (2, 4, 4)
     return jax.shard_map(
-        on_device, mesh=mesh, in_specs=in_specs, out_specs=out_specs, check_vma=False
-    )
+        on_small_slice if small else on_device, mesh=mesh, in_specs=in_specs, out_specs=out_specs, check_vma=False
+    )

time: 301 us -> 212 us (0.70)
  blocking collectives: 146 us -> 0 us
  matrix products: 73.3 us -> 0 us
  Pallas kernels: 0 us -> 66.4 us
  waiting for transfers between devices: 37 us -> 96.9 us
  starting transfers between devices: 6.55 us -> 33.1 us
  between operations: 14 us -> 0.75 us
  local copies, waits for them, and re-layouts: 21.2 us -> 9.08 us
    all_to_all x3 -> x0, blocking collectives: 146 us -> none  [the longest x1 57.4 us: on_device(): lax.all_to_all(rounded, 'seq', split_axis=2, concat_axis=0, tiled=True)]
    ppermute x0 -> x14, waiting for transfers between devices: none -> 70.4 us  [the longest x12 61.9 us: xor_send(): return lax.ppermute(value, axis, [(i, i ^ distance) for i in range(count)])]
    pallas_call x0 -> x9, Pallas kernels: none -> 66.4 us  [the longest x4 17.8 us: weight_grad(): pl.pallas_call(weight_grad_kernel, grid_spec=pltpu.PrefetchScalarGridSpec...]
    dot_general x9 -> x0, matrix products: 63.5 us -> none  [the longest x1 15.2 us: on_device(): jnp.einsum('fhqk,fkhd->fqhd', score_grad, space_keys, preferred_element_t...]
    all_gather x2 -> x0, waiting for transfers between devices: 18.4 us -> none  [the longest x1 18.3 us: on_device(): weight_rows = lax.all_gather(out_weight, 'seq', axis=1, tiled=True)]
    ppermute x0 -> x14, starting transfers between devices: none -> 14.8 us  [the longest x12 11.7 us: xor_send(): return lax.ppermute(value, axis, [(i, i ^ distance) for i in range(count)])]
    all_to_all x1 -> x4, starting transfers between devices: 6.48 us -> 18.3 us  [trade(): return lax.all_to_all(value, 'seq', split_axis=0, concat_axis=0, tiled=True)]
    reshape x13 -> x2, local copies, waits for them, and re-layouts: 12.3 us -> 1.89 us  [on_small_slice(): picked.reshape(local, seq_count, time_len, depth // 2).transpose(1, 0, 2, 3)]
  transfers between devices with their start and end apart: 4 -> 18, of which waited for: 2 -> 7; matrix products, arithmetic and copies ran while one was open for 31% -> 3% of each run, Pallas kernels for 0% -> 32%
where the time goes in v2:
time: 212 us; the launch traced here: 210 us
  waiting for transfers between devices  96.9 us (46%)
  Pallas kernels  66.4 us (31%)
  starting transfers between devices  33.1 us (16%)
  local copies, waits for them, and re-layouts  9.08 us (4%)
  other arithmetic  3.72 us (2%)
    ppermute x12, waiting for transfers between devices, xor_send(): return lax.ppermute(value, axis, [(i, i ^ distance) for i in range(count)])  61.9 us
    all_to_all x4, waiting for transfers between devices, trade(): return lax.all_to_all(value, 'seq', split_axis=0, concat_axis=0, tiled=True)  26.5 us
    all_to_all x4, starting transfers between devices, trade(): return lax.all_to_all(value, 'seq', split_axis=0, concat_axis=0, tiled=True)  18.3 us
    pallas_call x4, Pallas kernels, weight_grad(): pl.pallas_call(weight_grad_kernel, grid_spec=pltpu.PrefetchScalarGridSpec...  17.8 us
    pallas_call x1, Pallas kernels, time_probs(): pl.pallas_call(time_probs_kernel, grid_spec=pltpu.PrefetchScalarGridSpec(...  11.9 us
    ppermute x12, starting transfers between devices, xor_send(): return lax.ppermute(value, axis, [(i, i ^ distance) for i in range(count)])  11.7 us
    pallas_call x1, Pallas kernels, space_backward(): pl.pallas_call(space_backward_kernel, grid=(frames, heads), in_specs=[wid...  11.1 us
    pallas_call x1, Pallas kernels, space_grad(): pl.pallas_call(functools.partial(space_grad_kernel, seq_count=seq_count,...  10.5 us
  transfers between devices with their start and end apart: 18, of which 7 were waited for; matrix products, arithmetic and copies ran while one was open for 3% of the time, Pallas kernels for 32%

profile of v2, /device:TPU:0, one launch (start us, length us, event | category | flops | bytes accessed | tf_op | source)
XLA Modules:
  0.0 209.9 jit_solution(13875181585349915272)
XLA Ops:
  0.6 1.7 fusion
  2.3 0.1 pad_maximum_fusion
  2.5 0.9 copy.12
  3.4 6.3 %all-to-all-start = ((bf16[8,32,1536]{2,1,0:T(8,128)(2,1)}), bf16[8,32,1536]{2,1,0:T(8,128)(2,1)S(1)}, u32[]{:S(2)}, u32[]{:S(2)}) async-start(bf16[8,32,1536]{2,1,0:T(8,128)(2,1)} %bitcast.5), calls=%async_computation | async-start | bytes 1572864 | tf_op jit(solution)/shard_map/all_to_all | solution.py:128
  9.7 1.0 copy.11
  10.7 19.2 %all-to-all-done.rest_4_ = bf16[8,32,1536]{2,1,0:T(8,128)(2,1)S(1)} async-done(((bf16[8,32,1536]{2,1,0:T(8,128)(2,1)}), bf16[8,32,1536]{2,1,0:T(8,128)(2,1)S(1)}, u32[]{:S(2)}, u32[]{:S(2)}) %all-to-all-start) | async-done | bytes 786464 | tf_op jit(solution)/shard_map/all_to_all | solution.py:128
  29.8 3.5 %all-to-all-start.1 = ((bf16[8,32,1536]{2,1,0:T(8,128)(2,1)}), bf16[8,32,1536]{2,1,0:T(8,128)(2,1)S(1)}, u32[]{:S(2)}, u32[]{:S(2)}) async-start(bf16[8,32,1536]{2,1,0:T(8,128)(2,1)} %bitcast.2), calls=%async_computation.1 | async-start | bytes 1572864 | tf_op jit(solution)/shard_map/all_to_all | solution.py:128
  33.3 10.2 %space_forward.1 = (bf16[4,2,4,32,512]{4,3,2,1,0:T(8,128)(2,1)}, bf16[8,512,512]{2,1,0:T(8,128)(2,1)}) custom-call(bf16[2,512,512]{2,1,0:T(8,128)(2,1)} %q.2, bf16[2,512,512]{2,1,0:T(8,128)(2,1)} %k.5, bf16[2,512,512]{2,1,0:T(8,128)(2,1)} %v.3), custom_call_target="tpu_custom_call" | custom-call | tf_op jit(solution)/shard_map/space_forward/pallas_call | solution.py:173
  43.5 0.7 pad_add_fusion.ids
  44.2 11.9 %time_probs.1.probs_t = bf16[4,4,256,256]{3,2,1,0:T(8,128)(2,1)} custom-call(s32[3]{0:T(128)} %pad_add_fusion.ids, bf16[8,4,32,512]{3,2,1,0:T(8,128)(2,1)} %q.1, bf16[8,4,32,512]{3,2,1,0:T(8,128)(2,1)} %k.4), custom_call_target="tpu_custom_call" | custom-call | tf_op jit(solution)/shard_map/time_probs/pallas_call | solution.py:208
  56.1 0.0 all-to-all-done.1.rest_0_
  56.1 5.0 %all-to-all-start.3 = ((bf16[4,2,4,32,512]{4,3,2,1,0:T(8,128)(2,1)}), bf16[4,2,4,32,512]{4,3,2,1,0:T(8,128)(2,1)}, u32[]{:S(2)}, u32[]{:S(2)}) async-start(bf16[4,2,4,32,512]{4,3,2,1,0:T(8,128)(2,1)} %get-tuple-element.15), calls=%async_computation.3 | async-start | bytes 2097152 | tf_op jit(solution)/shard_map/all_to_all | solution.py:128
  61.1 1.5 collective-permute-start.6
  62.6 0.5 collective-permute-start.9
  63.1 0.0 collective-permute-start.5
  63.1 1.0 constant_dynamic-slice_fusion
  64.1 3.0 %collective-permute-start.1 = (bf16[256,768]{1,0:T(8,128)(2,1)S(1)}, bf16[256,768]{1,0:T(8,128)(2,1)S(1)}, u32[]{:S(2)}, u32[]{:S(2)}) collective-permute-start(bf16[256,768]{1,0:T(8,128)(2,1)S(1)} %constant_dynamic-slice_fusion), channel_id=1, source_target_pairs={{0,8},{4,12},{8,0},{12,4},{1,9},{5,13},{9,1},{13,5},{2,10},{6,14},... | collective-permute-start | bytes 1179656 | tf_op jit(solution)/shard_map/ppermute | solution.py:124
  67.1 1.5 collective-permute-start
  68.6 34.0 %collective-permute-done.1 = bf16[256,768]{1,0:T(8,128)(2,1)S(1)} collective-permute-done((bf16[256,768]{1,0:T(8,128)(2,1)S(1)}, bf16[256,768]{1,0:T(8,128)(2,1)S(1)}, u32[]{:S(2)}, u32[]{:S(2)}) %collective-permute-start.1) | collective-permute-done | bytes 393248 | tf_op jit(solution)/shard_map/ppermute | solution.py:124
  102.6 0.0 collective-permute-start.8
  102.6 0.0 collective-permute-done.6.rest_2_
  102.6 0.5 collective-permute-start.7
  103.1 0.1 collective-permute-start.10
  103.2 0.9 constant_dynamic-update-slice_fusion.1
  104.1 0.8 constant_dynamic-update-slice_fusion.near
  104.9 0.9 copy-done.4
  105.8 1.5 collective-permute-start.3
  107.3 7.4 %collective-permute-done.2.third = bf16[256,768]{1,0:T(8,128)(2,1)S(1)} collective-permute-done((bf16[256,768]{1,0:T(8,128)(2,1)S(1)}, bf16[256,768]{1,0:T(8,128)(2,1)S(1)}, u32[]{:S(2)}, u32[]{:S(2)}) %collective-permute-start.2) | collective-permute-done | bytes 393248 | tf_op jit(solution)/shard_map/ppermute | solution.py:124
  114.7 1.5 collective-permute-start.4
  116.2 4.9 %time_out.1.left = bf16[512,1024]{1,0:T(8,128)(2,1)} custom-call(s32[3]{0:T(128)} %pad_add_fusion.ids, bf16[4,4,256,256]{3,2,1,0:T(8,128)(2,1)} %time_probs.1.probs_t, bf16[4,2,4,32,512]{4,3,2,1,0:T(8,128)(2,1)} %all-to-all-done.3.values), custom_call_target="tpu_custom_call" | custom-call | tf_op jit(solution)/shard_map/time_out/pallas_call | solution.py:234
  121.1 4.3 %weight_grad.7 = bf16[512,768]{1,0:T(8,128)(2,1)} custom-call(s32[3]{0:T(128)} %pad_add_fusion.ids, bf16[512,1024]{1,0:T(8,128)(2,1)} %time_out.1.left, bf16[8,32,1536]{2,1,0:T(8,128)(2,1)} %copy-done.1, bf16[8,32,1536]{2,1,0:T(8,128)(2,1)} %copy-done.4, bf16[8,32,1536]{2,1,0:T(8,128)(2,1)} %copy-done.2, ...), custom_call_target="tpu_custom_call" | custom-call | tf_op jit(solution)/shard_map/weight_grad/pallas_call | solution.py:265
  125.5 0.3 collective-permute-start.12
  125.7 8.6 %collective-permute-done.4.other_third = bf16[256,768]{1,0:T(8,128)(2,1)} collective-permute-done((bf16[256,768]{1,0:T(8,128)(2,1)S(1)}, bf16[256,768]{1,0:T(8,128)(2,1)}, u32[]{:S(2)}, u32[]{:S(2)}) %collective-permute-start.4) | collective-permute-done | bytes 393248 | tf_op jit(solution)/shard_map/ppermute | solution.py:132
  134.3 0.9 copy-done.7
  135.2 10.5 %space_grad.1 = bf16[4,2,4,32,512]{4,3,2,1,0:T(8,128)(2,1)} custom-call(s32[3]{0:T(128)} %pad_add_fusion.ids, bf16[4,4,256,256]{3,2,1,0:T(8,128)(2,1)} %time_probs.1.probs_t, bf16[512,768]{1,0:T(8,128)(2,1)} %own.1, bf16[512,768]{1,0:T(8,128)(2,1)} %constant_dynamic-update-slice_fusion.near, bf16[256,768]{1,0:T(8,128)(2,1)} %copy-done.8, ...), custom_call_target="tpu_custom_call" | custom-call | tf_op jit(solution)/shard_map/space_grad/pallas_call | solution.py:322
  145.7 3.5 %all-to-all-start.2 = ((bf16[4,2,4,32,512]{4,3,2,1,0:T(8,128)(2,1)}), bf16[4,2,4,32,512]{4,3,2,1,0:T(8,128)(2,1)S(1)}, u32[]{:S(2)}, u32[]{:S(2)}) async-start(bf16[4,2,4,32,512]{4,3,2,1,0:T(8,128)(2,1)} %space_grad.1), calls=%async_computation.2 | async-start | bytes 2097152 | tf_op jit(solution)/shard_map/all_to_all | solution.py:128
  149.2 4.3 %weight_grad.5 = bf16[512,768]{1,0:T(8,128)(2,1)} custom-call(s32[3]{0:T(128)} %pad_add_fusion.ids, bf16[512,1024]{1,0:T(8,128)(2,1)} %time_out.1.left, bf16[8,32,1536]{2,1,0:T(8,128)(2,1)} %copy-done.1, bf16[8,32,1536]{2,1,0:T(8,128)(2,1)} %copy-done.4, bf16[8,32,1536]{2,1,0:T(8,128)(2,1)} %copy-done.2, ...), custom_call_target="tpu_custom_call" | custom-call | tf_op jit(solution)/shard_map/weight_grad/pallas_call | solution.py:265
  153.5 2.0 collective-permute-start.11
  155.5 4.6 %weight_grad.6 = f32[512,768]{1,0:T(8,128)} custom-call(s32[3]{0:T(128)} %pad_add_fusion.ids, bf16[512,1024]{1,0:T(8,128)(2,1)} %time_out.1.left, bf16[8,32,1536]{2,1,0:T(8,128)(2,1)} %copy-done.1, bf16[8,32,1536]{2,1,0:T(8,128)(2,1)} %copy-done.4, bf16[8,32,1536]{2,1,0:T(8,128)(2,1)} %copy-done.2, bf16[8,32,1536]{2,1,0:T(8,128)(2,1)} %collective-permute-done.7.rest_3_, ...), custom_call_target="tpu_custom_call" | custom-call | tf_op jit(solution)/shard_map/weight_grad/pallas_call | solution.py:265
  160.1 1.6 add_convert_fusion
  161.7 2.4 %collective-permute-start.13 = (bf16[512,768]{1,0:T(8,128)(2,1)S(1)}, bf16[512,768]{1,0:T(8,128)(2,1)S(1)}, u32[]{:S(2)}, u32[]{:S(2)}) collective-permute-start(bf16[512,768]{1,0:T(8,128)(2,1)S(1)} %add_convert_fusion), channel_id=1, source_target_pairs={{0,8},{4,12},{8,0},{12,4},{1,9},{5,13},{9,1},{13,5},{2,10},{6,14},... | collective-permute-start | bytes 2359304 | tf_op jit(solution)/shard_map/ppermute | solution.py:124
  164.1 4.6 %weight_grad.4 = f32[512,768]{1,0:T(8,128)} custom-call(s32[3]{0:T(128)} %pad_add_fusion.ids, bf16[512,1024]{1,0:T(8,128)(2,1)} %time_out.1.left, bf16[8,32,1536]{2,1,0:T(8,128)(2,1)} %copy-done.1, bf16[8,32,1536]{2,1,0:T(8,128)(2,1)} %copy-done.4, bf16[8,32,1536]{2,1,0:T(8,128)(2,1)} %copy-done.2, bf16[8,32,1536]{2,1,0:T(8,128)(2,1)} %collective-permute-done.7.rest_3_, ...), custom_call_target="tpu_custom_call" | custom-call | tf_op jit(solution)/shard_map/weight_grad/pallas_call | solution.py:265
  168.7 7.3 %all-to-all-done.2.piece = bf16[4,2,4,32,512]{4,3,2,1,0:T(8,128)(2,1)S(1)} async-done(((bf16[4,2,4,32,512]{4,3,2,1,0:T(8,128)(2,1)}), bf16[4,2,4,32,512]{4,3,2,1,0:T(8,128)(2,1)S(1)}, u32[]{:S(2)}, u32[]{:S(2)}) %all-to-all-start.2) | async-done | bytes 1048608 | tf_op jit(solution)/shard_map/all_to_all | solution.py:128
  176.0 1.0 copy-done.6
  177.0 11.1 %space_backward.1 = (bf16[2,512,512]{2,1,0:T(8,128)(2,1)}, bf16[2,512,512]{2,1,0:T(8,128)(2,1)}, bf16[2,512,512]{2,1,0:T(8,128)(2,1)}) custom-call(bf16[2,512,512]{2,1,0:T(8,128)(2,1)} %q.2, bf16[2,512,512]{2,1,0:T(8,128)(2,1)} %k.5, bf16[2,512,512]{2,1,0:T(8,128)(2,1)} %v.3, bf16[8,512,512]{2,1,0:T(8,128)(2,1)} %get-tuple-element.14.probs, ...), custom_call_target="tpu_custom_call" | custom-call | tf_op jit(solution)/shard_map/space_backward/pallas_call | solution.py:358
  188.1 9.3 %collective-permute-done.11 = bf16[512,768]{1,0:T(8,128)(2,1)S(1)} collective-permute-done((bf16[512,768]{1,0:T(8,128)(2,1)}, bf16[512,768]{1,0:T(8,128)(2,1)S(1)}, u32[]{:S(2)}, u32[]{:S(2)}) %collective-permute-start.11) | collective-permute-done | bytes 786464 | tf_op jit(solution)/shard_map/ppermute | solution.py:124
  197.5 11.1 %collective-permute-done.13 = bf16[512,768]{1,0:T(8,128)(2,1)S(1)} collective-permute-done((bf16[512,768]{1,0:T(8,128)(2,1)S(1)}, bf16[512,768]{1,0:T(8,128)(2,1)S(1)}, u32[]{:S(2)}, u32[]{:S(2)}) %collective-permute-start.13) | collective-permute-done | bytes 786464 | tf_op jit(solution)/shard_map/ppermute | solution.py:124
  208.6 1.3 convert_add_fusion
  (25 shorter events, 0.1 us)
Async XLA Ops:
  3.4 26.4 %all-to-all-start = ((bf16[8,32,1536]{2,1,0:T(8,128)(2,1)}), bf16[8,32,1536]{2,1,0:T(8,128)(2,1)S(1)}, u32[]{:S(2)}, u32[]{:S(2)}) async-start(bf16[8,32,1536]{2,1,0:T(8,128)(2,1)} %bitcast.5), calls=%async_computation | async-start | bytes 1572864 | tf_op jit(solution)/shard_map/all_to_all | solution.py:128
  29.8 72.8 %copy-start = (bf16[8,32,1536]{2,1,0:T(8,128)(2,1)}, bf16[8,32,1536]{2,1,0:T(8,128)(2,1)S(1)}, u32[]{:S(2)}) copy-start(bf16[8,32,1536]{2,1,0:T(8,128)(2,1)S(1)} %all-to-all-done.rest_4_) | copy-start | bytes 2359300
  29.8 26.2 %all-to-all-start.1 = ((bf16[8,32,1536]{2,1,0:T(8,128)(2,1)}), bf16[8,32,1536]{2,1,0:T(8,128)(2,1)S(1)}, u32[]{:S(2)}, u32[]{:S(2)}) async-start(bf16[8,32,1536]{2,1,0:T(8,128)(2,1)} %bitcast.2), calls=%async_computation.1 | async-start | bytes 1572864 | tf_op jit(solution)/shard_map/all_to_all | solution.py:128
  56.1 48.1 %copy-start.1 = (bf16[8,32,1536]{2,1,0:T(8,128)(2,1)}, bf16[8,32,1536]{2,1,0:T(8,128)(2,1)S(1)}, u32[]{:S(2)}) copy-start(bf16[8,32,1536]{2,1,0:T(8,128)(2,1)S(1)} %all-to-all-done.1.rest_0_) | copy-start | bytes 2359300
  56.1 60.1 %all-to-all-start.3 = ((bf16[4,2,4,32,512]{4,3,2,1,0:T(8,128)(2,1)}), bf16[4,2,4,32,512]{4,3,2,1,0:T(8,128)(2,1)}, u32[]{:S(2)}, u32[]{:S(2)}) async-start(bf16[4,2,4,32,512]{4,3,2,1,0:T(8,128)(2,1)} %get-tuple-element.15), calls=%async_computation.3 | async-start | bytes 2097152 | tf_op jit(solution)/shard_map/all_to_all | solution.py:128
  61.1 41.5 %collective-permute-start.6 = (bf16[8,32,1536]{2,1,0:T(8,128)(2,1)S(1)}, bf16[8,32,1536]{2,1,0:T(8,128)(2,1)S(1)}, u32[]{:S(2)}, u32[]{:S(2)}) collective-permute-start(bf16[8,32,1536]{2,1,0:T(8,128)(2,1)S(1)} %all-to-all-done.1.rest_0_), channel_id=1, source_target_pairs={{0,2},{1,3},{2,0},{3,1},{4,6},{5,7},{6,4},{7,5},{8,10},{9,11},{10,... | collective-permute-start | bytes 2359304 | tf_op jit(solution)/shard_map/ppermute | solution.py:124
  62.6 40.5 %collective-permute-start.9 = (bf16[8,32,1536]{2,1,0:T(8,128)(2,1)S(1)}, bf16[8,32,1536]{2,1,0:T(8,128)(2,1)S(1)}, u32[]{:S(2)}, u32[]{:S(2)}) collective-permute-start(bf16[8,32,1536]{2,1,0:T(8,128)(2,1)S(1)} %all-to-all-done.rest_4_), channel_id=1, source_target_pairs={{0,2},{1,3},{2,0},{3,1},{4,6},{5,7},{6,4},{7,5},{8,10},{9,11},{10,... | collective-permute-start | bytes 2359304 | tf_op jit(solution)/shard_map/ppermute | solution.py:124
  63.1 41.8 %collective-permute-start.5 = (bf16[8,32,1536]{2,1,0:T(8,128)(2,1)S(1)}, bf16[8,32,1536]{2,1,0:T(8,128)(2,1)S(1)}, u32[]{:S(2)}, u32[]{:S(2)}) collective-permute-start(bf16[8,32,1536]{2,1,0:T(8,128)(2,1)S(1)} %all-to-all-done.1.rest_0_), channel_id=1, source_target_pairs={{0,1},{1,0},{2,3},{3,2},{4,5},{5,4},{6,7},{7,6},{8,9},{9,8},{10,11... | collective-permute-start | bytes 2359304 | tf_op jit(solution)/shard_map/ppermute | solution.py:124
  64.1 38.5 %collective-permute-start.1 = (bf16[256,768]{1,0:T(8,128)(2,1)S(1)}, bf16[256,768]{1,0:T(8,128)(2,1)S(1)}, u32[]{:S(2)}, u32[]{:S(2)}) collective-permute-start(bf16[256,768]{1,0:T(8,128)(2,1)S(1)} %constant_dynamic-slice_fusion), channel_id=1, source_target_pairs={{0,8},{4,12},{8,0},{12,4},{1,9},{5,13},{9,1},{13,5},{2,10},{6,14},... | collective-permute-start | bytes 1179656 | tf_op jit(solution)/shard_map/ppermute | solution.py:124
  67.1 36.1 %collective-permute-start = (bf16[256,768]{1,0:T(8,128)(2,1)S(1)}, bf16[256,768]{1,0:T(8,128)(2,1)S(1)}, u32[]{:S(2)}, u32[]{:S(2)}) collective-permute-start(bf16[256,768]{1,0:T(8,128)(2,1)S(1)} %constant_dynamic-slice_fusion), channel_id=1, source_target_pairs={{0,4},{4,0},{8,12},{12,8},{1,5},{5,1},{9,13},{13,9},{2,6},{6,2},{1... | collective-permute-start | bytes 1179656 | tf_op jit(solution)/shard_map/ppermute | solution.py:124
  102.6 18.5 %collective-permute-start.8 = (bf16[8,32,1536]{2,1,0:T(8,128)(2,1)S(1)}, bf16[8,32,1536]{2,1,0:T(8,128)(2,1)}, u32[]{:S(2)}, u32[]{:S(2)}) collective-permute-start(bf16[8,32,1536]{2,1,0:T(8,128)(2,1)S(1)} %all-to-all-done.rest_4_), channel_id=1, source_target_pairs={{0,1},{1,0},{2,3},{3,2},{4,5},{5,4},{6,7},{7,6},{8,9},{9,8},{10,11... | collective-permute-start | bytes 2359304 | tf_op jit(solution)/shard_map/ppermute | solution.py:124
  102.6 18.5 %copy-start.2 = (bf16[8,32,1536]{2,1,0:T(8,128)(2,1)}, bf16[8,32,1536]{2,1,0:T(8,128)(2,1)S(1)}, u32[]{:S(2)}) copy-start(bf16[8,32,1536]{2,1,0:T(8,128)(2,1)S(1)} %collective-permute-done.6.rest_2_) | copy-start | bytes 2359300
  102.6 18.5 %collective-permute-start.7 = (bf16[8,32,1536]{2,1,0:T(8,128)(2,1)S(1)}, bf16[8,32,1536]{2,1,0:T(8,128)(2,1)}, u32[]{:S(2)}, u32[]{:S(2)}) collective-permute-start(bf16[8,32,1536]{2,1,0:T(8,128)(2,1)S(1)} %collective-permute-done.6.rest_2_), channel_id=1, source_target_pairs={{0,1},{1,0},{2,3},{3,2},{4,5},{5,4},{6,7},{7,6},{8,9},{9,8},{10,11... | collective-permute-start | bytes 2359304 | tf_op jit(solution)/shard_map/ppermute | solution.py:124
  103.1 18.0 %copy-start.3 = (bf16[8,32,1536]{2,1,0:T(8,128)(2,1)}, bf16[8,32,1536]{2,1,0:T(8,128)(2,1)S(1)}, u32[]{:S(2)}) copy-start(bf16[8,32,1536]{2,1,0:T(8,128)(2,1)S(1)} %collective-permute-done.9.rest_6_) | copy-start | bytes 2359300
  103.1 18.0 %collective-permute-start.10 = (bf16[8,32,1536]{2,1,0:T(8,128)(2,1)S(1)}, bf16[8,32,1536]{2,1,0:T(8,128)(2,1)}, u32[]{:S(2)}, u32[]{:S(2)}) collective-permute-start(bf16[8,32,1536]{2,1,0:T(8,128)(2,1)S(1)} %collective-permute-done.9.rest_6_), channel_id=1, source_target_pairs={{0,1},{1,0},{2,3},{3,2},{4,5},{5,4},{6,7},{7,6},{8,9},{9,8},{10,11... | collective-permute-start | bytes 2359304 | tf_op jit(solution)/shard_map/ppermute | solution.py:124
  103.2 11.5 %collective-permute-start.2 = (bf16[256,768]{1,0:T(8,128)(2,1)S(1)}, bf16[256,768]{1,0:T(8,128)(2,1)S(1)}, u32[]{:S(2)}, u32[]{:S(2)}) collective-permute-start(bf16[256,768]{1,0:T(8,128)(2,1)S(1)} %collective-permute-done.1), channel_id=1, source_target_pairs={{0,4},{4,0},{8,12},{12,8},{1,5},{5,1},{9,13},{13,9},{2,6},{6,2},{1... | collective-permute-start | bytes 1179656 | tf_op jit(solution)/shard_map/ppermute | solution.py:124
  104.9 0.9 copy-start.4
  105.8 28.5 %collective-permute-start.3 = (bf16[512,768]{1,0:T(8,128)(2,1)}, bf16[512,768]{1,0:T(8,128)(2,1)S(1)}, u32[]{:S(2)}, u32[]{:S(2)}) collective-permute-start(bf16[512,768]{1,0:T(8,128)(2,1)} %constant_dynamic-update-slice_fusion.near), channel_id=1, source_target_pairs={{0,16},{16,0},{1,17},{17,1},{2,18},{18,2},{3,19},{19,3},{4,20},{20... | collective-permute-start | bytes 2359304 | tf_op jit(solution)/shard_map/ppermute | solution.py:132
  114.7 6.4 %copy-start.8 = (bf16[256,768]{1,0:T(8,128)(2,1)}, bf16[256,768]{1,0:T(8,128)(2,1)S(1)}, u32[]{:S(2)}) copy-start(bf16[256,768]{1,0:T(8,128)(2,1)S(1)} %collective-permute-done.2.third) | copy-start | bytes 1179652
  114.7 19.6 %collective-permute-start.4 = (bf16[256,768]{1,0:T(8,128)(2,1)S(1)}, bf16[256,768]{1,0:T(8,128)(2,1)}, u32[]{:S(2)}, u32[]{:S(2)}) collective-permute-start(bf16[256,768]{1,0:T(8,128)(2,1)S(1)} %collective-permute-done.2.third), channel_id=1, source_target_pairs={{0,16},{16,0},{1,17},{17,1},{2,18},{18,2},{3,19},{19,3},{4,20},{20... | collective-permute-start | bytes 1179656 | tf_op jit(solution)/shard_map/ppermute | solution.py:132
  125.5 34.6 %collective-permute-start.12 = (bf16[512,768]{1,0:T(8,128)(2,1)}, bf16[512,768]{1,0:T(8,128)(2,1)S(1)}, u32[]{:S(2)}, u32[]{:S(2)}) collective-permute-start(bf16[512,768]{1,0:T(8,128)(2,1)} %weight_grad.7), channel_id=1, source_target_pairs={{0,4},{4,0},{8,12},{12,8},{1,5},{5,1},{9,13},{13,9},{2,6},{6,2},{1... | collective-permute-start | bytes 2359304 | tf_op jit(solution)/shard_map/ppermute | solution.py:124
  134.3 0.9 copy-start.7
  145.7 30.3 %all-to-all-start.2 = ((bf16[4,2,4,32,512]{4,3,2,1,0:T(8,128)(2,1)}), bf16[4,2,4,32,512]{4,3,2,1,0:T(8,128)(2,1)S(1)}, u32[]{:S(2)}, u32[]{:S(2)}) async-start(bf16[4,2,4,32,512]{4,3,2,1,0:T(8,128)(2,1)} %space_grad.1), calls=%async_computation.2 | async-start | bytes 2097152 | tf_op jit(solution)/shard_map/all_to_all | solution.py:128
  153.5 43.9 %collective-permute-start.11 = (bf16[512,768]{1,0:T(8,128)(2,1)}, bf16[512,768]{1,0:T(8,128)(2,1)S(1)}, u32[]{:S(2)}, u32[]{:S(2)}) collective-permute-start(bf16[512,768]{1,0:T(8,128)(2,1)} %weight_grad.5), channel_id=1, source_target_pairs={{0,4},{4,0},{8,12},{12,8},{1,5},{5,1},{9,13},{13,9},{2,6},{6,2},{1... | collective-permute-start | bytes 2359304 | tf_op jit(solution)/shard_map/ppermute | solution.py:124
  161.7 46.9 %collective-permute-start.13 = (bf16[512,768]{1,0:T(8,128)(2,1)S(1)}, bf16[512,768]{1,0:T(8,128)(2,1)S(1)}, u32[]{:S(2)}, u32[]{:S(2)}) collective-permute-start(bf16[512,768]{1,0:T(8,128)(2,1)S(1)} %add_convert_fusion), channel_id=1, source_target_pairs={{0,8},{4,12},{8,0},{12,4},{1,9},{5,13},{9,1},{13,5},{2,10},{6,14},... | collective-permute-start | bytes 2359304 | tf_op jit(solution)/shard_map/ppermute | solution.py:124
  176.0 1.0 copy-start.6
  177.0 31.6 %copy-start.5 = (f32[512,768]{1,0:T(8,128)S(1)}, f32[512,768]{1,0:T(8,128)}, u32[]{:S(2)}) copy-start(f32[512,768]{1,0:T(8,128)} %weight_grad.4) | copy-start | bytes 4718596

commit v3 on v0

--- a/solution.py
+++ b/solution.py
@@ -1,11 +1,15 @@
+import functools
 import math
 
 import jax
 import jax.numpy as jnp
 from jax import lax
+from jax.experimental import pallas as pl
+from jax.experimental.pallas import tpu as pltpu
 from jax.sharding import PartitionSpec as P
 
 HD = 128
+SCALE = 1.0 / math.sqrt(HD)
 
 
 def normalize(scores):
@@ -115,6 +119,363 @@
     )
 
 
+def xor_send(value, axis, distance):
+    count = lax.axis_size(axis)
+    return lax.ppermute(value, axis, [(i, i ^ distance) for i in range(count)])
+
+
+def trade(value):
+    return lax.all_to_all(value, "seq", split_axis=0, concat_axis=0, tiled=True)
+
+
+def swap_parts(value):
+    return lax.ppermute(value, "parts", [(0, 1), (1, 0)])
+
+
+def after(value, other):
+    return lax.optimization_barrier((value, other))[0]
+
+
+def gate(values, other):
+    return lax.optimization_barrier((values, other))[0]
+
+
+def nt_dot(a, b):
+    return lax.dot_general(a, b, (((1,), (1,)), ((), ())), preferred_element_type=jnp.float32)
+
+
+def tn_dot(a, b):
+    return lax.dot_general(a, b, (((0,), (0,)), ((), ())), preferred_element_type=jnp.float32)
+
+
+def nn_dot(a, b):
+    return lax.dot_general(a, b, (((1,), (0,)), ((), ())), preferred_element_type=jnp.float32)
+
+
+def softmax_rows(scores, scale, axis):
+    raised = jnp.exp((scores - jnp.max(scores, axis=axis, keepdims=True)) * scale)
+    return raised * (1.0 / jnp.sum(raised, axis=axis, keepdims=True))
+
+
+def params():
+    return pltpu.CompilerParams(vmem_limit_bytes=56 * 1024 * 1024)
+
+
+def whole(*arrays):
+    return [pl.BlockSpec(array.shape, lambda i, ids, rank=len(array.shape): (0,) * rank) for array in arrays]
+
+
+PAIR = 2
+
+
+def space_forward_kernel(q, k, v, out, probs):
+    seq_count, _, band_count, time_len, _ = out.shape
+    for head in range(PAIR):
+        lanes = slice(head * HD, (head + 1) * HD)
+        low = softmax_rows(nt_dot(k[0, :, lanes], q[0, :, lanes]), SCALE, 0).astype(jnp.bfloat16)
+        probs[head] = low
+        mixed = tn_dot(v[0, :, lanes], low).T.astype(jnp.bfloat16)
+        mixed = mixed.reshape(band_count, seq_count, time_len, HD)
+        for step in range(seq_count):
+            out[step, 0, :, :, lanes] = mixed[:, step]
+
+
+def space_forward(q, k, v, seq_count, band_count, time_len):
+    frames, patches, columns = q.shape
+    heads = columns // HD
+    steps = heads // PAIR
+    wide = pl.BlockSpec((1, patches, PAIR * HD), lambda f, h: (f, 0, h))
+    return pl.pallas_call(
+        space_forward_kernel,
+        grid=(frames, steps),
+        in_specs=[wide, wide, wide],
+        out_specs=[
+            pl.BlockSpec((seq_count, 1, band_count, time_len, PAIR * HD), lambda f, h: (0, f, 0, 0, h)),
+            pl.BlockSpec((PAIR, patches, patches), lambda f, h: (f * steps + h, 0, 0)),
+        ],
+        out_shape=[
+            jax.ShapeDtypeStruct((seq_count, frames, band_count, time_len, columns), jnp.bfloat16),
+            jax.ShapeDtypeStruct((frames * heads, patches, patches), jnp.bfloat16),
+        ],
+        compiler_params=params(),
+        name="space_forward",
+    )(q, k, v)
+
+
+def time_probs_kernel(ids, q, k, probs_t, bias):
+    frames, _, time_len, columns = q.shape
+    rows = frames * time_len
+
+    @pl.when(pl.program_id(0) == 0)
+    def _():
+        place = [lax.broadcasted_iota(jnp.int32, (rows, rows), axis) % time_len for axis in (0, 1)]
+        bias[...] = jnp.where(place[0] == place[1], 0.0, -1e30).astype(jnp.float32)
+
+    for head in range(columns // HD):
+        lanes = slice(head * HD, (head + 1) * HD)
+        scores = nt_dot(k[:, 0, :, lanes].reshape(rows, HD), q[:, 0, :, lanes].reshape(rows, HD))
+        probs_t[0, head] = softmax_rows(scores + bias[...], SCALE, 0).astype(jnp.bfloat16)
+
+
+def time_probs(ids, q, k):
+    frames, bands, time_len, columns = q.shape
+    heads = columns // HD
+    rows = frames * time_len
+    spec = pl.BlockSpec((frames, 1, time_len, columns), lambda r, ids: (0, ids[1] ^ r, 0, 0))
+    return pl.pallas_call(
+        time_probs_kernel,
+        grid_spec=pltpu.PrefetchScalarGridSpec(
+            num_scalar_prefetch=1,
+            grid=(bands,),
+            in_specs=[spec, spec],
+            out_specs=pl.BlockSpec((1, heads, rows, rows), lambda r, ids: (r, 0, 0, 0)),
+            scratch_shapes=[pltpu.VMEM((rows, rows), jnp.float32)],
+        ),
+        out_shape=jax.ShapeDtypeStruct((bands, heads, rows, rows), jnp.bfloat16),
+        compiler_params=params(),
+        name="time_probs",
+    )(ids, q, k)
+
+
+def weight_grad_kernel(ids, left, *rest):
+    cots, outs = rest[:-2], rest[-2:]
+    half = len(cots) // 2
+    for step, out in enumerate(outs):
+
+        @pl.when(pl.program_id(0) == step)
+        def _():
+            start = 0
+            for side in (cots[:half], cots[half:]):
+                width = side[0].shape[-1]
+                right = jnp.concatenate([ref[...].reshape(-1, width) for ref in side], axis=0)
+                out[:, start : start + width] = nn_dot(left[...], right).astype(out.dtype)
+                start += width
+
+
+def weight_first_kernel(ids, probs_t, values, *rest):
+    cots, (left, *outs) = rest[:-3], rest[-3:]
+    bands, heads, rows, _ = probs_t.shape
+
+    @pl.when(pl.program_id(0) == 0)
+    def _():
+        for r in range(bands):
+            for head in range(heads):
+                lanes = slice(head * HD, (head + 1) * HD)
+                own = values[:, :, ids[1] ^ r, :, lanes].reshape(rows, HD)
+                left[lanes, r * rows : (r + 1) * rows] = tn_dot(own, probs_t[r, head]).astype(jnp.bfloat16)
+
+    weight_grad_kernel(ids, left, *cots, *outs)
+
+
+def weight_parts(columns, cots, shards, steps, dtype):
+    def place(i, ids):
+        return 0, 0, ids[0] ^ jnp.where(i == 0, steps[0], steps[1])
+
+    specs = [pl.BlockSpec((*piece.shape[:2], piece.shape[2] // shards), place) for piece in cots]
+    width = (cots[0].shape[2] + cots[-1].shape[2]) // shards
+    return specs, [jax.ShapeDtypeStruct((columns, width), dtype)] * 2
+
+
+def weight_first(ids, probs_t, values, cots):
+    bands, _, rows, _ = probs_t.shape
+    columns = values.shape[-1]
+    specs, sums = weight_parts(columns, cots, values.shape[0], (3, 1), jnp.bfloat16)
+    out_shape = [jax.ShapeDtypeStruct((columns, bands * rows), jnp.bfloat16)] + sums
+    return pl.pallas_call(
+        weight_first_kernel,
+        grid_spec=pltpu.PrefetchScalarGridSpec(
+            num_scalar_prefetch=1, grid=(2,), in_specs=whole(probs_t, values) + specs, out_specs=whole(*out_shape)
+        ),
+        out_shape=out_shape,
+        compiler_params=params(),
+        name="weight_first",
+    )(ids, probs_t, values, *cots)
+
+
+def weight_second(ids, left, cots, shards):
+    specs, sums = weight_parts(left.shape[0], cots, shards, (2, 0), jnp.float32)
+    return pl.pallas_call(
+        weight_grad_kernel,
+        grid_spec=pltpu.PrefetchScalarGridSpec(
+            num_scalar_prefetch=1, grid=(2,), in_specs=whole(left) + specs, out_specs=whole(*sums)
+        ),
+        out_shape=sums,
+        compiler_params=params(),
+        name="weight_second",
+    )(ids, left, *cots)
+
+
+def space_grad_kernel(ids, own, first, second, third, other_near, other_third, *rest):
+    cots, (probs_t, out, *weight, tokens_a, tokens_b, chances, sems) = rest[:-8], rest[-8:]
+    me, sub, part = ids[0], ids[1], ids[2]
+    rows = own.shape[0]
+    lines = rows // 2
+    mine, theirs = [pl.ds(pl.multiple_of(which * lines, 128), lines) for which in (part, 1 - part)]
+    copies = []
+
+    def fetch(source, target):
+        copies.append(pltpu.make_async_copy(source, target, sems.at[len(copies)]))
+        copies[-1].start()
+        return copies[-1]
+
+    def fetch_rows(side, start, width):
+        picked = slice(start, start + width)
+        started = [fetch(own.at[:, picked], weight[side].at[:, pl.ds(pl.multiple_of(me * width, 128), width)])]
+        for where, pieces in (
+            (mine, (first, second, third)),
+            (theirs, (other_near.at[:lines], other_near.at[lines:], other_third)),
+        ):
+            for step, piece in enumerate(pieces, 1):
+                place = pl.ds(pl.multiple_of((me ^ step) * width, 128), width)
+                started.append(fetch(piece.at[:, picked], weight[side].at[where, place]))
+        return started
+
+    bands, heads, block, _ = probs_t.shape
+    seq_count, local, _, time_len, _ = out.shape
+    widths = [ref.shape[-1] // seq_count for ref in (tokens_a, tokens_b)]
+    near_side = fetch_rows(0, 0, widths[0]) + [fetch(cots[0], tokens_a.at[0])]
+    far_side = fetch_rows(1, widths[0], widths[1])
+    far_side += [fetch(cots[bands], tokens_b.at[0]), fetch(probs_t.at[0], chances.at[0])]
+    later = [
+        [
+            fetch(cots[r], tokens_a.at[r]),
+            fetch(cots[bands + r], tokens_b.at[r]),
+            fetch(probs_t.at[r], chances.at[r]),
+        ]
+        for r in range(1, bands)
+    ]
+    for r in range(bands):
+        for copy in near_side if r == 0 else later[r - 1]:
+            copy.wait()
+        grad = nt_dot(tokens_a[r].reshape(block, -1), weight[0][...])
+        if r == 0:
+            for copy in far_side:
+                copy.wait()
+        grad = (grad + nt_dot(tokens_b[r].reshape(block, -1), weight[1][...])).astype(jnp.bfloat16)
+        for head in range(heads):
+            lanes = slice(head * HD, (head + 1) * HD)
+            back = nn_dot(chances[r, head], grad[:, lanes]).astype(jnp.bfloat16)
+            out[:, :, sub ^ r, :, lanes] = back.reshape(seq_count, local, time_len, HD)
+
+
+def space_grad(ids, probs_t, weights, cots, seq_count):
+    frames, time_len, _ = cots[0].shape
+    rows, bands = weights[0].shape[0], len(cots) // 2
+    out_shape = jax.ShapeDtypeStruct((seq_count, frames // seq_count, bands, time_len, rows), jnp.bfloat16)
+    depths = (cots[0].shape[2], cots[-1].shape[2])
+    return pl.pallas_call(
+        space_grad_kernel,
+        grid_spec=pltpu.PrefetchScalarGridSpec(
+            num_scalar_prefetch=1,
+            grid=(1,),
+            in_specs=[pl.BlockSpec(memory_space=pl.ANY)] * (len(weights) + len(cots) + 1),
+            out_specs=whole(out_shape)[0],
+            scratch_shapes=[pltpu.VMEM((rows, depth), jnp.bfloat16) for depth in depths]
+            + [pltpu.VMEM((bands, frames, time_len, depth), jnp.bfloat16) for depth in depths]
+            + [
+                pltpu.VMEM(probs_t.shape, jnp.bfloat16),
+                pltpu.SemaphoreType.DMA((2 * (2 * seq_count - 1) + 3 * bands,)),
+            ],
+        ),
+        out_shape=out_shape,
+        compiler_params=params(),
+        name="space_grad",
+    )(ids, *weights, *cots, probs_t)
+
+
+def space_backward_kernel(q, k, v, probs, piece, dq, dk, dv, spare):
+    for head in range(PAIR):
+        lanes = slice(head * HD, (head + 1) * HD)
+        for step in range(piece.shape[0]):
+            spare[head, :, step] = piece[step, 0, :, :, lanes]
+        upstream = spare[head].reshape(q.shape[1], HD)
+        low = probs[head]
+        dv[0, :, lanes] = nn_dot(low, upstream).astype(jnp.bfloat16)
+        chance = nt_dot(v[0, :, lanes], upstream)
+        wide = low.astype(jnp.float32)
+        centre = jnp.sum(wide * chance, axis=0, keepdims=True)
+        score = (wide * (chance - centre)).astype(jnp.bfloat16)
+        dk[0, :, lanes] = (nn_dot(score, q[0, :, lanes]) * SCALE).astype(jnp.bfloat16)
+        dq[0, :, lanes] = (tn_dot(k[0, :, lanes], score) * SCALE).T.astype(jnp.bfloat16)
+
+
+def space_backward(q, k, v, probs, back):
+    frames, patches, columns = q.shape
+    steps = columns // HD // PAIR
+    seq_count, _, band_count, time_len, _ = back.shape
+    wide = pl.BlockSpec((1, patches, PAIR * HD), lambda f, h: (f, 0, h))
+    piece = pl.BlockSpec((seq_count, 1, band_count, time_len, PAIR * HD), lambda f, h: (0, f, 0, 0, h))
+    square = pl.BlockSpec((PAIR, patches, patches), lambda f, h: (f * steps + h, 0, 0))
+    return pl.pallas_call(
+        space_backward_kernel,
+        grid=(frames, steps),
+        in_specs=[wide, wide, wide, square, piece],
+        out_specs=[wide, wide, wide],
+        out_shape=[jax.ShapeDtypeStruct(q.shape, jnp.bfloat16)] * 3,
+        scratch_shapes=[pltpu.VMEM((PAIR, band_count, seq_count, time_len, HD), jnp.bfloat16)],
+        compiler_params=params(),
+        name="space_backward",
+    )(q, k, v, probs, back)
+
+
+def on_small_slice(q_space, k_space, v_space, q_time, k_time, out_weight, cotangent):
+    seq_count, band_count = lax.axis_size("seq"), lax.axis_size("sub")
+    time_len = q_space.shape[1] // band_count // seq_count
+    me, sub, part = lax.axis_index("seq"), lax.axis_index("sub"), lax.axis_index("parts")
+    ids = jnp.stack([me, sub, part]).astype(jnp.int32)
+    rows, width = out_weight.shape
+
+    half = lax.dynamic_slice_in_dim(out_weight, part * (rows // 2), rows // 2, 0)
+    second = xor_send(half, "seq", 2)
+    first = xor_send(half, "seq", 1)
+
+    local = cotangent.shape[0]
+    bounds = (0, width // 3, width)
+    split = []
+    for low, high in zip(bounds, bounds[1:]):
+        picked = [cotangent[:, :, shard * width + low : shard * width + high] for shard in range(seq_count)]
+        picked = jnp.concatenate(picked, axis=2)
+        picked = picked.reshape(local, seq_count, time_len, -1).transpose(1, 0, 2, 3)
+        split.append(picked.reshape(seq_count * local, time_len, -1))
+    here = [trade(split[0]), None]
+    q_space = after(q_space, split)
+    mixed, probs = space_forward(q_space, k_space, v_space, seq_count, band_count, time_len)
+    q_time = after(q_time, mixed)
+    chances = time_probs(ids, q_time, k_time)
+    first, second, here[0], following, mixed = gate((first, second, here[0], split[1], mixed), chances)
+    here[1] = trade(following)
+    third = xor_send(second, "seq", 1)
+    other_near = swap_parts(jnp.concatenate([first, second], axis=0))
+    across = [xor_send(here[0], "sub", 2), None]
+    beside = [xor_send(here[0], "sub", 1), None]
+
+    here[1], third, other_near, across[0], mixed = gate((here[1], third, other_near, across[0], mixed), beside[0])
+    moved = trade(mixed)
+    across[1] = xor_send(here[1], "sub", 2)
+    beside[1] = xor_send(here[1], "sub", 1)
+    cross = [xor_send(across[0], "sub", 1), None]
+    other_third = swap_parts(third)
+    across[1] = after(across[1], (other_third, cross[0]))
+    cross[1] = xor_send(across[1], "sub", 1)
+    cots = []
+    for side in range(2):
+        cots += [here[side], beside[side], across[side], cross[side]]
+    weights = [out_weight, first, second, third, other_near, other_third]
+
+    turned, third_sum, first_sum = weight_first(ids, chances, moved, cots)
+    back = space_grad(ids, after(chances, third_sum), weights, cots, seq_count)
+    returned = trade(back)
+    second_sum, own_sum = weight_second(ids, after(turned, back), cots, seq_count)
+    third_sum = xor_send(third_sum, "seq", 1)
+    paired = (second_sum + third_sum.astype(jnp.float32)).astype(jnp.bfloat16)
+    far = xor_send(paired, "seq", 2)
+    near = xor_send(after(first_sum, third_sum), "seq", 1)
+    dq, dk, dv = space_backward(q_space, k_space, v_space, probs, returned)
+    far, near = gate((far, near), dq)
+    d_weight = own_sum + near.astype(jnp.float32) + far.astype(jnp.float32)
+    return dq, dk, dv, d_weight
+
+
 def solution(mesh):
     in_specs = (
         P(("parts", "seq"), None, "sub"),
@@ -131,6 +492,7 @@
         P(("parts", "seq"), None, "sub"),
         P(("parts", "sub"), "seq"),
     )
+    small = (mesh.shape["parts"], mesh.shape["seq"], mesh.shape["sub"]) == (2, 4, 4)
     return jax.shard_map(
-        on_device, mesh=mesh, in_specs=in_specs, out_specs=out_specs, check_vma=False
-    )
+        on_small_slice if small else on_device, mesh=mesh, in_specs=in_specs, out_specs=out_specs, check_vma=False
+    )

time: 301 us -> 187 us (0.62)
  blocking collectives: 146 us -> 0 us
  matrix products: 73.3 us -> 0 us
  waiting for transfers between devices: 37 us -> 97 us
  Pallas kernels: 0 us -> 46.1 us
  starting transfers between devices: 6.55 us -> 30.7 us
  local copies, waits for them, and re-layouts: 21.2 us -> 6.49 us
  between operations: 14 us -> 0.81 us
    all_to_all x3 -> x0, blocking collectives: 146 us -> none  [the longest x1 57.4 us: on_device(): lax.all_to_all(rounded, 'seq', split_axis=2, concat_axis=0, tiled=True)]
    ppermute x0 -> x14, waiting for transfers between devices: none -> 73.4 us  [the longest x12 63.4 us: xor_send(): return lax.ppermute(value, axis, [(i, i ^ distance) for i in range(count)])]
    dot_general x9 -> x0, matrix products: 63.5 us -> none  [the longest x1 15.2 us: on_device(): jnp.einsum('fhqk,fkhd->fqhd', score_grad, space_keys, preferred_element_t...]
    pallas_call x0 -> x6, Pallas kernels: none -> 46.1 us  [the longest x1 9.54 us: space_grad(): pl.pallas_call(space_grad_kernel, grid_spec=pltpu.PrefetchScalarGridSpec(...]
    all_gather x2 -> x0, waiting for transfers between devices: 18.4 us -> none  [the longest x1 18.3 us: on_device(): weight_rows = lax.all_gather(out_weight, 'seq', axis=1, tiled=True)]
    ppermute x0 -> x14, starting transfers between devices: none -> 12.9 us  [the longest x12 9.72 us: xor_send(): return lax.ppermute(value, axis, [(i, i ^ distance) for i in range(count)])]
    all_to_all x1 -> x4, starting transfers between devices: 6.48 us -> 17.8 us  [trade(): return lax.all_to_all(value, 'seq', split_axis=0, concat_axis=0, tiled=True)]
    reshape x13 -> x2, local copies, waits for them, and re-layouts: 12.3 us -> 1.87 us  [on_small_slice(): picked.reshape(local, seq_count, time_len, -1).transpose(1, 0, 2, 3)]
  transfers between devices with their start and end apart: 4 -> 18, of which waited for: 2 -> 9; matrix products, arithmetic and copies ran while one was open for 31% -> 3% of each run, Pallas kernels for 0% -> 21%
where the time goes in v3:
time: 187 us; the launch traced here: 186 us
  waiting for transfers between devices  97 us (52%)
  Pallas kernels  46.1 us (25%)
  starting transfers between devices  30.7 us (16%)
  local copies, waits for them, and re-layouts  6.49 us (3%)
  other arithmetic  4.75 us (3%)
    ppermute x12, waiting for transfers between devices, xor_send(): return lax.ppermute(value, axis, [(i, i ^ distance) for i in range(count)])  63.4 us
    all_to_all x4, waiting for transfers between devices, trade(): return lax.all_to_all(value, 'seq', split_axis=0, concat_axis=0, tiled=True)  23.6 us
    all_to_all x4, starting transfers between devices, trade(): return lax.all_to_all(value, 'seq', split_axis=0, concat_axis=0, tiled=True)  17.8 us
    ppermute x2, waiting for transfers between devices, swap_parts(): return lax.ppermute(value, 'parts', [(0, 1), (1, 0)])  9.99 us
    ppermute x12, starting transfers between devices, xor_send(): return lax.ppermute(value, axis, [(i, i ^ distance) for i in range(count)])  9.72 us
    pallas_call x1, Pallas kernels, space_grad(): pl.pallas_call(space_grad_kernel, grid_spec=pltpu.PrefetchScalarGridSpec(...  9.54 us
    pallas_call x1, Pallas kernels, space_backward(): pl.pallas_call(space_backward_kernel, grid=(frames, steps), in_specs=[wid...  8.92 us
    pallas_call x1, Pallas kernels, space_forward(): pl.pallas_call(space_forward_kernel, grid=(frames, steps), in_specs=[wide...  8.31 us
  transfers between devices with their start and end apart: 18, of which 9 were waited for; matrix products, arithmetic and copies ran while one was open for 3% of the time, Pallas kernels for 21%

profile of v3, /device:TPU:0, one launch (start us, length us, event | category | flops | bytes accessed | tf_op | source)
XLA Modules:
  0.0 185.8 jit_solution(6260682212688729716)
XLA Ops:
  0.6 1.1 fusion.1
  1.8 0.0 copy-start.6
  1.8 0.1 pad_maximum_fusion.2
  1.8 0.0 copy-start.9
  1.9 0.8 copy.11
  2.7 6.3 %all-to-all-start = ((bf16[8,32,1024]{2,1,0:T(8,128)(2,1)}), bf16[8,32,1024]{2,1,0:T(8,128)(2,1)S(1)}, u32[]{:S(2)}, u32[]{:S(2)}) async-start(bf16[8,32,1024]{2,1,0:T(8,128)(2,1)} %bitcast.2), calls=%async_computation | async-start | bytes 1048576 | tf_op jit(solution)/shard_map/all_to_all | solution.py:128
  9.0 0.8 constant_dynamic-slice_fusion
  9.8 2.9 %collective-permute-start.1 = (bf16[256,768]{1,0:T(8,128)(2,1)}, bf16[256,768]{1,0:T(8,128)(2,1)S(1)}, u32[]{:S(2)}, u32[]{:S(2)}) collective-permute-start(bf16[256,768]{1,0:T(8,128)(2,1)} %constant_dynamic-slice_fusion), channel_id=1, source_target_pairs={{0,8},{4,12},{8,0},{12,4},{1,9},{5,13},{9,1},{13,5},{2,10},{6,14},... | collective-permute-start | bytes 1179656 | tf_op jit(solution)/shard_map/ppermute | solution.py:124
  12.7 1.5 collective-permute-start
  14.2 0.9 fusion
  15.1 1.1 pad_maximum_fusion
  16.2 1.0 copy.12
  17.2 8.3 %space_forward.1 = (bf16[4,2,4,32,512]{4,3,2,1,0:T(8,128)(2,1)}, bf16[8,512,512]{2,1,0:T(8,128)(2,1)}) custom-call(bf16[2,512,512]{2,1,0:T(8,128)(2,1)} %q.2, bf16[2,512,512]{2,1,0:T(8,128)(2,1)} %k.5, bf16[2,512,512]{2,1,0:T(8,128)(2,1)} %v.3), custom_call_target="tpu_custom_call" | custom-call | tf_op jit(solution)/shard_map/space_forward/pallas_call | solution.py:188
  25.6 0.6 pad_add_fusion.ids
  26.1 5.6 %time_probs.1.probs_t.rest_8_ = bf16[4,4,256,256]{3,2,1,0:T(8,128)(2,1)} custom-call(s32[3]{0:T(128)} %pad_add_fusion.ids, bf16[8,4,32,512]{3,2,1,0:T(8,128)(2,1)} %q.1, bf16[8,4,32,512]{3,2,1,0:T(8,128)(2,1)} %k.4), custom_call_target="tpu_custom_call" | custom-call | tf_op jit(solution)/shard_map/time_probs/pallas_call | solution.py:225
  31.8 8.6 %collective-permute-done.1.second = bf16[256,768]{1,0:T(8,128)(2,1)S(1)} collective-permute-done((bf16[256,768]{1,0:T(8,128)(2,1)}, bf16[256,768]{1,0:T(8,128)(2,1)S(1)}, u32[]{:S(2)}, u32[]{:S(2)}) %collective-permute-start.1) | collective-permute-done | bytes 393248 | tf_op jit(solution)/shard_map/ppermute | solution.py:124
  40.4 0.0 collective-permute-done.first
  40.4 0.0 all-to-all-done.rest_0_
  40.4 3.5 %all-to-all-start.1 = ((bf16[8,32,2048]{2,1,0:T(8,128)(2,1)}), bf16[8,32,2048]{2,1,0:T(8,128)(2,1)S(1)}, u32[]{:S(2)}, u32[]{:S(2)}) async-start(bf16[8,32,2048]{2,1,0:T(8,128)(2,1)} %bitcast.5), calls=%async_computation.1 | async-start | bytes 2097152 | tf_op jit(solution)/shard_map/all_to_all | solution.py:128
  43.9 0.1 pad_maximum_fusion.1
  44.0 1.6 collective-permute-start.3
  45.6 0.0 collective-permute-start.5
  45.6 1.5 collective-permute-start.4
  47.1 2.0 %collective-permute-start.2 = (bf16[256,768]{1,0:T(8,128)(2,1)S(1)}, bf16[256,768]{1,0:T(8,128)(2,1)}, u32[]{:S(2)}, u32[]{:S(2)}) collective-permute-start(bf16[256,768]{1,0:T(8,128)(2,1)S(1)} %collective-permute-done.1.second), channel_id=1, source_target_pairs={{0,4},{4,0},{8,12},{12,8},{1,5},{5,1},{9,13},{13,9},{2,6},{6,2},{1... | collective-permute-start | bytes 1179656 | tf_op jit(solution)/shard_map/ppermute | solution.py:124
  49.0 22.1 %collective-permute-done.2.third = bf16[256,768]{1,0:T(8,128)(2,1)} collective-permute-done((bf16[256,768]{1,0:T(8,128)(2,1)S(1)}, bf16[256,768]{1,0:T(8,128)(2,1)}, u32[]{:S(2)}, u32[]{:S(2)}) %collective-permute-start.2) | collective-permute-done | bytes 393248 | tf_op jit(solution)/shard_map/ppermute | solution.py:124
  71.1 0.0 collective-permute-done.5.rest_1_
  71.1 0.8 copy-done.4
  72.0 1.6 collective-permute-start.9
  73.5 4.2 %all-to-all-start.2 = ((bf16[4,2,4,32,512]{4,3,2,1,0:T(8,128)(2,1)}), bf16[4,2,4,32,512]{4,3,2,1,0:T(8,128)(2,1)}, u32[]{:S(2)}, u32[]{:S(2)}) async-start(bf16[4,2,4,32,512]{4,3,2,1,0:T(8,128)(2,1)} %get-tuple-element.46), calls=%async_computation.2 | async-start | bytes 2097152 | tf_op jit(solution)/shard_map/all_to_all | solution.py:128
  77.8 1.6 collective-permute-start.6
  79.3 0.2 collective-permute-start.8
  79.6 10.0 %collective-permute-done.6.other_third = bf16[256,768]{1,0:T(8,128)(2,1)S(1)} collective-permute-done((bf16[256,768]{1,0:T(8,128)(2,1)}, bf16[256,768]{1,0:T(8,128)(2,1)S(1)}, u32[]{:S(2)}, u32[]{:S(2)}) %collective-permute-start.6) | collective-permute-done | bytes 393248 | tf_op jit(solution)/shard_map/ppermute | solution.py:132
  89.6 3.7 %collective-permute-done.9.rest_6_ = bf16[8,32,2048]{2,1,0:T(8,128)(2,1)S(1)} collective-permute-done((bf16[8,32,2048]{2,1,0:T(8,128)(2,1)S(1)}, bf16[8,32,2048]{2,1,0:T(8,128)(2,1)S(1)}, u32[]{:S(2)}, u32[]{:S(2)}) %collective-permute-start.9) | collective-permute-done | bytes 1048608 | tf_op jit(solution)/shard_map/ppermute | solution.py:124
  93.3 0.0 copy-start.2
  93.3 11.2 %all-to-all-done.2.values = bf16[4,2,4,32,512]{4,3,2,1,0:T(8,128)(2,1)} async-done(((bf16[4,2,4,32,512]{4,3,2,1,0:T(8,128)(2,1)}), bf16[4,2,4,32,512]{4,3,2,1,0:T(8,128)(2,1)}, u32[]{:S(2)}, u32[]{:S(2)}) %all-to-all-start.2) | async-done | bytes 1048608 | tf_op jit(solution)/shard_map/all_to_all | solution.py:128
  104.5 7.2 %weight_first.1 = (bf16[512,1024]{1,0:T(8,128)(2,1)}, bf16[512,768]{1,0:T(8,128)(2,1)}, bf16[512,768]{1,0:T(8,128)(2,1)}) custom-call(s32[3]{0:T(128)} %pad_add_fusion.ids, bf16[4,4,256,256]{3,2,1,0:T(8,128)(2,1)} %time_probs.1.probs_t.rest_8_, bf16[4,2,4,32,512]{4,3,2,1,0:T(8,128)(2,1)} %all-to-all-done.2.values, bf16[8,32,1024]{2,1,0:T(8,128)(2,1)} %copy-done.3, ...), custom_call_target="tpu_custom_call" | custom-call | tf_op jit(solution)/shard_map/weight_first/pallas_call | solution.py:284
  111.8 9.5 %space_grad.1 = bf16[4,2,4,32,512]{4,3,2,1,0:T(8,128)(2,1)} custom-call(s32[3]{0:T(128)} %pad_add_fusion.ids, bf16[512,768]{1,0:T(8,128)(2,1)} %own.1, bf16[256,768]{1,0:T(8,128)(2,1)} %copy-done.8, bf16[256,768]{1,0:T(8,128)(2,1)} %copy-done.7, bf16[256,768]{1,0:T(8,128)(2,1)} %collective-permute-done.2.third, ...), custom_call_target="tpu_custom_call" | custom-call | tf_op jit(solution)/shard_map/space_grad/pallas_call | solution.py:366
  121.3 3.7 %all-to-all-start.3 = ((bf16[4,2,4,32,512]{4,3,2,1,0:T(8,128)(2,1)}), bf16[4,2,4,32,512]{4,3,2,1,0:T(8,128)(2,1)S(1)}, u32[]{:S(2)}, u32[]{:S(2)}) async-start(bf16[4,2,4,32,512]{4,3,2,1,0:T(8,128)(2,1)} %space_grad.1), calls=%async_computation.3 | async-start | bytes 2097152 | tf_op jit(solution)/shard_map/all_to_all | solution.py:128
  125.0 6.4 %weight_second.1 = (f32[512,768]{1,0:T(8,128)}, f32[512,768]{1,0:T(8,128)}) custom-call(s32[3]{0:T(128)} %pad_add_fusion.ids, bf16[512,1024]{1,0:T(8,128)(2,1)} %get-tuple-element.53.left, bf16[8,32,1024]{2,1,0:T(8,128)(2,1)} %copy-done.3, bf16[8,32,1024]{2,1,0:T(8,128)(2,1)} %copy-done.4, bf16[8,32,1024]{2,1,0:T(8,128)(2,1)} %collective-permute-done.4.rest_2_, ...), custom_call_target="tpu_custom_call" | custom-call | tf_op jit(solution)/shard_map/weight_second/pallas_call | solution.py:297
  131.5 6.6 %collective-permute-done.11 = bf16[512,768]{1,0:T(8,128)(2,1)S(1)} collective-permute-done((bf16[512,768]{1,0:T(8,128)(2,1)}, bf16[512,768]{1,0:T(8,128)(2,1)S(1)}, u32[]{:S(2)}, u32[]{:S(2)}) %collective-permute-start.11) | collective-permute-done | bytes 786464 | tf_op jit(solution)/shard_map/ppermute | solution.py:124
  138.0 1.6 add_convert_fusion
  139.6 0.1 collective-permute-start.12
  139.7 12.4 %all-to-all-done.3.piece = bf16[4,2,4,32,512]{4,3,2,1,0:T(8,128)(2,1)S(1)} async-done(((bf16[4,2,4,32,512]{4,3,2,1,0:T(8,128)(2,1)}), bf16[4,2,4,32,512]{4,3,2,1,0:T(8,128)(2,1)S(1)}, u32[]{:S(2)}, u32[]{:S(2)}) %all-to-all-start.3) | async-done | bytes 1048608 | tf_op jit(solution)/shard_map/all_to_all | solution.py:128
  152.1 1.0 copy-done.5
  153.1 8.9 %space_backward.1 = (bf16[2,512,512]{2,1,0:T(8,128)(2,1)}, bf16[2,512,512]{2,1,0:T(8,128)(2,1)}, bf16[2,512,512]{2,1,0:T(8,128)(2,1)}) custom-call(bf16[2,512,512]{2,1,0:T(8,128)(2,1)} %q.2, bf16[2,512,512]{2,1,0:T(8,128)(2,1)} %k.5, bf16[2,512,512]{2,1,0:T(8,128)(2,1)} %v.3, bf16[8,512,512]{2,1,0:T(8,128)(2,1)} %get-tuple-element.33.probs, ...), custom_call_target="tpu_custom_call" | custom-call | tf_op jit(solution)/shard_map/space_backward/pallas_call | solution.py:409
  162.0 16.9 %collective-permute-done.13 = bf16[512,768]{1,0:T(8,128)(2,1)S(1)} collective-permute-done((bf16[512,768]{1,0:T(8,128)(2,1)}, bf16[512,768]{1,0:T(8,128)(2,1)S(1)}, u32[]{:S(2)}, u32[]{:S(2)}) %collective-permute-start.13) | collective-permute-done | bytes 786464 | tf_op jit(solution)/shard_map/ppermute | solution.py:124
  178.8 5.6 %collective-permute-done.12 = bf16[512,768]{1,0:T(8,128)(2,1)S(1)} collective-permute-done((bf16[512,768]{1,0:T(8,128)(2,1)S(1)}, bf16[512,768]{1,0:T(8,128)(2,1)S(1)}, u32[]{:S(2)}, u32[]{:S(2)}) %collective-permute-start.12) | collective-permute-done | bytes 786464 | tf_op jit(solution)/shard_map/ppermute | solution.py:124
  184.5 1.3 convert_add_fusion
  (29 shorter events, 0.1 us)
Async XLA Ops:
  1.8 7.2 %copy-start.6 = (bf16[512,768]{1,0:T(8,128)(2,1)S(1)}, bf16[512,768]{1,0:T(8,128)(2,1)}, u32[]{:S(2)}) copy-start(bf16[512,768]{1,0:T(8,128)(2,1)} %own.1) | copy-start | bytes 2359300
  1.8 12.3 %copy-start.9 = (bf16[2,128,3072]{2,1,0:T(8,128)(2,1)S(1)}, bf16[2,128,3072]{2,1,0:T(8,128)(2,1)}, u32[]{:S(2)}) copy-start(bf16[2,128,3072]{2,1,0:T(8,128)(2,1)} %param.13) | copy-start | bytes 4718596
  2.7 37.7 %all-to-all-start = ((bf16[8,32,1024]{2,1,0:T(8,128)(2,1)}), bf16[8,32,1024]{2,1,0:T(8,128)(2,1)S(1)}, u32[]{:S(2)}, u32[]{:S(2)}) async-start(bf16[8,32,1024]{2,1,0:T(8,128)(2,1)} %bitcast.2), calls=%async_computation | async-start | bytes 1048576 | tf_op jit(solution)/shard_map/all_to_all | solution.py:128
  9.8 30.6 %collective-permute-start.1 = (bf16[256,768]{1,0:T(8,128)(2,1)}, bf16[256,768]{1,0:T(8,128)(2,1)S(1)}, u32[]{:S(2)}, u32[]{:S(2)}) collective-permute-start(bf16[256,768]{1,0:T(8,128)(2,1)} %constant_dynamic-slice_fusion), channel_id=1, source_target_pairs={{0,8},{4,12},{8,0},{12,4},{1,9},{5,13},{9,1},{13,5},{2,10},{6,14},... | collective-permute-start | bytes 1179656 | tf_op jit(solution)/shard_map/ppermute | solution.py:124
  12.7 27.7 %collective-permute-start = (bf16[256,768]{1,0:T(8,128)(2,1)}, bf16[256,768]{1,0:T(8,128)(2,1)S(1)}, u32[]{:S(2)}, u32[]{:S(2)}) collective-permute-start(bf16[256,768]{1,0:T(8,128)(2,1)} %constant_dynamic-slice_fusion), channel_id=1, source_target_pairs={{0,4},{4,0},{8,12},{12,8},{1,5},{5,1},{9,13},{13,9},{2,6},{6,2},{1... | collective-permute-start | bytes 1179656 | tf_op jit(solution)/shard_map/ppermute | solution.py:124
  40.4 6.7 %copy-start.7 = (bf16[256,768]{1,0:T(8,128)(2,1)}, bf16[256,768]{1,0:T(8,128)(2,1)S(1)}, u32[]{:S(2)}) copy-start(bf16[256,768]{1,0:T(8,128)(2,1)S(1)} %collective-permute-done.1.second) | copy-start | bytes 1179652
  40.4 3.6 %copy-start.8 = (bf16[256,768]{1,0:T(8,128)(2,1)}, bf16[256,768]{1,0:T(8,128)(2,1)S(1)}, u32[]{:S(2)}) copy-start(bf16[256,768]{1,0:T(8,128)(2,1)S(1)} %collective-permute-done.first) | copy-start | bytes 1179652
  40.4 5.2 %copy-start.3 = (bf16[8,32,1024]{2,1,0:T(8,128)(2,1)}, bf16[8,32,1024]{2,1,0:T(8,128)(2,1)S(1)}, u32[]{:S(2)}) copy-start(bf16[8,32,1024]{2,1,0:T(8,128)(2,1)S(1)} %all-to-all-done.rest_0_) | copy-start | bytes 1572868
  40.4 31.6 %all-to-all-start.1 = ((bf16[8,32,2048]{2,1,0:T(8,128)(2,1)}), bf16[8,32,2048]{2,1,0:T(8,128)(2,1)S(1)}, u32[]{:S(2)}, u32[]{:S(2)}) async-start(bf16[8,32,2048]{2,1,0:T(8,128)(2,1)} %bitcast.5), calls=%async_computation.1 | async-start | bytes 2097152 | tf_op jit(solution)/shard_map/all_to_all | solution.py:128
  44.0 28.0 %collective-permute-start.3 = (bf16[512,768]{1,0:T(8,128)(2,1)S(1)}, bf16[512,768]{1,0:T(8,128)(2,1)}, u32[]{:S(2)}, u32[]{:S(2)}) collective-permute-start(bf16[512,768]{1,0:T(8,128)(2,1)S(1)} %pad_maximum_fusion.1), channel_id=1, source_target_pairs={{0,16},{16,0},{1,17},{17,1},{2,18},{18,2},{3,19},{19,3},{4,20},{20... | collective-permute-start | bytes 2359304 | tf_op jit(solution)/shard_map/ppermute | solution.py:132
  45.6 25.6 %collective-permute-start.5 = (bf16[8,32,1024]{2,1,0:T(8,128)(2,1)S(1)}, bf16[8,32,1024]{2,1,0:T(8,128)(2,1)S(1)}, u32[]{:S(2)}, u32[]{:S(2)}) collective-permute-start(bf16[8,32,1024]{2,1,0:T(8,128)(2,1)S(1)} %all-to-all-done.rest_0_), channel_id=1, source_target_pairs={{0,1},{1,0},{2,3},{3,2},{4,5},{5,4},{6,7},{7,6},{8,9},{9,8},{10,11... | collective-permute-start | bytes 1572872 | tf_op jit(solution)/shard_map/ppermute | solution.py:124
  45.6 25.6 %collective-permute-start.4 = (bf16[8,32,1024]{2,1,0:T(8,128)(2,1)S(1)}, bf16[8,32,1024]{2,1,0:T(8,128)(2,1)}, u32[]{:S(2)}, u32[]{:S(2)}) collective-permute-start(bf16[8,32,1024]{2,1,0:T(8,128)(2,1)S(1)} %all-to-all-done.rest_0_), channel_id=1, source_target_pairs={{0,2},{1,3},{2,0},{3,1},{4,6},{5,7},{6,4},{7,5},{8,10},{9,11},{10,... | collective-permute-start | bytes 1572872 | tf_op jit(solution)/shard_map/ppermute | solution.py:124
  47.1 24.1 %collective-permute-start.2 = (bf16[256,768]{1,0:T(8,128)(2,1)S(1)}, bf16[256,768]{1,0:T(8,128)(2,1)}, u32[]{:S(2)}, u32[]{:S(2)}) collective-permute-start(bf16[256,768]{1,0:T(8,128)(2,1)S(1)} %collective-permute-done.1.second), channel_id=1, source_target_pairs={{0,4},{4,0},{8,12},{12,8},{1,5},{5,1},{9,13},{13,9},{2,6},{6,2},{1... | collective-permute-start | bytes 1179656 | tf_op jit(solution)/shard_map/ppermute | solution.py:124
  71.1 0.8 copy-start.4
  72.0 32.5 %copy-start = (bf16[8,32,2048]{2,1,0:T(8,128)(2,1)}, bf16[8,32,2048]{2,1,0:T(8,128)(2,1)S(1)}, u32[]{:S(2)}) copy-start(bf16[8,32,2048]{2,1,0:T(8,128)(2,1)S(1)} %all-to-all-done.1.rest_4_) | copy-start | bytes 3145732
  72.0 21.3 %collective-permute-start.9 = (bf16[8,32,2048]{2,1,0:T(8,128)(2,1)S(1)}, bf16[8,32,2048]{2,1,0:T(8,128)(2,1)S(1)}, u32[]{:S(2)}, u32[]{:S(2)}) collective-permute-start(bf16[8,32,2048]{2,1,0:T(8,128)(2,1)S(1)} %all-to-all-done.1.rest_4_), channel_id=1, source_target_pairs={{0,2},{1,3},{2,0},{3,1},{4,6},{5,7},{6,4},{7,5},{8,10},{9,11},{10,... | collective-permute-start | bytes 3145736 | tf_op jit(solution)/shard_map/ppermute | solution.py:124
  73.5 16.1 %collective-permute-start.7 = (bf16[8,32,1024]{2,1,0:T(8,128)(2,1)}, bf16[8,32,1024]{2,1,0:T(8,128)(2,1)}, u32[]{:S(2)}, u32[]{:S(2)}) collective-permute-start(bf16[8,32,1024]{2,1,0:T(8,128)(2,1)} %collective-permute-done.4.rest_2_), channel_id=1, source_target_pairs={{0,1},{1,0},{2,3},{3,2},{4,5},{5,4},{6,7},{7,6},{8,9},{9,8},{10,11... | collective-permute-start | bytes 1572872 | tf_op jit(solution)/shard_map/ppermute | solution.py:124
  73.5 31.0 %all-to-all-start.2 = ((bf16[4,2,4,32,512]{4,3,2,1,0:T(8,128)(2,1)}), bf16[4,2,4,32,512]{4,3,2,1,0:T(8,128)(2,1)}, u32[]{:S(2)}, u32[]{:S(2)}) async-start(bf16[4,2,4,32,512]{4,3,2,1,0:T(8,128)(2,1)} %get-tuple-element.46), calls=%async_computation.2 | async-start | bytes 2097152 | tf_op jit(solution)/shard_map/all_to_all | solution.py:128
  77.8 11.8 %collective-permute-start.6 = (bf16[256,768]{1,0:T(8,128)(2,1)}, bf16[256,768]{1,0:T(8,128)(2,1)S(1)}, u32[]{:S(2)}, u32[]{:S(2)}) collective-permute-start(bf16[256,768]{1,0:T(8,128)(2,1)} %collective-permute-done.2.third), channel_id=1, source_target_pairs={{0,16},{16,0},{1,17},{17,1},{2,18},{18,2},{3,19},{19,3},{4,20},{20... | collective-permute-start | bytes 1179656 | tf_op jit(solution)/shard_map/ppermute | solution.py:132
  79.3 13.9 %collective-permute-start.8 = (bf16[8,32,2048]{2,1,0:T(8,128)(2,1)S(1)}, bf16[8,32,2048]{2,1,0:T(8,128)(2,1)S(1)}, u32[]{:S(2)}, u32[]{:S(2)}) collective-permute-start(bf16[8,32,2048]{2,1,0:T(8,128)(2,1)S(1)} %all-to-all-done.1.rest_4_), channel_id=1, source_target_pairs={{0,1},{1,0},{2,3},{3,2},{4,5},{5,4},{6,7},{7,6},{8,9},{9,8},{10,11... | collective-permute-start | bytes 3145736 | tf_op jit(solution)/shard_map/ppermute | solution.py:124
  89.6 3.7 %copy-start.11 = (bf16[256,768]{1,0:T(8,128)(2,1)}, bf16[256,768]{1,0:T(8,128)(2,1)S(1)}, u32[]{:S(2)}) copy-start(bf16[256,768]{1,0:T(8,128)(2,1)S(1)} %collective-permute-done.6.other_third) | copy-start | bytes 1179652
  93.3 11.2 %copy-start.1 = (bf16[8,32,2048]{2,1,0:T(8,128)(2,1)}, bf16[8,32,2048]{2,1,0:T(8,128)(2,1)S(1)}, u32[]{:S(2)}) copy-start(bf16[8,32,2048]{2,1,0:T(8,128)(2,1)S(1)} %collective-permute-done.9.rest_6_) | copy-start | bytes 3145732
  93.3 11.2 %collective-permute-start.10 = (bf16[8,32,2048]{2,1,0:T(8,128)(2,1)S(1)}, bf16[8,32,2048]{2,1,0:T(8,128)(2,1)}, u32[]{:S(2)}, u32[]{:S(2)}) collective-permute-start(bf16[8,32,2048]{2,1,0:T(8,128)(2,1)S(1)} %collective-permute-done.9.rest_6_), channel_id=1, source_target_pairs={{0,1},{1,0},{2,3},{3,2},{4,5},{5,4},{6,7},{7,6},{8,9},{9,8},{10,11... | collective-permute-start | bytes 3145736 | tf_op jit(solution)/shard_map/ppermute | solution.py:124
  93.3 11.2 %copy-start.2 = (bf16[8,32,2048]{2,1,0:T(8,128)(2,1)}, bf16[8,32,2048]{2,1,0:T(8,128)(2,1)S(1)}, u32[]{:S(2)}) copy-start(bf16[8,32,2048]{2,1,0:T(8,128)(2,1)S(1)} %collective-permute-done.8.rest_5_) | copy-start | bytes 3145732
  111.8 26.3 %collective-permute-start.11 = (bf16[512,768]{1,0:T(8,128)(2,1)}, bf16[512,768]{1,0:T(8,128)(2,1)S(1)}, u32[]{:S(2)}, u32[]{:S(2)}) collective-permute-start(bf16[512,768]{1,0:T(8,128)(2,1)} %get-tuple-element.47), channel_id=1, source_target_pairs={{0,4},{4,0},{8,12},{12,8},{1,5},{5,1},{9,13},{13,9},{2,6},{6,2},{1... | collective-permute-start | bytes 2359304 | tf_op jit(solution)/shard_map/ppermute | solution.py:124
  121.3 30.8 %all-to-all-start.3 = ((bf16[4,2,4,32,512]{4,3,2,1,0:T(8,128)(2,1)}), bf16[4,2,4,32,512]{4,3,2,1,0:T(8,128)(2,1)S(1)}, u32[]{:S(2)}, u32[]{:S(2)}) async-start(bf16[4,2,4,32,512]{4,3,2,1,0:T(8,128)(2,1)} %space_grad.1), calls=%async_computation.3 | async-start | bytes 2097152 | tf_op jit(solution)/shard_map/all_to_all | solution.py:128
  138.0 40.8 %collective-permute-start.13 = (bf16[512,768]{1,0:T(8,128)(2,1)}, bf16[512,768]{1,0:T(8,128)(2,1)S(1)}, u32[]{:S(2)}, u32[]{:S(2)}) collective-permute-start(bf16[512,768]{1,0:T(8,128)(2,1)} %get-tuple-element.57), channel_id=1, source_target_pairs={{0,4},{4,0},{8,12},{12,8},{1,5},{5,1},{9,13},{13,9},{2,6},{6,2},{1... | collective-permute-start | bytes 2359304 | tf_op jit(solution)/shard_map/ppermute | solution.py:124
  139.6 44.9 %collective-permute-start.12 = (bf16[512,768]{1,0:T(8,128)(2,1)S(1)}, bf16[512,768]{1,0:T(8,128)(2,1)S(1)}, u32[]{:S(2)}, u32[]{:S(2)}) collective-permute-start(bf16[512,768]{1,0:T(8,128)(2,1)S(1)} %add_convert_fusion), channel_id=1, source_target_pairs={{0,8},{4,12},{8,0},{12,4},{1,9},{5,13},{9,1},{13,5},{2,10},{6,14},... | collective-permute-start | bytes 2359304 | tf_op jit(solution)/shard_map/ppermute | solution.py:124
  152.1 1.0 copy-start.5
  153.1 31.4 %copy-start.10 = (f32[512,768]{1,0:T(8,128)S(1)}, f32[512,768]{1,0:T(8,128)}, u32[]{:S(2)}) copy-start(f32[512,768]{1,0:T(8,128)} %get-tuple-element.54) | copy-start | bytes 4718596

commit v4 on v3

--- a/solution.py
+++ b/solution.py
@@ -237,8 +237,8 @@
     )(ids, q, k)
 
 
-def weight_grad_kernel(ids, left, *rest):
-    cots, outs = rest[:-2], rest[-2:]
+def weight_grad_kernel(ids, left, *rest, count):
+    cots, outs = rest[:-count], rest[-count:]
     half = len(cots) // 2
     for step, out in enumerate(outs):
 
@@ -253,7 +253,7 @@
 
 
 def weight_first_kernel(ids, probs_t, values, *rest):
-    cots, (left, *outs) = rest[:-3], rest[-3:]
+    cots, (left, out) = rest[:-2], rest[-2:]
     bands, heads, rows, _ = probs_t.shape
 
     @pl.when(pl.program_id(0) == 0)
@@ -264,27 +264,30 @@
                 own = values[:, :, ids[1] ^ r, :, lanes].reshape(rows, HD)
                 left[lanes, r * rows : (r + 1) * rows] = tn_dot(own, probs_t[r, head]).astype(jnp.bfloat16)
 
-    weight_grad_kernel(ids, left, *cots, *outs)
-
-
-def weight_parts(columns, cots, shards, steps, dtype):
+    weight_grad_kernel(ids, left, *cots, out, count=1)
+
+
+def weight_parts(columns, cots, shards, steps, dtypes):
     def place(i, ids):
-        return 0, 0, ids[0] ^ jnp.where(i == 0, steps[0], steps[1])
+        step = steps[0]
+        for at, other in enumerate(steps[1:], 1):
+            step = jnp.where(i == at, other, step)
+        return 0, 0, ids[0] ^ step
 
     specs = [pl.BlockSpec((*piece.shape[:2], piece.shape[2] // shards), place) for piece in cots]
     width = (cots[0].shape[2] + cots[-1].shape[2]) // shards
-    return specs, [jax.ShapeDtypeStruct((columns, width), dtype)] * 2
+    return specs, [jax.ShapeDtypeStruct((columns, width), dtype) for dtype in dtypes]
 
 
 def weight_first(ids, probs_t, values, cots):
     bands, _, rows, _ = probs_t.shape
     columns = values.shape[-1]
-    specs, sums = weight_parts(columns, cots, values.shape[0], (3, 1), jnp.bfloat16)
+    specs, sums = weight_parts(columns, cots, values.shape[0], (3,), (jnp.bfloat16,))
     out_shape = [jax.ShapeDtypeStruct((columns, bands * rows), jnp.bfloat16)] + sums
     return pl.pallas_call(
         weight_first_kernel,
         grid_spec=pltpu.PrefetchScalarGridSpec(
-            num_scalar_prefetch=1, grid=(2,), in_specs=whole(probs_t, values) + specs, out_specs=whole(*out_shape)
+            num_scalar_prefetch=1, grid=(1,), in_specs=whole(probs_t, values) + specs, out_specs=whole(*out_shape)
         ),
         out_shape=out_shape,
         compiler_params=params(),
@@ -293,11 +296,12 @@
 
 
 def weight_second(ids, left, cots, shards):
-    specs, sums = weight_parts(left.shape[0], cots, shards, (2, 0), jnp.float32)
+    dtypes = (jnp.float32, jnp.float32, jnp.bfloat16)
+    specs, sums = weight_parts(left.shape[0], cots, shards, (2, 0, 1), dtypes)
     return pl.pallas_call(
-        weight_grad_kernel,
+        functools.partial(weight_grad_kernel, count=3),
         grid_spec=pltpu.PrefetchScalarGridSpec(
-            num_scalar_prefetch=1, grid=(2,), in_specs=whole(left) + specs, out_specs=whole(*sums)
+            num_scalar_prefetch=1, grid=(3,), in_specs=whole(left) + specs, out_specs=whole(*sums)
         ),
         out_shape=sums,
         compiler_params=params(),
@@ -437,20 +441,25 @@
         picked = jnp.concatenate(picked, axis=2)
         picked = picked.reshape(local, seq_count, time_len, -1).transpose(1, 0, 2, 3)
         split.append(picked.reshape(seq_count * local, time_len, -1))
-    here = [trade(split[0]), None]
+    opening = split[0].reshape(seq_count, local, *split[0].shape[1:])
+    opening = [lax.dynamic_index_in_dim(opening, me ^ step, 0, keepdims=False) for step in range(seq_count)]
+    opening = [opening[0]] + [xor_send(opening[step], "seq", step) for step in range(1, seq_count)]
     q_space = after(q_space, split)
     mixed, probs = space_forward(q_space, k_space, v_space, seq_count, band_count, time_len)
     q_time = after(q_time, mixed)
     chances = time_probs(ids, q_time, k_time)
-    first, second, here[0], following, mixed = gate((first, second, here[0], split[1], mixed), chances)
-    here[1] = trade(following)
-    third = xor_send(second, "seq", 1)
+    first, second, opening, following, mixed = gate((first, second, opening, split[1], mixed), chances)
+    here = [jnp.zeros_like(split[0]), trade(following)]
+    for step in range(seq_count):
+        here[0] = lax.dynamic_update_slice_in_dim(here[0], opening[step], (me ^ step) * local, 0)
     other_near = swap_parts(jnp.concatenate([first, second], axis=0))
     across = [xor_send(here[0], "sub", 2), None]
     beside = [xor_send(here[0], "sub", 1), None]
 
-    here[1], third, other_near, across[0], mixed = gate((here[1], third, other_near, across[0], mixed), beside[0])
+    gated = gate((here[1], second, other_near, across[0], mixed), beside[0])
+    here[1], second, other_near, across[0], mixed = gated
     moved = trade(mixed)
+    third = xor_send(second, "seq", 1)
     across[1] = xor_send(here[1], "sub", 2)
     beside[1] = xor_send(here[1], "sub", 1)
     cross = [xor_send(across[0], "sub", 1), None]
@@ -462,10 +471,10 @@
         cots += [here[side], beside[side], across[side], cross[side]]
     weights = [out_weight, first, second, third, other_near, other_third]
 
-    turned, third_sum, first_sum = weight_first(ids, chances, moved, cots)
+    turned, third_sum = weight_first(ids, chances, moved, cots)
     back = space_grad(ids, after(chances, third_sum), weights, cots, seq_count)
     returned = trade(back)
-    second_sum, own_sum = weight_second(ids, after(turned, back), cots, seq_count)
+    second_sum, own_sum, first_sum = weight_second(ids, after(turned, back), cots, seq_count)
     third_sum = xor_send(third_sum, "seq", 1)
     paired = (second_sum + third_sum.astype(jnp.float32)).astype(jnp.bfloat16)
     far = xor_send(paired, "seq", 2)

time: 187 us -> 179 us (0.957)
  waiting for transfers between devices: 97 us -> 89.1 us
  local copies, waits for them, and re-layouts: 6.49 us -> 9.62 us
    all_to_all x4 -> x3, starting transfers between devices: 17.8 us -> 12.8 us  [trade(): return lax.all_to_all(value, 'seq', split_axis=0, concat_axis=0, tiled=True)]
    ppermute x12 -> x15, waiting for transfers between devices: 63.4 us -> 58.7 us  [xor_send(): return lax.ppermute(value, axis, [(i, i ^ distance) for i in range(count)])]
    ppermute x12 -> x15, starting transfers between devices: 9.72 us -> 13.3 us  [xor_send(): return lax.ppermute(value, axis, [(i, i ^ distance) for i in range(count)])]
    ppermute x2, waiting for transfers between devices: 9.99 us -> 6.73 us  [swap_parts(): return lax.ppermute(value, 'parts', [(0, 1), (1, 0)])]
    dynamic_update_slice x0 -> x4, local copies, waits for them, and re-layouts: none -> 2.78 us  [on_small_slice(): lax.dynamic_update_slice_in_dim(here[0], opening[step], (me ^ step) * loc...]
    pallas_call x1, Pallas kernels: 7.24 us -> 5.2 us  [weight_first(): pl.pallas_call(weight_first_kernel, grid_spec=pltpu.PrefetchScalarGridSpe...]
    all_to_all x4 -> x3, waiting for transfers between devices: 23.6 us -> 23.6 us  [trade(): return lax.all_to_all(value, 'seq', split_axis=0, concat_axis=0, tiled=True)]
  transfers between devices with their start and end apart: 18 -> 20, of which waited for: 9 -> 12; matrix products, arithmetic and copies ran while one was open for 3% -> 5% of each run, Pallas kernels for 21% -> 23%
where the time goes in v4:
time: 179 us; the launch traced here: 178 us
  waiting for transfers between devices  89.1 us (50%)
  Pallas kernels  45.6 us (25%)
  starting transfers between devices  29.2 us (16%)
  local copies, waits for them, and re-layouts  9.62 us (5%)
  other arithmetic  3.72 us (2%)
    ppermute x15, waiting for transfers between devices, xor_send(): return lax.ppermute(value, axis, [(i, i ^ distance) for i in range(count)])  58.7 us
    all_to_all x3, waiting for transfers between devices, trade(): return lax.all_to_all(value, 'seq', split_axis=0, concat_axis=0, tiled=True)  23.6 us
    ppermute x15, starting transfers between devices, xor_send(): return lax.ppermute(value, axis, [(i, i ^ distance) for i in range(count)])  13.3 us
    all_to_all x3, starting transfers between devices, trade(): return lax.all_to_all(value, 'seq', split_axis=0, concat_axis=0, tiled=True)  12.8 us
    pallas_call x1, Pallas kernels, space_grad(): pl.pallas_call(space_grad_kernel, grid_spec=pltpu.PrefetchScalarGridSpec(...  9.54 us
    pallas_call x1, Pallas kernels, space_backward(): pl.pallas_call(space_backward_kernel, grid=(frames, steps), in_specs=[wid...  8.93 us
    pallas_call x1, Pallas kernels, space_forward(): pl.pallas_call(space_forward_kernel, grid=(frames, steps), in_specs=[wide...  8.32 us
    pallas_call x1, Pallas kernels, weight_second(): pl.pallas_call(functools.partial(weight_grad_kernel, count=3), grid_spec=...  8.01 us
  transfers between devices with their start and end apart: 20, of which 12 were waited for; matrix products, arithmetic and copies ran while one was open for 5% of the time, Pallas kernels for 23%

profile of v4, /device:TPU:0, one launch (start us, length us, event | category | flops | bytes accessed | tf_op | source)
XLA Modules:
  0.0 178.1 jit_solution(3969708925231935)
XLA Ops:
  0.6 1.8 constant_dynamic-slice_fusion
  2.4 4.0 %collective-permute-start.1 = (bf16[256,768]{1,0:T(8,128)(2,1)}, bf16[256,768]{1,0:T(8,128)(2,1)S(1)}, u32[]{:S(2)}, u32[]{:S(2)}) collective-permute-start(bf16[256,768]{1,0:T(8,128)(2,1)} %constant_dynamic-slice_fusion), channel_id=1, source_target_pairs={{0,8},{4,12},{8,0},{12,4},{1,9},{5,13},{9,1},{13,5},{2,10},{6,14},... | collective-permute-start | bytes 1179656 | tf_op jit(solution)/shard_map/ppermute | solution.py:124
  6.4 1.6 collective-permute-start
  8.0 1.3 fusion
  9.3 0.1 pad_maximum_fusion.2
  9.4 0.7 dynamic-slice_bitcast_fusion
  10.1 1.9 %collective-permute-start.3 = (bf16[2,32,1024]{2,1,0:T(8,128)(2,1)}, bf16[2,32,1024]{2,1,0:T(8,128)(2,1)}, u32[]{:S(2)}, u32[]{:S(2)}) collective-permute-start(bf16[2,32,1024]{2,1,0:T(8,128)(2,1)} %get-tuple-element.75), channel_id=1, source_target_pairs={{0,8},{4,12},{8,0},{12,4},{1,9},{5,13},{9,1},{13,5},{2,10},{6,14},... | collective-permute-start | bytes 393224 | tf_op jit(solution)/shard_map/ppermute | solution.py:124
  12.0 2.5 %collective-permute-start.2 = (bf16[2,32,1024]{2,1,0:T(8,128)(2,1)}, bf16[2,32,1024]{2,1,0:T(8,128)(2,1)}, u32[]{:S(2)}, u32[]{:S(2)}) collective-permute-start(bf16[2,32,1024]{2,1,0:T(8,128)(2,1)} %get-tuple-element.76), channel_id=1, source_target_pairs={{0,4},{4,0},{8,12},{12,8},{1,5},{5,1},{9,13},{13,9},{2,6},{6,2},{1... | collective-permute-start | bytes 393224 | tf_op jit(solution)/shard_map/ppermute | solution.py:124
  14.5 0.1 fusion.1
  14.6 0.1 pad_maximum_fusion
  14.7 1.0 copy.11
  15.8 8.3 %space_forward.1 = (bf16[4,2,4,32,512]{4,3,2,1,0:T(8,128)(2,1)}, bf16[8,512,512]{2,1,0:T(8,128)(2,1)}) custom-call(bf16[2,512,512]{2,1,0:T(8,128)(2,1)} %q.2, bf16[2,512,512]{2,1,0:T(8,128)(2,1)} %k.5, bf16[2,512,512]{2,1,0:T(8,128)(2,1)} %v.3), custom_call_target="tpu_custom_call" | custom-call | tf_op jit(solution)/shard_map/space_forward/pallas_call | solution.py:188
  24.1 0.6 pad_add_fusion.ids
  24.7 5.6 %time_probs.1.probs_t.rest_8_ = bf16[4,4,256,256]{3,2,1,0:T(8,128)(2,1)} custom-call(s32[3]{0:T(128)} %pad_add_fusion.ids, bf16[8,4,32,512]{3,2,1,0:T(8,128)(2,1)} %q.1, bf16[8,4,32,512]{3,2,1,0:T(8,128)(2,1)} %k.4), custom_call_target="tpu_custom_call" | custom-call | tf_op jit(solution)/shard_map/time_probs/pallas_call | solution.py:225
  30.3 5.3 %collective-permute-done.3 = bf16[2,32,1024]{2,1,0:T(8,128)(2,1)} collective-permute-done((bf16[2,32,1024]{2,1,0:T(8,128)(2,1)}, bf16[2,32,1024]{2,1,0:T(8,128)(2,1)}, u32[]{:S(2)}, u32[]{:S(2)}) %collective-permute-start.3) | collective-permute-done | bytes 131104 | tf_op jit(solution)/shard_map/ppermute | solution.py:124
  35.6 4.8 %all-to-all-start = ((bf16[8,32,2048]{2,1,0:T(8,128)(2,1)}), bf16[8,32,2048]{2,1,0:T(8,128)(2,1)S(1)}, u32[]{:S(2)}, u32[]{:S(2)}) async-start(bf16[8,32,2048]{2,1,0:T(8,128)(2,1)} %bitcast.2), calls=%async_computation | async-start | bytes 2097152 | tf_op jit(solution)/shard_map/all_to_all | solution.py:128
  40.4 0.1 pad_maximum_fusion.1
  40.5 1.6 collective-permute-start.5
  42.2 0.9 constant_dynamic-update-slice_fusion.2
  43.1 0.9 constant_dynamic-update-slice_fusion.1
  44.0 0.9 constant_dynamic-update-slice_fusion.rest_0_
  44.9 0.1 collective-permute-start.7
  45.0 1.6 collective-permute-start.6
  46.6 0.3 collective-permute-done.7.rest_1_
  46.9 12.5 %collective-permute-done.6.rest_2_ = bf16[8,32,1024]{2,1,0:T(8,128)(2,1)} collective-permute-done((bf16[8,32,1024]{2,1,0:T(8,128)(2,1)S(1)}, bf16[8,32,1024]{2,1,0:T(8,128)(2,1)}, u32[]{:S(2)}, u32[]{:S(2)}) %collective-permute-start.6) | collective-permute-done | bytes 524320 | tf_op jit(solution)/shard_map/ppermute | solution.py:124
  59.5 0.3 collective-permute-done.5.other_near
  59.7 0.9 copy-done.10
  60.6 5.7 %all-to-all-done.rest_4_ = bf16[8,32,2048]{2,1,0:T(8,128)(2,1)S(1)} async-done(((bf16[8,32,2048]{2,1,0:T(8,128)(2,1)}), bf16[8,32,2048]{2,1,0:T(8,128)(2,1)S(1)}, u32[]{:S(2)}, u32[]{:S(2)}) %all-to-all-start) | async-done | bytes 1048608 | tf_op jit(solution)/shard_map/all_to_all | solution.py:128
  66.3 1.5 collective-permute-start.12
  67.8 4.3 %all-to-all-start.1 = ((bf16[4,2,4,32,512]{4,3,2,1,0:T(8,128)(2,1)}), bf16[4,2,4,32,512]{4,3,2,1,0:T(8,128)(2,1)}, u32[]{:S(2)}, u32[]{:S(2)}) async-start(bf16[4,2,4,32,512]{4,3,2,1,0:T(8,128)(2,1)} %get-tuple-element.52), calls=%async_computation.1 | async-start | bytes 2097152 | tf_op jit(solution)/shard_map/all_to_all | solution.py:128
  72.1 13.2 %collective-permute-done.8.third = bf16[256,768]{1,0:T(8,128)(2,1)} collective-permute-done((bf16[256,768]{1,0:T(8,128)(2,1)S(1)}, bf16[256,768]{1,0:T(8,128)(2,1)}, u32[]{:S(2)}, u32[]{:S(2)}) %collective-permute-start.8) | collective-permute-done | bytes 393248 | tf_op jit(solution)/shard_map/ppermute | solution.py:124
  85.3 1.5 collective-permute-start.9
  86.8 6.5 %collective-permute-done.9.other_third = bf16[256,768]{1,0:T(8,128)(2,1)S(1)} collective-permute-done((bf16[256,768]{1,0:T(8,128)(2,1)}, bf16[256,768]{1,0:T(8,128)(2,1)S(1)}, u32[]{:S(2)}, u32[]{:S(2)}) %collective-permute-start.9) | collective-permute-done | bytes 393248 | tf_op jit(solution)/shard_map/ppermute | solution.py:132
  93.3 0.1 collective-permute-start.13
  93.4 5.4 %all-to-all-done.1.values = bf16[4,2,4,32,512]{4,3,2,1,0:T(8,128)(2,1)} async-done(((bf16[4,2,4,32,512]{4,3,2,1,0:T(8,128)(2,1)}), bf16[4,2,4,32,512]{4,3,2,1,0:T(8,128)(2,1)}, u32[]{:S(2)}, u32[]{:S(2)}) %all-to-all-start.1) | async-done | bytes 1048608 | tf_op jit(solution)/shard_map/all_to_all | solution.py:128
  98.9 5.2 %weight_first.1 = (bf16[512,1024]{1,0:T(8,128)(2,1)}, bf16[512,768]{1,0:T(8,128)(2,1)}) custom-call(s32[3]{0:T(128)} %pad_add_fusion.ids, bf16[4,4,256,256]{3,2,1,0:T(8,128)(2,1)} %time_probs.1.probs_t.rest_8_, bf16[4,2,4,32,512]{4,3,2,1,0:T(8,128)(2,1)} %all-to-all-done.1.values, bf16[8,32,1024]{2,1,0:T(8,128)(2,1)} %copy-done.3, ...), custom_call_target="tpu_custom_call" | custom-call | tf_op jit(solution)/shard_map/weight_first/pallas_call | solution.py:287
  104.1 9.5 %space_grad.1 = bf16[4,2,4,32,512]{4,3,2,1,0:T(8,128)(2,1)} custom-call(s32[3]{0:T(128)} %pad_add_fusion.ids, bf16[512,768]{1,0:T(8,128)(2,1)} %own.1, bf16[256,768]{1,0:T(8,128)(2,1)} %copy-done.7, bf16[256,768]{1,0:T(8,128)(2,1)} %copy-done.6, bf16[256,768]{1,0:T(8,128)(2,1)} %collective-permute-done.8.third, bf16[512,768]{1,0:T(8,128)(2,1)} %copy-done.10, ...), custom_call_target="tpu_custom_call" | custom-call | tf_op jit(solution)/shard_map/space_grad/pallas_call | solution.py:370
  113.6 3.7 %all-to-all-start.2 = ((bf16[4,2,4,32,512]{4,3,2,1,0:T(8,128)(2,1)}), bf16[4,2,4,32,512]{4,3,2,1,0:T(8,128)(2,1)S(1)}, u32[]{:S(2)}, u32[]{:S(2)}) async-start(bf16[4,2,4,32,512]{4,3,2,1,0:T(8,128)(2,1)} %space_grad.1), calls=%async_computation.2 | async-start | bytes 2097152 | tf_op jit(solution)/shard_map/all_to_all | solution.py:128
  117.3 8.0 %weight_second.1 = (f32[512,768]{1,0:T(8,128)}, f32[512,768]{1,0:T(8,128)}, bf16[512,768]{1,0:T(8,128)(2,1)}) custom-call(s32[3]{0:T(128)} %pad_add_fusion.ids, bf16[512,1024]{1,0:T(8,128)(2,1)} %get-tuple-element.59.left, bf16[8,32,1024]{2,1,0:T(8,128)(2,1)} %copy-done.3, bf16[8,32,1024]{2,1,0:T(8,128)(2,1)} %copy-done.4, ...), custom_call_target="tpu_custom_call" | custom-call | tf_op jit(solution)/shard_map/weight_second/pallas_call | solution.py:301
  125.3 5.0 %collective-permute-done.14 = bf16[512,768]{1,0:T(8,128)(2,1)S(1)} collective-permute-done((bf16[512,768]{1,0:T(8,128)(2,1)}, bf16[512,768]{1,0:T(8,128)(2,1)S(1)}, u32[]{:S(2)}, u32[]{:S(2)}) %collective-permute-start.14) | collective-permute-done | bytes 786464 | tf_op jit(solution)/shard_map/ppermute | solution.py:124
  130.3 1.6 add_convert_fusion
  131.9 0.1 collective-permute-start.15
  132.0 12.5 %all-to-all-done.2.piece = bf16[4,2,4,32,512]{4,3,2,1,0:T(8,128)(2,1)S(1)} async-done(((bf16[4,2,4,32,512]{4,3,2,1,0:T(8,128)(2,1)}), bf16[4,2,4,32,512]{4,3,2,1,0:T(8,128)(2,1)S(1)}, u32[]{:S(2)}, u32[]{:S(2)}) %all-to-all-start.2) | async-done | bytes 1048608 | tf_op jit(solution)/shard_map/all_to_all | solution.py:128
  144.5 1.0 copy-done.5
  145.4 8.9 %space_backward.1 = (bf16[2,512,512]{2,1,0:T(8,128)(2,1)}, bf16[2,512,512]{2,1,0:T(8,128)(2,1)}, bf16[2,512,512]{2,1,0:T(8,128)(2,1)}) custom-call(bf16[2,512,512]{2,1,0:T(8,128)(2,1)} %q.2, bf16[2,512,512]{2,1,0:T(8,128)(2,1)} %k.5, bf16[2,512,512]{2,1,0:T(8,128)(2,1)} %v.3, bf16[8,512,512]{2,1,0:T(8,128)(2,1)} %get-tuple-element.36.probs, ...), custom_call_target="tpu_custom_call" | custom-call | tf_op jit(solution)/shard_map/space_backward/pallas_call | solution.py:413
  154.4 17.3 %collective-permute-done.16 = bf16[512,768]{1,0:T(8,128)(2,1)S(1)} collective-permute-done((bf16[512,768]{1,0:T(8,128)(2,1)}, bf16[512,768]{1,0:T(8,128)(2,1)S(1)}, u32[]{:S(2)}, u32[]{:S(2)}) %collective-permute-start.16) | collective-permute-done | bytes 786464 | tf_op jit(solution)/shard_map/ppermute | solution.py:124
  171.6 5.1 %collective-permute-done.15 = bf16[512,768]{1,0:T(8,128)(2,1)S(1)} collective-permute-done((bf16[512,768]{1,0:T(8,128)(2,1)S(1)}, bf16[512,768]{1,0:T(8,128)(2,1)S(1)}, u32[]{:S(2)}, u32[]{:S(2)}) %collective-permute-start.15) | collective-permute-done | bytes 786464 | tf_op jit(solution)/shard_map/ppermute | solution.py:124
  176.7 1.3 convert_add_fusion
  (38 shorter events, 0.1 us)
Async XLA Ops:
  2.4 33.2 %collective-permute-start.1 = (bf16[256,768]{1,0:T(8,128)(2,1)}, bf16[256,768]{1,0:T(8,128)(2,1)S(1)}, u32[]{:S(2)}, u32[]{:S(2)}) collective-permute-start(bf16[256,768]{1,0:T(8,128)(2,1)} %constant_dynamic-slice_fusion), channel_id=1, source_target_pairs={{0,8},{4,12},{8,0},{12,4},{1,9},{5,13},{9,1},{13,5},{2,10},{6,14},... | collective-permute-start | bytes 1179656 | tf_op jit(solution)/shard_map/ppermute | solution.py:124
  6.4 29.2 %collective-permute-start = (bf16[256,768]{1,0:T(8,128)(2,1)}, bf16[256,768]{1,0:T(8,128)(2,1)S(1)}, u32[]{:S(2)}, u32[]{:S(2)}) collective-permute-start(bf16[256,768]{1,0:T(8,128)(2,1)} %constant_dynamic-slice_fusion), channel_id=1, source_target_pairs={{0,4},{4,0},{8,12},{12,8},{1,5},{5,1},{9,13},{13,9},{2,6},{6,2},{1... | collective-permute-start | bytes 1179656 | tf_op jit(solution)/shard_map/ppermute | solution.py:124
  8.0 6.5 %copy-start.8 = (bf16[2,128,3072]{2,1,0:T(8,128)(2,1)S(1)}, bf16[2,128,3072]{2,1,0:T(8,128)(2,1)}, u32[]{:S(2)}) copy-start(bf16[2,128,3072]{2,1,0:T(8,128)(2,1)} %param.13) | copy-start | bytes 4718596
  10.1 20.2 %collective-permute-start.4 = (bf16[2,32,1024]{2,1,0:T(8,128)(2,1)}, bf16[2,32,1024]{2,1,0:T(8,128)(2,1)}, u32[]{:S(2)}, u32[]{:S(2)}) collective-permute-start(bf16[2,32,1024]{2,1,0:T(8,128)(2,1)} %get-tuple-element.74), channel_id=1, source_target_pairs={{0,12},{4,8},{8,4},{12,0},{1,13},{5,9},{9,5},{13,1},{2,14},{6,10},... | collective-permute-start | bytes 393224 | tf_op jit(solution)/shard_map/ppermute | solution.py:124
  10.1 25.5 %collective-permute-start.3 = (bf16[2,32,1024]{2,1,0:T(8,128)(2,1)}, bf16[2,32,1024]{2,1,0:T(8,128)(2,1)}, u32[]{:S(2)}, u32[]{:S(2)}) collective-permute-start(bf16[2,32,1024]{2,1,0:T(8,128)(2,1)} %get-tuple-element.75), channel_id=1, source_target_pairs={{0,8},{4,12},{8,0},{12,4},{1,9},{5,13},{9,1},{13,5},{2,10},{6,14},... | collective-permute-start | bytes 393224 | tf_op jit(solution)/shard_map/ppermute | solution.py:124
  12.0 23.6 %collective-permute-start.2 = (bf16[2,32,1024]{2,1,0:T(8,128)(2,1)}, bf16[2,32,1024]{2,1,0:T(8,128)(2,1)}, u32[]{:S(2)}, u32[]{:S(2)}) collective-permute-start(bf16[2,32,1024]{2,1,0:T(8,128)(2,1)} %get-tuple-element.76), channel_id=1, source_target_pairs={{0,4},{4,0},{8,12},{12,8},{1,5},{5,1},{9,13},{13,9},{2,6},{6,2},{1... | collective-permute-start | bytes 393224 | tf_op jit(solution)/shard_map/ppermute | solution.py:124
  35.6 32.2 %copy-start.6 = (bf16[256,768]{1,0:T(8,128)(2,1)}, bf16[256,768]{1,0:T(8,128)(2,1)S(1)}, u32[]{:S(2)}) copy-start(bf16[256,768]{1,0:T(8,128)(2,1)S(1)} %collective-permute-done.1.second) | copy-start | bytes 1179652
  35.6 4.9 %copy-start.7 = (bf16[256,768]{1,0:T(8,128)(2,1)}, bf16[256,768]{1,0:T(8,128)(2,1)S(1)}, u32[]{:S(2)}) copy-start(bf16[256,768]{1,0:T(8,128)(2,1)S(1)} %collective-permute-done.first) | copy-start | bytes 1179652
  35.6 30.7 %all-to-all-start = ((bf16[8,32,2048]{2,1,0:T(8,128)(2,1)}), bf16[8,32,2048]{2,1,0:T(8,128)(2,1)S(1)}, u32[]{:S(2)}, u32[]{:S(2)}) async-start(bf16[8,32,2048]{2,1,0:T(8,128)(2,1)} %bitcast.2), calls=%async_computation | async-start | bytes 2097152 | tf_op jit(solution)/shard_map/all_to_all | solution.py:128
  40.5 19.2 %collective-permute-start.5 = (bf16[512,768]{1,0:T(8,128)(2,1)S(1)}, bf16[512,768]{1,0:T(8,128)(2,1)S(1)}, u32[]{:S(2)}, u32[]{:S(2)}) collective-permute-start(bf16[512,768]{1,0:T(8,128)(2,1)S(1)} %pad_maximum_fusion.1), channel_id=1, source_target_pairs={{0,16},{16,0},{1,17},{17,1},{2,18},{18,2},{3,19},{19,3},{4,20},{20... | collective-permute-start | bytes 2359304 | tf_op jit(solution)/shard_map/ppermute | solution.py:132
  44.9 14.5 %copy-start.3 = (bf16[8,32,1024]{2,1,0:T(8,128)(2,1)}, bf16[8,32,1024]{2,1,0:T(8,128)(2,1)S(1)}, u32[]{:S(2)}) copy-start(bf16[8,32,1024]{2,1,0:T(8,128)(2,1)S(1)} %constant_dynamic-update-slice_fusion.rest_0_) | copy-start | bytes 1572868
  44.9 2.0 %collective-permute-start.7 = (bf16[8,32,1024]{2,1,0:T(8,128)(2,1)S(1)}, bf16[8,32,1024]{2,1,0:T(8,128)(2,1)S(1)}, u32[]{:S(2)}, u32[]{:S(2)}) collective-permute-start(bf16[8,32,1024]{2,1,0:T(8,128)(2,1)S(1)} %constant_dynamic-update-slice_fusion.rest_0_), channel_id=1, source_target_pairs={{0,1},{1,0},{2,3},{3,2},{4,5},{5,4},{6,7},{7,6},{8,9},{9,8},{10,11... | collective-permute-start | bytes 1572872 | tf_op jit(solution)/shard_map/ppermute | solution.py:124
  45.0 14.4 %collective-permute-start.6 = (bf16[8,32,1024]{2,1,0:T(8,128)(2,1)S(1)}, bf16[8,32,1024]{2,1,0:T(8,128)(2,1)}, u32[]{:S(2)}, u32[]{:S(2)}) collective-permute-start(bf16[8,32,1024]{2,1,0:T(8,128)(2,1)S(1)} %constant_dynamic-update-slice_fusion.rest_0_), channel_id=1, source_target_pairs={{0,2},{1,3},{2,0},{3,1},{4,6},{5,7},{6,4},{7,5},{8,10},{9,11},{10,... | collective-permute-start | bytes 1572872 | tf_op jit(solution)/shard_map/ppermute | solution.py:124
  46.9 12.6 %copy-start.4 = (bf16[8,32,1024]{2,1,0:T(8,128)(2,1)}, bf16[8,32,1024]{2,1,0:T(8,128)(2,1)S(1)}, u32[]{:S(2)}) copy-start(bf16[8,32,1024]{2,1,0:T(8,128)(2,1)S(1)} %collective-permute-done.7.rest_1_) | copy-start | bytes 1572868
  59.7 0.9 copy-start.10
  66.3 32.5 %copy-start = (bf16[8,32,2048]{2,1,0:T(8,128)(2,1)}, bf16[8,32,2048]{2,1,0:T(8,128)(2,1)S(1)}, u32[]{:S(2)}) copy-start(bf16[8,32,2048]{2,1,0:T(8,128)(2,1)S(1)} %all-to-all-done.rest_4_) | copy-start | bytes 3145732
  66.3 27.0 %collective-permute-start.12 = (bf16[8,32,2048]{2,1,0:T(8,128)(2,1)S(1)}, bf16[8,32,2048]{2,1,0:T(8,128)(2,1)S(1)}, u32[]{:S(2)}, u32[]{:S(2)}) collective-permute-start(bf16[8,32,2048]{2,1,0:T(8,128)(2,1)S(1)} %all-to-all-done.rest_4_), channel_id=1, source_target_pairs={{0,2},{1,3},{2,0},{3,1},{4,6},{5,7},{6,4},{7,5},{8,10},{9,11},{10,... | collective-permute-start | bytes 3145736 | tf_op jit(solution)/shard_map/ppermute | solution.py:124
  67.8 17.5 %collective-permute-start.8 = (bf16[256,768]{1,0:T(8,128)(2,1)S(1)}, bf16[256,768]{1,0:T(8,128)(2,1)}, u32[]{:S(2)}, u32[]{:S(2)}) collective-permute-start(bf16[256,768]{1,0:T(8,128)(2,1)S(1)} %collective-permute-done.1.second), channel_id=1, source_target_pairs={{0,4},{4,0},{8,12},{12,8},{1,5},{5,1},{9,13},{13,9},{2,6},{6,2},{1... | collective-permute-start | bytes 1179656 | tf_op jit(solution)/shard_map/ppermute | solution.py:124
  67.8 19.0 %collective-permute-start.10 = (bf16[8,32,1024]{2,1,0:T(8,128)(2,1)}, bf16[8,32,1024]{2,1,0:T(8,128)(2,1)}, u32[]{:S(2)}, u32[]{:S(2)}) collective-permute-start(bf16[8,32,1024]{2,1,0:T(8,128)(2,1)} %collective-permute-done.6.rest_2_), channel_id=1, source_target_pairs={{0,1},{1,0},{2,3},{3,2},{4,5},{5,4},{6,7},{7,6},{8,9},{9,8},{10,11... | collective-permute-start | bytes 1572872 | tf_op jit(solution)/shard_map/ppermute | solution.py:124
  67.8 31.0 %all-to-all-start.1 = ((bf16[4,2,4,32,512]{4,3,2,1,0:T(8,128)(2,1)}), bf16[4,2,4,32,512]{4,3,2,1,0:T(8,128)(2,1)}, u32[]{:S(2)}, u32[]{:S(2)}) async-start(bf16[4,2,4,32,512]{4,3,2,1,0:T(8,128)(2,1)} %get-tuple-element.52), calls=%async_computation.1 | async-start | bytes 2097152 | tf_op jit(solution)/shard_map/all_to_all | solution.py:128
  85.3 8.0 %collective-permute-start.9 = (bf16[256,768]{1,0:T(8,128)(2,1)}, bf16[256,768]{1,0:T(8,128)(2,1)S(1)}, u32[]{:S(2)}, u32[]{:S(2)}) collective-permute-start(bf16[256,768]{1,0:T(8,128)(2,1)} %collective-permute-done.8.third), channel_id=1, source_target_pairs={{0,16},{16,0},{1,17},{17,1},{2,18},{18,2},{3,19},{19,3},{4,20},{20... | collective-permute-start | bytes 1179656 | tf_op jit(solution)/shard_map/ppermute | solution.py:132
  86.8 6.6 %collective-permute-start.11 = (bf16[8,32,2048]{2,1,0:T(8,128)(2,1)S(1)}, bf16[8,32,2048]{2,1,0:T(8,128)(2,1)S(1)}, u32[]{:S(2)}, u32[]{:S(2)}) collective-permute-start(bf16[8,32,2048]{2,1,0:T(8,128)(2,1)S(1)} %all-to-all-done.rest_4_), channel_id=1, source_target_pairs={{0,1},{1,0},{2,3},{3,2},{4,5},{5,4},{6,7},{7,6},{8,9},{9,8},{10,11... | collective-permute-start | bytes 3145736 | tf_op jit(solution)/shard_map/ppermute | solution.py:124
  93.3 10.8 %copy-start.11 = (bf16[256,768]{1,0:T(8,128)(2,1)}, bf16[256,768]{1,0:T(8,128)(2,1)S(1)}, u32[]{:S(2)}) copy-start(bf16[256,768]{1,0:T(8,128)(2,1)S(1)} %collective-permute-done.9.other_third) | copy-start | bytes 1179652
  93.3 5.5 %copy-start.1 = (bf16[8,32,2048]{2,1,0:T(8,128)(2,1)}, bf16[8,32,2048]{2,1,0:T(8,128)(2,1)S(1)}, u32[]{:S(2)}) copy-start(bf16[8,32,2048]{2,1,0:T(8,128)(2,1)S(1)} %collective-permute-done.12.rest_6_) | copy-start | bytes 3145732
  93.3 5.5 %collective-permute-start.13 = (bf16[8,32,2048]{2,1,0:T(8,128)(2,1)S(1)}, bf16[8,32,2048]{2,1,0:T(8,128)(2,1)}, u32[]{:S(2)}, u32[]{:S(2)}) collective-permute-start(bf16[8,32,2048]{2,1,0:T(8,128)(2,1)S(1)} %collective-permute-done.12.rest_6_), channel_id=1, source_target_pairs={{0,1},{1,0},{2,3},{3,2},{4,5},{5,4},{6,7},{7,6},{8,9},{9,8},{10,11... | collective-permute-start | bytes 3145736 | tf_op jit(solution)/shard_map/ppermute | solution.py:124
  93.4 5.4 %copy-start.2 = (bf16[8,32,2048]{2,1,0:T(8,128)(2,1)}, bf16[8,32,2048]{2,1,0:T(8,128)(2,1)S(1)}, u32[]{:S(2)}) copy-start(bf16[8,32,2048]{2,1,0:T(8,128)(2,1)S(1)} %collective-permute-done.11.rest_5_) | copy-start | bytes 3145732
  104.1 26.3 %collective-permute-start.14 = (bf16[512,768]{1,0:T(8,128)(2,1)}, bf16[512,768]{1,0:T(8,128)(2,1)S(1)}, u32[]{:S(2)}, u32[]{:S(2)}) collective-permute-start(bf16[512,768]{1,0:T(8,128)(2,1)} %get-tuple-element.53), channel_id=1, source_target_pairs={{0,4},{4,0},{8,12},{12,8},{1,5},{5,1},{9,13},{13,9},{2,6},{6,2},{1... | collective-permute-start | bytes 2359304 | tf_op jit(solution)/shard_map/ppermute | solution.py:124
  113.6 30.8 %all-to-all-start.2 = ((bf16[4,2,4,32,512]{4,3,2,1,0:T(8,128)(2,1)}), bf16[4,2,4,32,512]{4,3,2,1,0:T(8,128)(2,1)S(1)}, u32[]{:S(2)}, u32[]{:S(2)}) async-start(bf16[4,2,4,32,512]{4,3,2,1,0:T(8,128)(2,1)} %space_grad.1), calls=%async_computation.2 | async-start | bytes 2097152 | tf_op jit(solution)/shard_map/all_to_all | solution.py:128
  130.3 41.3 %collective-permute-start.16 = (bf16[512,768]{1,0:T(8,128)(2,1)}, bf16[512,768]{1,0:T(8,128)(2,1)S(1)}, u32[]{:S(2)}, u32[]{:S(2)}) collective-permute-start(bf16[512,768]{1,0:T(8,128)(2,1)} %get-tuple-element.63), channel_id=1, source_target_pairs={{0,4},{4,0},{8,12},{12,8},{1,5},{5,1},{9,13},{13,9},{2,6},{6,2},{1... | collective-permute-start | bytes 2359304 | tf_op jit(solution)/shard_map/ppermute | solution.py:124
  131.9 44.9 %collective-permute-start.15 = (bf16[512,768]{1,0:T(8,128)(2,1)S(1)}, bf16[512,768]{1,0:T(8,128)(2,1)S(1)}, u32[]{:S(2)}, u32[]{:S(2)}) collective-permute-start(bf16[512,768]{1,0:T(8,128)(2,1)S(1)} %add_convert_fusion), channel_id=1, source_target_pairs={{0,8},{4,12},{8,0},{12,4},{1,9},{5,13},{9,1},{13,5},{2,10},{6,14},... | collective-permute-start | bytes 2359304 | tf_op jit(solution)/shard_map/ppermute | solution.py:124
  144.5 1.0 copy-start.5
  145.4 31.3 %copy-start.9 = (f32[512,768]{1,0:T(8,128)S(1)}, f32[512,768]{1,0:T(8,128)}, u32[]{:S(2)}) copy-start(f32[512,768]{1,0:T(8,128)} %get-tuple-element.60) | copy-start | bytes 4718596

commit v5 on v4

--- a/solution.py
+++ b/solution.py
@@ -237,6 +237,27 @@
     )(ids, q, k)
 
 
+def in_order_kernel(ids, *rest):
+    pieces, out = rest[:-1], rest[-1]
+    local = pieces[0].shape[0]
+    for step, piece in enumerate(pieces):
+        out[pl.ds((ids[0] ^ step) * local, local)] = piece[...]
+
+
+def in_order(ids, pieces):
+    local, *inner = pieces[0].shape
+    out_shape = jax.ShapeDtypeStruct((len(pieces) * local, *inner), pieces[0].dtype)
+    return pl.pallas_call(
+        in_order_kernel,
+        grid_spec=pltpu.PrefetchScalarGridSpec(
+            num_scalar_prefetch=1, grid=(1,), in_specs=whole(*pieces), out_specs=whole(out_shape)[0]
+        ),
+        out_shape=out_shape,
+        compiler_params=params(),
+        name="in_order",
+    )(ids, *pieces)
+
+
 def weight_grad_kernel(ids, left, *rest, count):
     cots, outs = rest[:-count], rest[-count:]
     half = len(cots) // 2
@@ -449,17 +470,18 @@
     q_time = after(q_time, mixed)
     chances = time_probs(ids, q_time, k_time)
     first, second, opening, following, mixed = gate((first, second, opening, split[1], mixed), chances)
-    here = [jnp.zeros_like(split[0]), trade(following)]
-    for step in range(seq_count):
-        here[0] = lax.dynamic_update_slice_in_dim(here[0], opening[step], (me ^ step) * local, 0)
+    here = [in_order(ids, opening), trade(following)]
+    quarter = rows // 4
+    third = [xor_send(second[:quarter], "seq", 1), None]
     other_near = swap_parts(jnp.concatenate([first, second], axis=0))
     across = [xor_send(here[0], "sub", 2), None]
     beside = [xor_send(here[0], "sub", 1), None]
 
-    gated = gate((here[1], second, other_near, across[0], mixed), beside[0])
-    here[1], second, other_near, across[0], mixed = gated
+    gated = gate((here[1], second, third[0], other_near, across[0], mixed), beside[0])
+    here[1], second, third[0], other_near, across[0], mixed = gated
     moved = trade(mixed)
-    third = xor_send(second, "seq", 1)
+    third[1] = xor_send(second[quarter:], "seq", 1)
+    third = jnp.concatenate(third, axis=0)
     across[1] = xor_send(here[1], "sub", 2)
     beside[1] = xor_send(here[1], "sub", 1)
     cross = [xor_send(across[0], "sub", 1), None]

time: 179 us -> 177 us (0.989)
  waiting for transfers between devices: 89.1 us -> 83.7 us
  Pallas kernels: 45.6 us -> 48.2 us
  starting transfers between devices: 29.2 us -> 31.5 us
  local copies, waits for them, and re-layouts: 9.62 us -> 7.77 us
    ppermute x15 -> x16, waiting for transfers between devices: 58.7 us -> 54.1 us  [xor_send(): return lax.ppermute(value, axis, [(i, i ^ distance) for i in range(count)])]
    all_to_all x3, waiting for transfers between devices: 23.6 us -> 20.6 us  [trade(): return lax.all_to_all(value, 'seq', split_axis=0, concat_axis=0, tiled=True)]
    dynamic_update_slice x4 -> x0, local copies, waits for them, and re-layouts: 2.78 us -> none  [on_small_slice(): lax.dynamic_update_slice_in_dim(here[0], opening[step], (me ^ step) * loc...]
    pallas_call x0 -> x1, Pallas kernels: none -> 2.61 us  [in_order(): pl.pallas_call(in_order_kernel, grid_spec=pltpu.PrefetchScalarGridSpec(nu...]
    ppermute x2, waiting for transfers between devices: 6.73 us -> 8.99 us  [swap_parts(): return lax.ppermute(value, 'parts', [(0, 1), (1, 0)])]
    ppermute x15 -> x16, starting transfers between devices: 13.3 us -> 15.2 us  [xor_send(): return lax.ppermute(value, axis, [(i, i ^ distance) for i in range(count)])]
  transfers between devices with their start and end apart: 20 -> 21, of which waited for: 12 -> 11; matrix products, arithmetic and copies ran while one was open for 5% -> 3% of each run, Pallas kernels for 23% -> 24%
where the time goes in v5:
time: 177 us; the launch traced here: 176 us
  waiting for transfers between devices  83.7 us (47%)
  Pallas kernels  48.2 us (27%)
  starting transfers between devices  31.5 us (18%)
  local copies, waits for them, and re-layouts  7.77 us (4%)
  other arithmetic  3.75 us (2%)
    ppermute x16, waiting for transfers between devices, xor_send(): return lax.ppermute(value, axis, [(i, i ^ distance) for i in range(count)])  54.1 us
    all_to_all x3, waiting for transfers between devices, trade(): return lax.all_to_all(value, 'seq', split_axis=0, concat_axis=0, tiled=True)  20.6 us
    ppermute x16, starting transfers between devices, xor_send(): return lax.ppermute(value, axis, [(i, i ^ distance) for i in range(count)])  15.2 us
    all_to_all x3, starting transfers between devices, trade(): return lax.all_to_all(value, 'seq', split_axis=0, concat_axis=0, tiled=True)  13.1 us
    pallas_call x1, Pallas kernels, space_grad(): pl.pallas_call(space_grad_kernel, grid_spec=pltpu.PrefetchScalarGridSpec(...  9.54 us
    ppermute x2, waiting for transfers between devices, swap_parts(): return lax.ppermute(value, 'parts', [(0, 1), (1, 0)])  8.99 us
    pallas_call x1, Pallas kernels, space_backward(): pl.pallas_call(space_backward_kernel, grid=(frames, steps), in_specs=[wid...  8.93 us
    pallas_call x1, Pallas kernels, space_forward(): pl.pallas_call(space_forward_kernel, grid=(frames, steps), in_specs=[wide...  8.3 us
  transfers between devices with their start and end apart: 21, of which 11 were waited for; matrix products, arithmetic and copies ran while one was open for 3% of the time, Pallas kernels for 24%

profile of v5, /device:TPU:0, one launch (start us, length us, event | category | flops | bytes accessed | tf_op | source)
XLA Modules:
  0.0 175.8 jit_solution(4040992515393145215)
XLA Ops:
  0.6 1.8 %constant_dynamic-slice_fusion = bf16[256,768]{1,0:T(8,128)(2,1)} fusion(bf16[512,768]{1,0:T(8,128)(2,1)} %own.1, s32[]{:T(128)S(6)} %select_n.16), kind=kLoop, calls=%fused_computation.11 | loop fusion | bytes 786436 | tf_op jit(solution)/shard_map/dynamic_slice | solution.py:453
  2.4 4.0 %collective-permute-start.1 = (bf16[256,768]{1,0:T(8,128)(2,1)}, bf16[256,768]{1,0:T(8,128)(2,1)S(1)}, u32[]{:S(2)}, u32[]{:S(2)}) collective-permute-start(bf16[256,768]{1,0:T(8,128)(2,1)} %constant_dynamic-slice_fusion), channel_id=1, source_target_pairs={{0,8},{4,12},{8,0},{12,4},{1,9},{5,13},{9,1},{13,5},{2,10},{6,14},... | collective-permute-start | bytes 1179656 | tf_op jit(solution)/shard_map/ppermute | solution.py:124
  6.4 1.6 collective-permute-start
  8.0 1.3 fusion
  9.3 0.1 pad_maximum_fusion.2
  9.4 0.8 dynamic-slice_bitcast_fusion
  10.2 1.9 %collective-permute-start.3 = (bf16[2,32,1024]{2,1,0:T(8,128)(2,1)}, bf16[2,32,1024]{2,1,0:T(8,128)(2,1)}, u32[]{:S(2)}, u32[]{:S(2)}) collective-permute-start(bf16[2,32,1024]{2,1,0:T(8,128)(2,1)} %get-tuple-element.77), channel_id=1, source_target_pairs={{0,8},{4,12},{8,0},{12,4},{1,9},{5,13},{9,1},{13,5},{2,10},{6,14},... | collective-permute-start | bytes 393224 | tf_op jit(solution)/shard_map/ppermute | solution.py:124
  12.1 2.5 %collective-permute-start.2 = (bf16[2,32,1024]{2,1,0:T(8,128)(2,1)}, bf16[2,32,1024]{2,1,0:T(8,128)(2,1)}, u32[]{:S(2)}, u32[]{:S(2)}) collective-permute-start(bf16[2,32,1024]{2,1,0:T(8,128)(2,1)} %get-tuple-element.78), channel_id=1, source_target_pairs={{0,4},{4,0},{8,12},{12,8},{1,5},{5,1},{9,13},{13,9},{2,6},{6,2},{1... | collective-permute-start | bytes 393224 | tf_op jit(solution)/shard_map/ppermute | solution.py:124
  14.6 0.1 fusion.1
  14.7 0.1 pad_maximum_fusion
  14.8 1.0 copy.11
  15.8 8.3 %space_forward.1 = (bf16[4,2,4,32,512]{4,3,2,1,0:T(8,128)(2,1)}, bf16[8,512,512]{2,1,0:T(8,128)(2,1)}) custom-call(bf16[2,512,512]{2,1,0:T(8,128)(2,1)} %q.2, bf16[2,512,512]{2,1,0:T(8,128)(2,1)} %k.5, bf16[2,512,512]{2,1,0:T(8,128)(2,1)} %v.3), custom_call_target="tpu_custom_call" | custom-call | tf_op jit(solution)/shard_map/space_forward/pallas_call | solution.py:188
  24.1 0.6 pad_add_fusion.ids
  24.7 5.6 %time_probs.1.probs_t.rest_8_ = bf16[4,4,256,256]{3,2,1,0:T(8,128)(2,1)} custom-call(s32[3]{0:T(128)} %pad_add_fusion.ids, bf16[8,4,32,512]{3,2,1,0:T(8,128)(2,1)} %q.1, bf16[8,4,32,512]{3,2,1,0:T(8,128)(2,1)} %k.4), custom_call_target="tpu_custom_call" | custom-call | tf_op jit(solution)/shard_map/time_probs/pallas_call | solution.py:225
  30.3 5.2 %collective-permute-done.3.rest_2_ = bf16[2,32,1024]{2,1,0:T(8,128)(2,1)} collective-permute-done((bf16[2,32,1024]{2,1,0:T(8,128)(2,1)}, bf16[2,32,1024]{2,1,0:T(8,128)(2,1)}, u32[]{:S(2)}, u32[]{:S(2)}) %collective-permute-start.3) | collective-permute-done | bytes 131104 | tf_op jit(solution)/shard_map/ppermute | solution.py:124
  35.6 0.0 collective-permute-done.2.rest_1_
  35.6 4.8 %all-to-all-start = ((bf16[8,32,2048]{2,1,0:T(8,128)(2,1)}), bf16[8,32,2048]{2,1,0:T(8,128)(2,1)S(1)}, u32[]{:S(2)}, u32[]{:S(2)}) async-start(bf16[8,32,2048]{2,1,0:T(8,128)(2,1)} %bitcast.2), calls=%async_computation | async-start | bytes 2097152 | tf_op jit(solution)/shard_map/all_to_all | solution.py:128
  40.4 0.1 pad_maximum_fusion.1
  40.5 1.6 collective-permute-start.6
  42.1 2.6 %in_order.1.rest_0_ = bf16[8,32,1024]{2,1,0:T(8,128)(2,1)} custom-call(s32[3]{0:T(128)} %pad_add_fusion.ids, bf16[2,32,1024]{2,1,0:T(8,128)(2,1)} %get-tuple-element.43.rest_0_, bf16[2,32,1024]{2,1,0:T(8,128)(2,1)} %collective-permute-done.2.rest_1_, bf16[2,32,1024]{2,1,0:T(8,128)(2,1)} %collective-permute-done.3.rest_2_, bf16[2,32,1024]{2,1,0:T(8,128)(2,1)} %copy-done.15), custom_call_target="tpu_custom_call" | custom-call | tf_op jit(solution)/shard_map/in_order/pallas_call | solution.py:250
  44.7 1.5 collective-permute-start.7
  46.2 2.1 %collective-permute-start.5 = (bf16[128,768]{1,0:T(8,128)(2,1)S(1)}, bf16[128,768]{1,0:T(8,128)(2,1)S(1)}, u32[]{:S(2)}, u32[]{:S(2)}) collective-permute-start(bf16[128,768]{1,0:T(8,128)(2,1)S(1)} %slice.38), channel_id=1, source_target_pairs={{0,4},{4,0},{8,12},{12,8},{1,5},{5,1},{9,13},{13,9},{2,6},{6,2},{1... | collective-permute-start | bytes 589832 | tf_op jit(solution)/shard_map/ppermute | solution.py:124
  48.3 13.6 %collective-permute-done.5 = bf16[128,768]{1,0:T(8,128)(2,1)S(1)} collective-permute-done((bf16[128,768]{1,0:T(8,128)(2,1)S(1)}, bf16[128,768]{1,0:T(8,128)(2,1)S(1)}, u32[]{:S(2)}, u32[]{:S(2)}) %collective-permute-start.5) | collective-permute-done | bytes 196640 | tf_op jit(solution)/shard_map/ppermute | solution.py:124
  61.9 0.8 copy-done.3
  62.8 0.9 copy-done.11
  63.6 2.7 %all-to-all-done.rest_4_ = bf16[8,32,2048]{2,1,0:T(8,128)(2,1)S(1)} async-done(((bf16[8,32,2048]{2,1,0:T(8,128)(2,1)}), bf16[8,32,2048]{2,1,0:T(8,128)(2,1)S(1)}, u32[]{:S(2)}, u32[]{:S(2)}) %all-to-all-start) | async-done | bytes 1048608 | tf_op jit(solution)/shard_map/all_to_all | solution.py:128
  66.3 1.5 collective-permute-start.13
  67.9 0.1 collective-permute-start.9
  67.9 4.6 %all-to-all-start.1 = ((bf16[4,2,4,32,512]{4,3,2,1,0:T(8,128)(2,1)}), bf16[4,2,4,32,512]{4,3,2,1,0:T(8,128)(2,1)}, u32[]{:S(2)}, u32[]{:S(2)}) async-start(bf16[4,2,4,32,512]{4,3,2,1,0:T(8,128)(2,1)} %get-tuple-element.54), calls=%async_computation.1 | async-start | bytes 2097152 | tf_op jit(solution)/shard_map/all_to_all | solution.py:128
  72.6 1.0 collective-permute-done.9
  73.6 1.6 collective-permute-start.10
  75.2 9.0 %collective-permute-done.10.other_third = bf16[256,768]{1,0:T(8,128)(2,1)S(1)} collective-permute-done((bf16[256,768]{1,0:T(8,128)(2,1)S(1)}, bf16[256,768]{1,0:T(8,128)(2,1)S(1)}, u32[]{:S(2)}, u32[]{:S(2)}) %collective-permute-start.10) | collective-permute-done | bytes 393248 | tf_op jit(solution)/shard_map/ppermute | solution.py:132
  84.2 6.3 %collective-permute-done.13.rest_6_ = bf16[8,32,2048]{2,1,0:T(8,128)(2,1)S(1)} collective-permute-done((bf16[8,32,2048]{2,1,0:T(8,128)(2,1)S(1)}, bf16[8,32,2048]{2,1,0:T(8,128)(2,1)S(1)}, u32[]{:S(2)}, u32[]{:S(2)}) %collective-permute-start.13) | collective-permute-done | bytes 1048608 | tf_op jit(solution)/shard_map/ppermute | solution.py:124
  90.5 0.0 copy-start.2
  90.5 6.7 %all-to-all-done.1.values = bf16[4,2,4,32,512]{4,3,2,1,0:T(8,128)(2,1)} async-done(((bf16[4,2,4,32,512]{4,3,2,1,0:T(8,128)(2,1)}), bf16[4,2,4,32,512]{4,3,2,1,0:T(8,128)(2,1)}, u32[]{:S(2)}, u32[]{:S(2)}) %all-to-all-start.1) | async-done | bytes 1048608 | tf_op jit(solution)/shard_map/all_to_all | solution.py:128
  97.3 5.2 %weight_first.1 = (bf16[512,1024]{1,0:T(8,128)(2,1)}, bf16[512,768]{1,0:T(8,128)(2,1)}) custom-call(s32[3]{0:T(128)} %pad_add_fusion.ids, bf16[4,4,256,256]{3,2,1,0:T(8,128)(2,1)} %time_probs.1.probs_t.rest_8_, bf16[4,2,4,32,512]{4,3,2,1,0:T(8,128)(2,1)} %all-to-all-done.1.values, bf16[8,32,1024]{2,1,0:T(8,128)(2,1)} %in_order.1.rest_0_, ...), custom_call_target="tpu_custom_call" | custom-call | tf_op jit(solution)/shard_map/weight_first/pallas_call | solution.py:308
  102.4 9.5 %space_grad.1 = bf16[4,2,4,32,512]{4,3,2,1,0:T(8,128)(2,1)} custom-call(s32[3]{0:T(128)} %pad_add_fusion.ids, bf16[512,768]{1,0:T(8,128)(2,1)} %own.1, bf16[256,768]{1,0:T(8,128)(2,1)} %copy-done.7, bf16[256,768]{1,0:T(8,128)(2,1)} %copy-done.6, bf16[256,768]{1,0:T(8,128)(2,1)} %copy-done.10, bf16[512,768]{1,0:T(8,128)(2,1)} %copy-done.11, ...), custom_call_target="tpu_custom_call" | custom-call | tf_op jit(solution)/shard_map/space_grad/pallas_call | solution.py:391
  112.0 3.7 %all-to-all-start.2 = ((bf16[4,2,4,32,512]{4,3,2,1,0:T(8,128)(2,1)}), bf16[4,2,4,32,512]{4,3,2,1,0:T(8,128)(2,1)S(1)}, u32[]{:S(2)}, u32[]{:S(2)}) async-start(bf16[4,2,4,32,512]{4,3,2,1,0:T(8,128)(2,1)} %space_grad.1), calls=%async_computation.2 | async-start | bytes 2097152 | tf_op jit(solution)/shard_map/all_to_all | solution.py:128
  115.7 8.0 %weight_second.1 = (f32[512,768]{1,0:T(8,128)}, f32[512,768]{1,0:T(8,128)}, bf16[512,768]{1,0:T(8,128)(2,1)}) custom-call(s32[3]{0:T(128)} %pad_add_fusion.ids, bf16[512,1024]{1,0:T(8,128)(2,1)} %get-tuple-element.61.left, bf16[8,32,1024]{2,1,0:T(8,128)(2,1)} %in_order.1.rest_0_, bf16[8,32,1024]{2,1,0:T(8,128)(2,1)} %copy-done.3, ...), custom_call_target="tpu_custom_call" | custom-call | tf_op jit(solution)/shard_map/weight_second/pallas_call | solution.py:322
  123.7 5.8 %collective-permute-done.15 = bf16[512,768]{1,0:T(8,128)(2,1)S(1)} collective-permute-done((bf16[512,768]{1,0:T(8,128)(2,1)}, bf16[512,768]{1,0:T(8,128)(2,1)S(1)}, u32[]{:S(2)}, u32[]{:S(2)}) %collective-permute-start.15) | collective-permute-done | bytes 786464 | tf_op jit(solution)/shard_map/ppermute | solution.py:124
  129.5 1.6 add_convert_fusion
  131.1 0.1 collective-permute-start.16
  131.2 11.1 %all-to-all-done.2.piece = bf16[4,2,4,32,512]{4,3,2,1,0:T(8,128)(2,1)S(1)} async-done(((bf16[4,2,4,32,512]{4,3,2,1,0:T(8,128)(2,1)}), bf16[4,2,4,32,512]{4,3,2,1,0:T(8,128)(2,1)S(1)}, u32[]{:S(2)}, u32[]{:S(2)}) %all-to-all-start.2) | async-done | bytes 1048608 | tf_op jit(solution)/shard_map/all_to_all | solution.py:128
  142.3 1.0 copy-done.5
  143.3 8.9 %space_backward.1 = (bf16[2,512,512]{2,1,0:T(8,128)(2,1)}, bf16[2,512,512]{2,1,0:T(8,128)(2,1)}, bf16[2,512,512]{2,1,0:T(8,128)(2,1)}) custom-call(bf16[2,512,512]{2,1,0:T(8,128)(2,1)} %q.2, bf16[2,512,512]{2,1,0:T(8,128)(2,1)} %k.5, bf16[2,512,512]{2,1,0:T(8,128)(2,1)} %v.3, bf16[8,512,512]{2,1,0:T(8,128)(2,1)} %get-tuple-element.37.probs, ...), custom_call_target="tpu_custom_call" | custom-call | tf_op jit(solution)/shard_map/space_backward/pallas_call | solution.py:434
  152.2 15.9 %collective-permute-done.17 = bf16[512,768]{1,0:T(8,128)(2,1)S(1)} collective-permute-done((bf16[512,768]{1,0:T(8,128)(2,1)}, bf16[512,768]{1,0:T(8,128)(2,1)S(1)}, u32[]{:S(2)}, u32[]{:S(2)}) %collective-permute-start.17) | collective-permute-done | bytes 786464 | tf_op jit(solution)/shard_map/ppermute | solution.py:124
  168.1 6.3 %collective-permute-done.16 = bf16[512,768]{1,0:T(8,128)(2,1)S(1)} collective-permute-done((bf16[512,768]{1,0:T(8,128)(2,1)S(1)}, bf16[512,768]{1,0:T(8,128)(2,1)S(1)}, u32[]{:S(2)}, u32[]{:S(2)}) %collective-permute-start.16) | collective-permute-done | bytes 786464 | tf_op jit(solution)/shard_map/ppermute | solution.py:124
  174.5 1.3 convert_add_fusion
  (48 shorter events, 0.2 us)
Async XLA Ops:
  2.4 33.2 %collective-permute-start.1 = (bf16[256,768]{1,0:T(8,128)(2,1)}, bf16[256,768]{1,0:T(8,128)(2,1)S(1)}, u32[]{:S(2)}, u32[]{:S(2)}) collective-permute-start(bf16[256,768]{1,0:T(8,128)(2,1)} %constant_dynamic-slice_fusion), channel_id=1, source_target_pairs={{0,8},{4,12},{8,0},{12,4},{1,9},{5,13},{9,1},{13,5},{2,10},{6,14},... | collective-permute-start | bytes 1179656 | tf_op jit(solution)/shard_map/ppermute | solution.py:124
  6.4 29.2 %collective-permute-start = (bf16[256,768]{1,0:T(8,128)(2,1)}, bf16[256,768]{1,0:T(8,128)(2,1)S(1)}, u32[]{:S(2)}, u32[]{:S(2)}) collective-permute-start(bf16[256,768]{1,0:T(8,128)(2,1)} %constant_dynamic-slice_fusion), channel_id=1, source_target_pairs={{0,4},{4,0},{8,12},{12,8},{1,5},{5,1},{9,13},{13,9},{2,6},{6,2},{1... | collective-permute-start | bytes 1179656 | tf_op jit(solution)/shard_map/ppermute | solution.py:124
  8.0 6.5 %copy-start.8 = (bf16[2,128,3072]{2,1,0:T(8,128)(2,1)S(1)}, bf16[2,128,3072]{2,1,0:T(8,128)(2,1)}, u32[]{:S(2)}) copy-start(bf16[2,128,3072]{2,1,0:T(8,128)(2,1)} %param.13) | copy-start | bytes 4718596
  10.2 20.2 %collective-permute-start.4 = (bf16[2,32,1024]{2,1,0:T(8,128)(2,1)}, bf16[2,32,1024]{2,1,0:T(8,128)(2,1)S(1)}, u32[]{:S(2)}, u32[]{:S(2)}) collective-permute-start(bf16[2,32,1024]{2,1,0:T(8,128)(2,1)} %get-tuple-element.76), channel_id=1, source_target_pairs={{0,12},{4,8},{8,4},{12,0},{1,13},{5,9},{9,5},{13,1},{2,14},{6,10},... | collective-permute-start | bytes 393224 | tf_op jit(solution)/shard_map/ppermute | solution.py:124
  10.2 25.4 %collective-permute-start.3 = (bf16[2,32,1024]{2,1,0:T(8,128)(2,1)}, bf16[2,32,1024]{2,1,0:T(8,128)(2,1)}, u32[]{:S(2)}, u32[]{:S(2)}) collective-permute-start(bf16[2,32,1024]{2,1,0:T(8,128)(2,1)} %get-tuple-element.77), channel_id=1, source_target_pairs={{0,8},{4,12},{8,0},{12,4},{1,9},{5,13},{9,1},{13,5},{2,10},{6,14},... | collective-permute-start | bytes 393224 | tf_op jit(solution)/shard_map/ppermute | solution.py:124
  12.1 23.5 %collective-permute-start.2 = (bf16[2,32,1024]{2,1,0:T(8,128)(2,1)}, bf16[2,32,1024]{2,1,0:T(8,128)(2,1)}, u32[]{:S(2)}, u32[]{:S(2)}) collective-permute-start(bf16[2,32,1024]{2,1,0:T(8,128)(2,1)} %get-tuple-element.78), channel_id=1, source_target_pairs={{0,4},{4,0},{8,12},{12,8},{1,5},{5,1},{9,13},{13,9},{2,6},{6,2},{1... | collective-permute-start | bytes 393224 | tf_op jit(solution)/shard_map/ppermute | solution.py:124
  30.3 10.1 %copy-start.15 = (bf16[2,32,1024]{2,1,0:T(8,128)(2,1)}, bf16[2,32,1024]{2,1,0:T(8,128)(2,1)S(1)}, u32[]{:S(2)}) copy-start(bf16[2,32,1024]{2,1,0:T(8,128)(2,1)S(1)} %collective-permute-done.4.rest_3_) | copy-start | bytes 393220
  35.6 32.2 %copy-start.6 = (bf16[256,768]{1,0:T(8,128)(2,1)}, bf16[256,768]{1,0:T(8,128)(2,1)S(1)}, u32[]{:S(2)}) copy-start(bf16[256,768]{1,0:T(8,128)(2,1)S(1)} %collective-permute-done.1.second) | copy-start | bytes 1179652
  35.6 4.9 %copy-start.7 = (bf16[256,768]{1,0:T(8,128)(2,1)}, bf16[256,768]{1,0:T(8,128)(2,1)S(1)}, u32[]{:S(2)}) copy-start(bf16[256,768]{1,0:T(8,128)(2,1)S(1)} %collective-permute-done.first) | copy-start | bytes 1179652
  35.6 30.7 %all-to-all-start = ((bf16[8,32,2048]{2,1,0:T(8,128)(2,1)}), bf16[8,32,2048]{2,1,0:T(8,128)(2,1)S(1)}, u32[]{:S(2)}, u32[]{:S(2)}) async-start(bf16[8,32,2048]{2,1,0:T(8,128)(2,1)} %bitcast.2), calls=%async_computation | async-start | bytes 2097152 | tf_op jit(solution)/shard_map/all_to_all | solution.py:128
  40.5 22.2 %collective-permute-start.6 = (bf16[512,768]{1,0:T(8,128)(2,1)S(1)}, bf16[512,768]{1,0:T(8,128)(2,1)S(1)}, u32[]{:S(2)}, u32[]{:S(2)}) collective-permute-start(bf16[512,768]{1,0:T(8,128)(2,1)S(1)} %pad_maximum_fusion.1), channel_id=1, source_target_pairs={{0,16},{16,0},{1,17},{17,1},{2,18},{18,2},{3,19},{19,3},{4,20},{20... | collective-permute-start | bytes 2359304 | tf_op jit(solution)/shard_map/ppermute | solution.py:132
  44.7 17.2 %collective-permute-start.8 = (bf16[8,32,1024]{2,1,0:T(8,128)(2,1)}, bf16[8,32,1024]{2,1,0:T(8,128)(2,1)S(1)}, u32[]{:S(2)}, u32[]{:S(2)}) collective-permute-start(bf16[8,32,1024]{2,1,0:T(8,128)(2,1)} %in_order.1.rest_0_), channel_id=1, source_target_pairs={{0,1},{1,0},{2,3},{3,2},{4,5},{5,4},{6,7},{7,6},{8,9},{9,8},{10,11... | collective-permute-start | bytes 1572872 | tf_op jit(solution)/shard_map/ppermute | solution.py:124
  44.7 17.2 %collective-permute-start.7 = (bf16[8,32,1024]{2,1,0:T(8,128)(2,1)}, bf16[8,32,1024]{2,1,0:T(8,128)(2,1)}, u32[]{:S(2)}, u32[]{:S(2)}) collective-permute-start(bf16[8,32,1024]{2,1,0:T(8,128)(2,1)} %in_order.1.rest_0_), channel_id=1, source_target_pairs={{0,2},{1,3},{2,0},{3,1},{4,6},{5,7},{6,4},{7,5},{8,10},{9,11},{10,... | collective-permute-start | bytes 1572872 | tf_op jit(solution)/shard_map/ppermute | solution.py:124
  46.2 15.7 %collective-permute-start.5 = (bf16[128,768]{1,0:T(8,128)(2,1)S(1)}, bf16[128,768]{1,0:T(8,128)(2,1)S(1)}, u32[]{:S(2)}, u32[]{:S(2)}) collective-permute-start(bf16[128,768]{1,0:T(8,128)(2,1)S(1)} %slice.38), channel_id=1, source_target_pairs={{0,4},{4,0},{8,12},{12,8},{1,5},{5,1},{9,13},{13,9},{2,6},{6,2},{1... | collective-permute-start | bytes 589832 | tf_op jit(solution)/shard_map/ppermute | solution.py:124
  61.9 0.9 copy-start.13
  61.9 0.9 copy-start.3
  62.7 0.9 copy-start.11
  66.3 8.9 %copy-start = (bf16[8,32,2048]{2,1,0:T(8,128)(2,1)}, bf16[8,32,2048]{2,1,0:T(8,128)(2,1)S(1)}, u32[]{:S(2)}) copy-start(bf16[8,32,2048]{2,1,0:T(8,128)(2,1)S(1)} %all-to-all-done.rest_4_) | copy-start | bytes 3145732
  66.3 6.2 %copy-start.14 = (bf16[128,768]{1,0:T(8,128)(2,1)S(1)}, bf16[128,768]{1,0:T(8,128)(2,1)}, u32[]{:S(2)}) copy-start(bf16[128,768]{1,0:T(8,128)(2,1)} %copy-done.13) | copy-start | bytes 589828
  66.3 24.1 %collective-permute-start.13 = (bf16[8,32,2048]{2,1,0:T(8,128)(2,1)S(1)}, bf16[8,32,2048]{2,1,0:T(8,128)(2,1)S(1)}, u32[]{:S(2)}, u32[]{:S(2)}) collective-permute-start(bf16[8,32,2048]{2,1,0:T(8,128)(2,1)S(1)} %all-to-all-done.rest_4_), channel_id=1, source_target_pairs={{0,2},{1,3},{2,0},{3,1},{4,6},{5,7},{6,4},{7,5},{8,10},{9,11},{10,... | collective-permute-start | bytes 3145736 | tf_op jit(solution)/shard_map/ppermute | solution.py:124
  67.9 5.7 %collective-permute-start.9 = (bf16[128,768]{1,0:T(8,128)(2,1)S(1)}, bf16[128,768]{1,0:T(8,128)(2,1)S(1)}, u32[]{:S(2)}, u32[]{:S(2)}) collective-permute-start(bf16[128,768]{1,0:T(8,128)(2,1)S(1)} %slice.39), channel_id=1, source_target_pairs={{0,4},{4,0},{8,12},{12,8},{1,5},{5,1},{9,13},{13,9},{2,6},{6,2},{1... | collective-permute-start | bytes 589832 | tf_op jit(solution)/shard_map/ppermute | solution.py:124
  67.9 29.3 %all-to-all-start.1 = ((bf16[4,2,4,32,512]{4,3,2,1,0:T(8,128)(2,1)}), bf16[4,2,4,32,512]{4,3,2,1,0:T(8,128)(2,1)}, u32[]{:S(2)}, u32[]{:S(2)}) async-start(bf16[4,2,4,32,512]{4,3,2,1,0:T(8,128)(2,1)} %get-tuple-element.54), calls=%async_computation.1 | async-start | bytes 2097152 | tf_op jit(solution)/shard_map/all_to_all | solution.py:128
  72.6 2.7 %collective-permute-start.11 = (bf16[8,32,1024]{2,1,0:T(8,128)(2,1)}, bf16[8,32,1024]{2,1,0:T(8,128)(2,1)S(1)}, u32[]{:S(2)}, u32[]{:S(2)}) collective-permute-start(bf16[8,32,1024]{2,1,0:T(8,128)(2,1)} %collective-permute-done.7.rest_2_), channel_id=1, source_target_pairs={{0,1},{1,0},{2,3},{3,2},{4,5},{5,4},{6,7},{7,6},{8,9},{9,8},{10,11... | collective-permute-start | bytes 1572872 | tf_op jit(solution)/shard_map/ppermute | solution.py:124
  73.6 28.8 %copy-start.10 = (bf16[256,768]{1,0:T(8,128)(2,1)}, bf16[256,768]{1,0:T(8,128)(2,1)S(1)}, u32[]{:S(2)}) copy-start(bf16[256,768]{1,0:T(8,128)(2,1)S(1)} %constant_dynamic-update-slice_fusion.third) | copy-start | bytes 1179652
  73.6 10.6 %collective-permute-start.10 = (bf16[256,768]{1,0:T(8,128)(2,1)S(1)}, bf16[256,768]{1,0:T(8,128)(2,1)S(1)}, u32[]{:S(2)}, u32[]{:S(2)}) collective-permute-start(bf16[256,768]{1,0:T(8,128)(2,1)S(1)} %constant_dynamic-update-slice_fusion.third), channel_id=1, source_target_pairs={{0,16},{16,0},{1,17},{17,1},{2,18},{18,2},{3,19},{19,3},{4,20},{20... | collective-permute-start | bytes 1179656 | tf_op jit(solution)/shard_map/ppermute | solution.py:132
  75.2 15.3 %collective-permute-start.12 = (bf16[8,32,2048]{2,1,0:T(8,128)(2,1)S(1)}, bf16[8,32,2048]{2,1,0:T(8,128)(2,1)S(1)}, u32[]{:S(2)}, u32[]{:S(2)}) collective-permute-start(bf16[8,32,2048]{2,1,0:T(8,128)(2,1)S(1)} %all-to-all-done.rest_4_), channel_id=1, source_target_pairs={{0,1},{1,0},{2,3},{3,2},{4,5},{5,4},{6,7},{7,6},{8,9},{9,8},{10,11... | collective-permute-start | bytes 3145736 | tf_op jit(solution)/shard_map/ppermute | solution.py:124
  75.2 15.3 %copy-start.4 = (bf16[8,32,1024]{2,1,0:T(8,128)(2,1)}, bf16[8,32,1024]{2,1,0:T(8,128)(2,1)S(1)}, u32[]{:S(2)}) copy-start(bf16[8,32,1024]{2,1,0:T(8,128)(2,1)S(1)} %collective-permute-done.11.rest_3_) | copy-start | bytes 1572868
  84.2 6.3 %copy-start.12 = (bf16[256,768]{1,0:T(8,128)(2,1)}, bf16[256,768]{1,0:T(8,128)(2,1)S(1)}, u32[]{:S(2)}) copy-start(bf16[256,768]{1,0:T(8,128)(2,1)S(1)} %collective-permute-done.10.other_third) | copy-start | bytes 1179652
  90.5 6.8 %copy-start.1 = (bf16[8,32,2048]{2,1,0:T(8,128)(2,1)}, bf16[8,32,2048]{2,1,0:T(8,128)(2,1)S(1)}, u32[]{:S(2)}) copy-start(bf16[8,32,2048]{2,1,0:T(8,128)(2,1)S(1)} %collective-permute-done.13.rest_6_) | copy-start | bytes 3145732
  90.5 6.8 %collective-permute-start.14 = (bf16[8,32,2048]{2,1,0:T(8,128)(2,1)S(1)}, bf16[8,32,2048]{2,1,0:T(8,128)(2,1)}, u32[]{:S(2)}, u32[]{:S(2)}) collective-permute-start(bf16[8,32,2048]{2,1,0:T(8,128)(2,1)S(1)} %collective-permute-done.13.rest_6_), channel_id=1, source_target_pairs={{0,1},{1,0},{2,3},{3,2},{4,5},{5,4},{6,7},{7,6},{8,9},{9,8},{10,11... | collective-permute-start | bytes 3145736 | tf_op jit(solution)/shard_map/ppermute | solution.py:124
  90.5 6.7 %copy-start.2 = (bf16[8,32,2048]{2,1,0:T(8,128)(2,1)}, bf16[8,32,2048]{2,1,0:T(8,128)(2,1)S(1)}, u32[]{:S(2)}) copy-start(bf16[8,32,2048]{2,1,0:T(8,128)(2,1)S(1)} %collective-permute-done.12.rest_5_) | copy-start | bytes 3145732
  102.4 27.1 %collective-permute-start.15 = (bf16[512,768]{1,0:T(8,128)(2,1)}, bf16[512,768]{1,0:T(8,128)(2,1)S(1)}, u32[]{:S(2)}, u32[]{:S(2)}) collective-permute-start(bf16[512,768]{1,0:T(8,128)(2,1)} %get-tuple-element.55), channel_id=1, source_target_pairs={{0,4},{4,0},{8,12},{12,8},{1,5},{5,1},{9,13},{13,9},{2,6},{6,2},{1... | collective-permute-start | bytes 2359304 | tf_op jit(solution)/shard_map/ppermute | solution.py:124
  112.0 30.3 %all-to-all-start.2 = ((bf16[4,2,4,32,512]{4,3,2,1,0:T(8,128)(2,1)}), bf16[4,2,4,32,512]{4,3,2,1,0:T(8,128)(2,1)S(1)}, u32[]{:S(2)}, u32[]{:S(2)}) async-start(bf16[4,2,4,32,512]{4,3,2,1,0:T(8,128)(2,1)} %space_grad.1), calls=%async_computation.2 | async-start | bytes 2097152 | tf_op jit(solution)/shard_map/all_to_all | solution.py:128
  129.5 38.6 %collective-permute-start.17 = (bf16[512,768]{1,0:T(8,128)(2,1)}, bf16[512,768]{1,0:T(8,128)(2,1)S(1)}, u32[]{:S(2)}, u32[]{:S(2)}) collective-permute-start(bf16[512,768]{1,0:T(8,128)(2,1)} %get-tuple-element.65), channel_id=1, source_target_pairs={{0,4},{4,0},{8,12},{12,8},{1,5},{5,1},{9,13},{13,9},{2,6},{6,2},{1... | collective-permute-start | bytes 2359304 | tf_op jit(solution)/shard_map/ppermute | solution.py:124
  131.1 43.4 %collective-permute-start.16 = (bf16[512,768]{1,0:T(8,128)(2,1)S(1)}, bf16[512,768]{1,0:T(8,128)(2,1)S(1)}, u32[]{:S(2)}, u32[]{:S(2)}) collective-permute-start(bf16[512,768]{1,0:T(8,128)(2,1)S(1)} %add_convert_fusion), channel_id=1, source_target_pairs={{0,8},{4,12},{8,0},{12,4},{1,9},{5,13},{9,1},{13,5},{2,10},{6,14},... | collective-permute-start | bytes 2359304 | tf_op jit(solution)/shard_map/ppermute | solution.py:124
  142.3 1.0 copy-start.5
  143.3 31.2 %copy-start.9 = (f32[512,768]{1,0:T(8,128)S(1)}, f32[512,768]{1,0:T(8,128)}, u32[]{:S(2)}) copy-start(f32[512,768]{1,0:T(8,128)} %get-tuple-element.62) | copy-start | bytes 4718596
